TPU v7x, 256 devices: a whole 4x4x8 slice. The times are simulated.
256 devices in a mesh: ctx: 128 (over x_lo, z, y, core), section: 2 (over x_hi).
Axes of the slice: x: 4 (x_hi: 2, x_lo: 2; x = x_hi * 2 + x_lo), y: 4, z: 8, core: 2. Of those that a mesh axis runs over, the one named last changes fastest.
Arguments:
- queries: bfloat16 [32768, 5120], P('ctx', 'section'), as said below
- key_states: bfloat16 [32768, 5120], P('ctx', 'section'), as said below
- value_states: bfloat16 [32768, 5120], P('ctx', 'section'), may hold values from -6 to 6
- out_grad: bfloat16 [32768, 5120], P('ctx', 'section'), may hold values from -6 to 6
- tile_mask: int32 [256, 6], replicated, may hold values from 0 to 1, as said below
Outputs:
- query_grad: bfloat16 [32768, 5120], P(('ctx', 'section'))
- key_grad: bfloat16 [32768, 5120], P(('ctx', 'section'))
- value_grad: bfloat16 [32768, 5120], P(('ctx', 'section'))
Inputs may be any that keep to these rules, and one draw needn't show every extreme that they name: tile_mask[t, 2 + (t mod 2)] is 1 for every tile t: each tile attends to itself. `queries`: entries lie within -6 and 6. `key_states`: entries lie within -6 and 6.
All inputs are finite; a program needn't handle non-finite values.
Results may differ from a plain program's by a relative error of at most 0.0096.
Values may be sent and summed in bfloat16 or wider, within the bound.
No kernel may reach another device: no remote copies, remote signals or barrier semaphores. Data moves between devices by JAX's collectives and lax.ppermute only.
A program may use at most 128 MiB of HBM per device.

v0:
```python
import math

import jax
import jax.numpy as jnp
from jax import lax
from jax.sharding import PartitionSpec as P

HEAD = 128
H = 20
TILE = 128


def with_halo(shard, sides, width):
    for axis, dim in sides:
        count, length = (lax.axis_size(axis), shard.shape[dim])
        up = [(i, (i + 1) % count) for i in range(count)]
        down = [(j, i) for i, j in up]
        last = lax.slice_in_dim(shard, length - width, length, axis=dim)
        first = lax.slice_in_dim(shard, 0, width, axis=dim)
        before = lax.ppermute(last, axis, up)
        after = lax.ppermute(first, axis, down)
        shard = jnp.concatenate([before, shard, after], axis=dim)
    return shard


def from_behind(shard, axis, by):
    count = lax.axis_size(axis)
    return lax.ppermute(shard, axis, [(i, (i + by) % count) for i in range(count)])


def expand_mask(mask_rows, tile_rows):
    grown = jnp.repeat(jnp.repeat(mask_rows, tile_rows, axis=0), tile_rows, axis=1)
    return grown > 0


def query_pass(queries, grads_in, key_band, value_band, live_mask):
    row_count = queries.shape[0]
    score_scale = 1.0 / math.sqrt(HEAD)
    query_heads = queries.reshape(row_count, H, HEAD)
    grad_heads = grads_in.reshape(row_count, H, HEAD)
    key_heads = key_band.reshape(key_band.shape[0], H, HEAD)
    value_heads = value_band.reshape(value_band.shape[0], H, HEAD)
    scores = (
        jnp.einsum("qhd,khd->hqk", query_heads, key_heads, preferred_element_type=jnp.float32)
        * score_scale
    )
    scores = jnp.where(live_mask[None], scores, -jnp.inf)
    row_top = jnp.max(scores, axis=-1, keepdims=True)
    log_total = row_top + jnp.log(jnp.sum(jnp.exp(scores - row_top), axis=-1, keepdims=True))
    attn_weights = jnp.exp(scores - log_total)
    dweights = jnp.einsum(
        "qhd,khd->hqk", grad_heads, value_heads, preferred_element_type=jnp.float32
    )
    row_delta = jnp.sum(attn_weights * dweights, axis=-1, keepdims=True)
    dscores = (attn_weights * (dweights - row_delta) * score_scale).astype(jnp.bfloat16)
    grad_query = jnp.einsum("hqk,khd->qhd", dscores, key_heads, preferred_element_type=jnp.float32)
    grad_query = grad_query.reshape(row_count, H * HEAD).astype(jnp.bfloat16)
    weights_low = attn_weights.astype(jnp.bfloat16)
    key_part = jnp.einsum("hqk,qhd->khd", dscores, query_heads, preferred_element_type=jnp.float32)
    value_part = jnp.einsum(
        "hqk,qhd->khd", weights_low, grad_heads, preferred_element_type=jnp.float32
    )
    key_part = key_part.reshape(key_band.shape[0], H * HEAD).astype(jnp.bfloat16)
    value_part = value_part.reshape(key_band.shape[0], H * HEAD).astype(jnp.bfloat16)
    return (grad_query, log_total[..., 0], row_delta[..., 0], key_part, value_part)


def on_device(queries, key_states, value_states, out_grad, tile_mask):
    row_count = queries.shape[0]
    tile_count = row_count // TILE
    position = lax.axis_index("ctx")
    own_mask = lax.dynamic_slice_in_dim(tile_mask, position * tile_count, tile_count, 0)
    paired = jnp.stack([key_states, value_states])
    paired_band = with_halo(paired, (("ctx", 1),), row_count)
    live_mask = expand_mask(own_mask, TILE)
    grad_query, log_total, row_delta, key_part, value_part = query_pass(
        queries, out_grad, paired_band[0], paired_band[1], live_mask
    )
    partials = jnp.stack([key_part, value_part])
    from_next = from_behind(partials[:, :row_count], "ctx", -1)
    from_prev = from_behind(partials[:, 2 * row_count :], "ctx", 1)
    summed = (
        partials[:, row_count : 2 * row_count].astype(jnp.float32)
        + from_next.astype(jnp.float32)
        + from_prev.astype(jnp.float32)
    )
    grad_pair = summed.astype(jnp.bfloat16)
    query_out, key_out, value_out = (
        lax.all_to_all(grad_query, "section", split_axis=0, concat_axis=1, tiled=True),
        lax.all_to_all(grad_pair[0], "section", split_axis=0, concat_axis=1, tiled=True),
        lax.all_to_all(grad_pair[1], "section", split_axis=0, concat_axis=1, tiled=True),
    )
    return (query_out, key_out, value_out)


def solution(mesh):
    placed = (
        P("ctx", "section"),
        P("ctx", "section"),
        P("ctx", "section"),
        P("ctx", "section"),
        P(),
    )
    return jax.shard_map(
        on_device,
        mesh=mesh,
        in_specs=placed,
        out_specs=(
            P(("ctx", "section"), None),
            P(("ctx", "section"), None),
            P(("ctx", "section"), None),
        ),
        check_vma=False,
    )
```

profile of v0, /device:TPU:24, one launch (start us, length us, event | category | flops | bytes accessed | tf_op | source)
XLA Modules:
  0.0 209.3 jit_solution(12413543343537095242)
XLA Ops:
  0.6 1.6 copy.50
  2.2 1.6 copy.51
  3.9 1.9 pad_maximum_fusion.2
  6.5 2.4 %copy.53 = bf16[256,2560]{0,1:T(8,128)(2,1)} copy(bf16[256,2560]{1,0:T(8,128)(2,1)} %param.5) | data formatting | bytes 2621440 | tf_op args[0]
  8.9 1.6 copy.56
  10.6 24.9 %collective-permute-done.1 = bf16[2,256,2560]{1,2,0:T(8,128)(2,1)} collective-permute-done((bf16[2,256,2560]{1,2,0:T(8,128)(2,1)}, bf16[2,256,2560]{1,2,0:T(8,128)(2,1)}, u32[]{:S(2)}, u32[]{:S(2)}) %collective-permute-start.1) | collective-permute-done | bytes 2621472 | tf_op jit(solution)/shard_map/ppermute | solution.py:21
  35.4 1.9 collective-permute-done
  37.3 3.7 %pad_maximum_fusion = bf16[2,768,2560]{1,2,0:T(8,128)(2,1)S(1)} fusion(bf16[2,256,2560]{1,2,0:T(8,128)(2,1)} %collective-permute-done.1, bf16[1,256,2560]{1,2,0:T(8,128)(2,1)} %bitcast.83, bf16[1,256,2560]{1,2,0:T(8,128)(2,1)S(1)} %bitcast.81, bf16[2,256,2560]{1,2,0:T(8,128)(2,1)} %collective-permute-done), kind=kLoop, calls=%fused_computation.15 | loop fusion | flops 31457280 | bytes 15728640 | tf_op jit(solution)/shard_map/concatenate | solution.py:22
  41.7 0.7 copy-done.2
  42.4 7.1 %fusion.25 = (f32[20,256]{1,0:T(8,128)S(1)}, f32[20,256,768]{1,2,0:T(8,128)}) fusion(bf16[768,20,128]{0,2,1:T(8,128)(2,1)S(1)} %bitcast.76, bf16[256,20,128]{0,2,1:T(8,128)(2,1)S(1)} %bitcast.84, pred[256,768]{0,1:T(8,128)(4,1)S(1)} %bitcast.90), kind=kOutput, calls=%fused_computation.38 | convolution fusion | flops 1018424320 | bytes 21188608 | tf_op jit(solution)/shard_map/qhd,khd->hqk/dot_general | solution.py:44
  49.4 7.6 %exponential_reduce_fusion = f32[20,256]{1,0:T(8,128)S(1)} fusion(f32[20,256,768]{1,2,0:T(8,128)} %get-tuple-element.16, f32[20,256]{1,0:T(8,128)S(1)} %get-tuple-element.15), kind=kLoop, calls=%fused_computation.8 | loop fusion | flops 7859200 | bytes 15769600 | tf_op jit(solution)/shard_map/reduce_sum | solution.py:49
  57.1 7.7 %fusion.26 = f32[20,768,256]{2,1,0:T(8,128)} fusion(bf16[768,20,128]{0,2,1:T(8,128)(2,1)S(1)} %bitcast.73, bf16[256,20,128]{0,2,1:T(8,128)(2,1)S(1)} %bitcast.78), kind=kOutput, calls=%fused_computation.39 | convolution fusion | flops 1006632960 | bytes 20971520 | tf_op jit(solution)/shard_map/qhd,khd->hqk/dot_general | solution.py:51
  64.8 10.1 %fusion.14 = bf16[20,768,128]{1,2,0:T(8,128)(2,1)} fusion(bf16[256,20,128]{0,2,1:T(8,128)(2,1)S(1)} %bitcast.79, f32[20,256,768]{1,2,0:T(8,128)} %get-tuple-element.16, f32[20,256]{1,0:T(8,128)S(1)} %log_add_fusion), kind=kOutput, calls=%fused_computation.26 | convolution fusion | flops 1016463360 | bytes 20992000 | tf_op jit(solution)/shard_map/hqk,qhd->khd/dot_general | solution.py:60
  75.0 23.2 %fusion.13 = bf16[20,768,128]{1,2,0:T(8,128)(2,1)} fusion(bf16[256,20,128]{0,2,1:T(8,128)(2,1)S(1)} %bitcast.85, f32[20,768,256]{2,1,0:T(8,128)} %fusion.26, f32[20,256,768]{1,2,0:T(8,128)} %get-tuple-element.16, f32[20,256]{1,0:T(8,128)S(1)} %log_add_fusion), kind=kOutput, calls=%fused_computation.25 | convolution fusion | flops 1036130048 | bytes 36720640 | tf_op jit(solution)/shard_map/hqk,qhd->khd/dot_general | solution.py:59
  98.1 4.2 %fusion.11 = (bf16[2,256,2560]{1,2,0:T(8,128)(2,1)}, bf16[2,256,2560]{1,2,0:T(8,128)(2,1)}) fusion(bf16[1,768,2560]{1,2,0:T(8,128)(2,1)} %bitcast.74, bf16[1,768,2560]{1,2,0:T(8,128)(2,1)} %bitcast.71), kind=kLoop, calls=%fused_computation.21 | loop fusion | flops 10485760 | bytes 13107200 | tf_op jit(solution)/shard_map/stack | solution.py:79
  102.6 1.6 collective-permute-start.3
  104.2 26.5 %fusion.18 = bf16[256,20,128]{0,2,1:T(8,128)(2,1)S(1)} fusion(bf16[768,20,128]{0,2,1:T(8,128)(2,1)} %bitcast.77, f32[20,768,256]{2,1,0:T(8,128)} %fusion.26, f32[20,256,768]{1,2,0:T(8,128)} %get-tuple-element.16, f32[20,256]{1,0:T(8,128)S(1)} %log_add_fusion), kind=kOutput, calls=%fused_computation.28 | convolution fusion | flops 1034819328 | bytes 36720640 | tf_op jit(solution)/shard_map/hqk,khd->qhd/dot_general | solution.py:56
  131.0 1.2 copy.60
  132.2 4.5 %all-to-all-start = ((bf16[2,128,2560]{1,2,0:T(8,128)(2,1)}), bf16[2,128,2560]{1,2,0:T(8,128)(2,1)}, u32[]{:S(2)}, u32[]{:S(2)}) async-start(bf16[2,128,2560]{1,2,0:T(8,128)(2,1)} %copy.60), calls=%async_computation | async-start | bytes 2621440 | tf_op jit(solution)/shard_map/all_to_all | solution.py:89
  136.8 3.8 %add_convert_fusion = bf16[2,256,2560]{1,2,0:T(8,128)(2,1)S(1)} fusion(bf16[2,256,2560]{1,2,0:T(8,128)(2,1)} %collective-permute-done.3, bf16[2,256,2560]{1,2,0:T(8,128)(2,1)} %collective-permute-done.2, bf16[1,768,2560]{1,2,0:T(8,128)(2,1)} %bitcast.75, bf16[1,768,2560]{1,2,0:T(8,128)(2,1)} %bitcast.72), kind=kLoop, calls=%fused_computation.20 | loop fusion | flops 9175040 | bytes 15728640 | tf_op jit(solution)/shard_map/convert_element_type | solution.py:87
  140.7 1.6 copy.65
  142.3 21.5 %all-to-all-done = bf16[2,128,2560]{1,2,0:T(8,128)(2,1)} async-done(((bf16[2,128,2560]{1,2,0:T(8,128)(2,1)}), bf16[2,128,2560]{1,2,0:T(8,128)(2,1)}, u32[]{:S(2)}, u32[]{:S(2)}) %all-to-all-start) | async-done | bytes 1310752 | tf_op jit(solution)/shard_map/all_to_all | solution.py:89
  163.8 3.6 %all-to-all-start.2 = ((bf16[2,128,2560]{2,1,0:T(8,128)(2,1)}), bf16[2,128,2560]{2,1,0:T(8,128)(2,1)S(1)}, u32[]{:S(2)}, u32[]{:S(2)}) async-start(bf16[2,128,2560]{2,1,0:T(8,128)(2,1)} %bitcast.87), calls=%async_computation.2 | async-start | bytes 2621440 | tf_op jit(solution)/shard_map/all_to_all | solution.py:91
  167.4 1.6 copy.63
  169.0 16.9 %all-to-all-done.2 = bf16[2,128,2560]{2,1,0:T(8,128)(2,1)S(1)} async-done(((bf16[2,128,2560]{2,1,0:T(8,128)(2,1)}), bf16[2,128,2560]{2,1,0:T(8,128)(2,1)S(1)}, u32[]{:S(2)}, u32[]{:S(2)}) %all-to-all-start.2) | async-done | bytes 1310752 | tf_op jit(solution)/shard_map/all_to_all | solution.py:91
  185.8 3.6 %all-to-all-start.1 = ((bf16[2,128,2560]{2,1,0:T(8,128)(2,1)}), bf16[2,128,2560]{2,1,0:T(8,128)(2,1)S(1)}, u32[]{:S(2)}, u32[]{:S(2)}) async-start(bf16[2,128,2560]{2,1,0:T(8,128)(2,1)} %bitcast.86), calls=%async_computation.1 | async-start | bytes 2621440 | tf_op jit(solution)/shard_map/all_to_all | solution.py:90
  189.5 2.4 %copy.67 = bf16[128,5120]{1,0:T(8,128)(2,1)} copy(bf16[128,5120]{0,1:T(8,128)(2,1)} %bitcast.12) | data formatting | bytes 2621440
  191.9 1.4 copy.66
  193.3 2.4 %copy.69 = bf16[128,5120]{1,0:T(8,128)(2,1)} copy(bf16[128,5120]{0,1:T(8,128)(2,1)} %bitcast.88) | data formatting | bytes 2621440
  195.8 11.3 %all-to-all-done.1 = bf16[2,128,2560]{2,1,0:T(8,128)(2,1)S(1)} async-done(((bf16[2,128,2560]{2,1,0:T(8,128)(2,1)}), bf16[2,128,2560]{2,1,0:T(8,128)(2,1)S(1)}, u32[]{:S(2)}, u32[]{:S(2)}) %all-to-all-start.1) | async-done | bytes 1310752 | tf_op jit(solution)/shard_map/all_to_all | solution.py:90
  207.1 0.8 copy.64
  207.9 1.4 copy.68
  (20 shorter events, 2.2 us)
Async XLA Ops:
  0.6 5.7 %copy-start.3 = (s32[256,6]{0,1:T(8,128)S(1)}, s32[256,6]{0,1:T(8,128)}, u32[]{:S(2)}) copy-start(s32[256,6]{0,1:T(8,128)} %param.9) | copy-start | bytes 18436
  3.8 2.6 %copy-start.1 = (bf16[256,2560]{0,1:T(8,128)(2,1)}, bf16[256,2560]{0,1:T(8,128)(2,1)S(1)}, u32[]{:S(2)}) copy-start(bf16[256,2560]{0,1:T(8,128)(2,1)S(1)} %copy.51) | copy-start | bytes 3932164
  5.8 29.7 %collective-permute-start.1 = (bf16[2,256,2560]{1,2,0:T(8,128)(2,1)}, bf16[2,256,2560]{1,2,0:T(8,128)(2,1)}, u32[]{:S(2)}, u32[]{:S(2)}) collective-permute-start(bf16[2,256,2560]{1,2,0:T(8,128)(2,1)} %pad_maximum_fusion.2), channel_id=1, source_target_pairs={{2,0},{4,2},{6,4},{8,6},{10,8},{12,10},{14,12},{16,14},{18,16},{20... | collective-permute-start | bytes 7864328 | tf_op jit(solution)/shard_map/ppermute | solution.py:21
  6.0 31.4 %collective-permute-start = (bf16[2,256,2560]{1,2,0:T(8,128)(2,1)}, bf16[2,256,2560]{1,2,0:T(8,128)(2,1)}, u32[]{:S(2)}, u32[]{:S(2)}) collective-permute-start(bf16[2,256,2560]{1,2,0:T(8,128)(2,1)} %pad_maximum_fusion.2), channel_id=1, source_target_pairs={{0,2},{2,4},{4,6},{6,8},{8,10},{10,12},{12,14},{14,16},{16,18},{18... | collective-permute-start | bytes 7864328 | tf_op jit(solution)/shard_map/ppermute | solution.py:20
  41.0 1.3 copy-start.2
  41.6 7.8 %copy-start = (bf16[1,768,2560]{1,2,0:T(8,128)(2,1)}, bf16[1,768,2560]{1,2,0:T(8,128)(2,1)S(1)}, u32[]{:S(2)}) copy-start(bf16[1,768,2560]{1,2,0:T(8,128)(2,1)S(1)} %get-tuple-element.12) | copy-start | bytes 11796484
  102.3 34.4 %collective-permute-start.2 = (bf16[2,256,2560]{1,2,0:T(8,128)(2,1)}, bf16[2,256,2560]{1,2,0:T(8,128)(2,1)}, u32[]{:S(2)}, u32[]{:S(2)}) collective-permute-start(bf16[2,256,2560]{1,2,0:T(8,128)(2,1)} %get-tuple-element.9), channel_id=1, source_target_pairs={{0,254},{2,0},{4,2},{6,4},{8,6},{10,8},{12,10},{14,12},{16,14},{18... | collective-permute-start | bytes 7864328 | tf_op jit(solution)/shard_map/ppermute | solution.py:28
  102.6 34.1 %collective-permute-start.3 = (bf16[2,256,2560]{1,2,0:T(8,128)(2,1)}, bf16[2,256,2560]{1,2,0:T(8,128)(2,1)}, u32[]{:S(2)}, u32[]{:S(2)}) collective-permute-start(bf16[2,256,2560]{1,2,0:T(8,128)(2,1)} %get-tuple-element.10), channel_id=1, source_target_pairs={{0,2},{2,4},{4,6},{6,8},{8,10},{10,12},{12,14},{14,16},{16,18},{18... | collective-permute-start | bytes 7864328 | tf_op jit(solution)/shard_map/ppermute | solution.py:28
  132.2 31.5 %all-to-all-start = ((bf16[2,128,2560]{1,2,0:T(8,128)(2,1)}), bf16[2,128,2560]{1,2,0:T(8,128)(2,1)}, u32[]{:S(2)}, u32[]{:S(2)}) async-start(bf16[2,128,2560]{1,2,0:T(8,128)(2,1)} %copy.60), calls=%async_computation | async-start | bytes 2621440 | tf_op jit(solution)/shard_map/all_to_all | solution.py:89
  163.8 22.1 %all-to-all-start.2 = ((bf16[2,128,2560]{2,1,0:T(8,128)(2,1)}), bf16[2,128,2560]{2,1,0:T(8,128)(2,1)S(1)}, u32[]{:S(2)}, u32[]{:S(2)}) async-start(bf16[2,128,2560]{2,1,0:T(8,128)(2,1)} %bitcast.87), calls=%async_computation.2 | async-start | bytes 2621440 | tf_op jit(solution)/shard_map/all_to_all | solution.py:91
  185.8 21.2 %all-to-all-start.1 = ((bf16[2,128,2560]{2,1,0:T(8,128)(2,1)}), bf16[2,128,2560]{2,1,0:T(8,128)(2,1)S(1)}, u32[]{:S(2)}, u32[]{:S(2)}) async-start(bf16[2,128,2560]{2,1,0:T(8,128)(2,1)} %bitcast.86), calls=%async_computation.1 | async-start | bytes 2621440 | tf_op jit(solution)/shard_map/all_to_all | solution.py:90
where the time goes:
time: 210 us; the launch traced here: 209 us
  waiting for transfers between devices  76.5 us (36%)
  matrix products  74.6 us (36%)
  local copies, waits for them, and re-layouts  22.1 us (11%)
  other arithmetic  21.3 us (10%)
  starting transfers between devices  14.1 us (7%)
    dot_general x1, matrix products, query_pass(): jnp.einsum('hqk,khd->qhd', dscores, key_heads, preferred_element_type=jnp...  26.5 us
    ppermute x1, waiting for transfers between devices, with_halo(): after = lax.ppermute(first, axis, down)  24.9 us
    dot_general x1, matrix products, query_pass(): jnp.einsum('hqk,qhd->khd', dscores, query_heads, preferred_element_type=j...  23.2 us
    all_to_all x1, waiting for transfers between devices, on_device(): lax.all_to_all(grad_query, 'section', split_axis=0, concat_axis=1, tiled=...  21.5 us
    all_to_all x1, waiting for transfers between devices, on_device(): lax.all_to_all(grad_pair[1], 'section', split_axis=0, concat_axis=1, tile...  16.9 us
    unnamed x15, local copies, waits for them, and re-layouts  14.2 us
    all_to_all x1, waiting for transfers between devices, on_device(): lax.all_to_all(grad_pair[0], 'section', split_axis=0, concat_axis=1, tile...  11.3 us
    dot_general x1, matrix products, query_pass(): jnp.einsum('hqk,qhd->khd', weights_low, grad_heads, preferred_element_typ...  10.1 us
  transfers between devices with their start and end apart: 7, of which 5 were waited for; matrix products, arithmetic and copies ran while one was open for 22% of the time, Pallas kernels for 0%

commit v1 on v0

v1 whole, which is shorter than its diff:
```python
import functools
import math

import jax
import jax.numpy as jnp
from jax import lax
from jax.experimental import pallas as pl
from jax.experimental.pallas import tpu as pltpu
from jax.sharding import PartitionSpec as P

HEAD = 128
H = 20
TILE = 128
ROWS = 256
CHUNKS = (5, 5, 5, 5)
SCALE = 1.0 / math.sqrt(HEAD)
LOG2E = math.log2(math.e)
DEAD = -1e30
BF16 = jnp.bfloat16
PARAMS = pltpu.CompilerParams(vmem_limit_bytes=66_000_000)

NT = (((1,), (1,)), ((), ()))
NN = (((1,), (0,)), ((), ()))
TN = (((0,), (0,)), ((), ()))


def dot(a, b, dims):
    return lax.dot_general(a, b, dims, preferred_element_type=jnp.float32)


def split_rows(side, rows, keep_ref, send_ref):
    @pl.when(side == 0)
    def _():
        keep_ref[...] = rows[:TILE]
        send_ref[...] = rows[TILE:]

    @pl.when(side == 1)
    def _():
        keep_ref[...] = rows[TILE:]
        send_ref[...] = rows[:TILE]


def attn_kernel(
    side_ref, q_ref, do_ref, k_ref, v_ref, nk_ref, nv_ref, far_ref, bias_ref, *refs
):
    keep_ref, send_ref, own_ref, near_out, far_out = refs[-5:]
    q, do = q_ref[...], do_ref[...]
    groups = [
        (nk_ref[...], nv_ref[...], near_out),
        (k_ref[...], v_ref[...], own_ref),
        (far_ref[0], far_ref[1], far_out),
    ]
    ts, tops = [], []
    for g, (kg, _, _) in enumerate(groups):
        s = dot(kg, q, NT) * (SCALE * LOG2E)
        for half in range(2):
            t = s[half * TILE : (half + 1) * TILE] + bias_ref[2 * g + half : 2 * g + half + 1, :]
            ts.append(t)
            tops.append(jnp.max(t, axis=0, keepdims=True))
    top = functools.reduce(jnp.maximum, tops)
    es = [jnp.exp2(t - top) for t in ts]
    total = sum(jnp.sum(e, axis=0, keepdims=True) for e in es)
    dps, acc = [], 0.0
    for g, (_, vg, _) in enumerate(groups):
        dp = dot(vg, do, NT)
        for half in range(2):
            d = dp[half * TILE : (half + 1) * TILE]
            dps.append(d)
            acc = acc + jnp.sum(es[2 * g + half] * d, axis=0, keepdims=True)
    inv = 1.0 / total
    delta = acc * inv
    inv_scaled = inv * SCALE
    dq = None
    for g, (kg, _, out) in enumerate(groups):
        pair = (2 * g, 2 * g + 1)
        w = jnp.concatenate([(es[j] * inv).astype(BF16) for j in pair], axis=0)
        ds = jnp.concatenate(
            [((es[j] * inv_scaled) * (dps[j] - delta)).astype(BF16) for j in pair], axis=0
        )
        out[0] = dot(ds, q, NN).astype(BF16)
        out[1] = dot(w, do, NN).astype(BF16)
        part = dot(ds, kg, TN)
        dq = part if dq is None else dq + part
    split_rows(side_ref[0], dq.astype(BF16), keep_ref, send_ref)


def attn_chunk(side, q, do, k, v, near_k, near_v, far, bias, out, h0, hc):
    block = pl.BlockSpec((ROWS, HEAD), lambda i, s: (0, h0 + i))
    pair = pl.BlockSpec((2, ROWS, HEAD), lambda i, s: (0, 0, i))
    specs = [block] * 6 + [pair, pl.BlockSpec((8, ROWS), lambda i, s: (0, 0))]
    args, alias = [q, do, k, v, near_k, near_v, far, bias], {}
    if out is not None:
        specs.append(pl.BlockSpec(memory_space=pl.ANY))
        args.append(out)
        alias = {9: 0}
    return pl.pallas_call(
        attn_kernel,
        grid_spec=pltpu.PrefetchScalarGridSpec(
            num_scalar_prefetch=1,
            grid=(hc,),
            in_specs=specs,
            out_specs=[
                pl.BlockSpec((TILE, HEAD), lambda i, s: (0, s[0] * H + h0 + i)),
                pl.BlockSpec((TILE, HEAD), lambda i, s: (0, i)),
                pair,
                pair,
                pair,
            ],
        ),
        out_shape=[
            pltpu.HBM((TILE, 2 * H * HEAD), BF16),
            pltpu.HBM((TILE, hc * HEAD), BF16),
        ]
        + [pltpu.HBM((2, ROWS, hc * HEAD), BF16)] * 3,
        input_output_aliases=alias,
        compiler_params=PARAMS,
        name="attn",
    )(side, *args)


def combine_kernel(side_ref, own_ref, fn_ref, fp_ref, *refs):
    keep_k, keep_v, send_ref = refs[-3:]
    f32 = jnp.float32
    for j, keep in enumerate((keep_k, keep_v)):
        total = own_ref[j].astype(f32) + fn_ref[j].astype(f32) + fp_ref[j].astype(f32)
        split_rows(side_ref[0], total.astype(BF16), keep, send_ref.at[pl.ds(j * TILE, TILE)])


def combine(side, own, from_near, from_far, outs, h0, hc):
    pair = pl.BlockSpec((2, ROWS, HEAD), lambda i, s: (0, 0, i))
    specs, args, alias = [pair] * 3, [own, from_near, from_far], {}
    if outs is not None:
        specs += [pl.BlockSpec(memory_space=pl.ANY)] * 2
        args += list(outs)
        alias = {4: 0, 5: 1}
    keep = pl.BlockSpec((TILE, HEAD), lambda i, s: (0, s[0] * H + h0 + i))
    return pl.pallas_call(
        combine_kernel,
        grid_spec=pltpu.PrefetchScalarGridSpec(
            num_scalar_prefetch=1,
            grid=(hc,),
            in_specs=specs,
            out_specs=[keep, keep, pl.BlockSpec((2 * TILE, HEAD), lambda i, s: (0, i))],
        ),
        out_shape=[pltpu.HBM((TILE, 2 * H * HEAD), BF16)] * 2
        + [pltpu.HBM((2 * TILE, hc * HEAD), BF16)],
        input_output_aliases=alias,
        compiler_params=PARAMS,
        name="combine",
    )(side, *args)


def place_kernel(side_ref, src_ref, *refs):
    outs = refs[len(refs) // 2 :]
    for j, out in enumerate(outs):
        out[...] = src_ref[j * TILE : (j + 1) * TILE]


def place(side, part, outs, h0, hc):
    n = len(outs)
    dest = pl.BlockSpec((TILE, HEAD), lambda i, s: (0, (1 - s[0]) * H + h0 + i))
    return pl.pallas_call(
        place_kernel,
        grid_spec=pltpu.PrefetchScalarGridSpec(
            num_scalar_prefetch=1,
            grid=(hc,),
            in_specs=[pl.BlockSpec((n * TILE, HEAD), lambda i, s: (0, i))]
            + [pl.BlockSpec(memory_space=pl.ANY)] * n,
            out_specs=[dest] * n,
        ),
        out_shape=[pltpu.HBM((TILE, 2 * H * HEAD), BF16)] * n,
        input_output_aliases={2 + j: j for j in range(n)},
        compiler_params=PARAMS,
        name="place",
    )(side, part, *outs)


def pack_kernel(k_ref, v_ref, out_ref):
    out_ref[0] = k_ref[...]
    out_ref[1] = v_ref[...]


def pack(k, v, h0, hc):
    block = pl.BlockSpec((ROWS, HEAD), lambda i: (0, h0 + i))
    return pl.pallas_call(
        pack_kernel,
        grid=(hc,),
        in_specs=[block] * 2,
        out_specs=pl.BlockSpec((2, ROWS, HEAD), lambda i: (0, 0, i)),
        out_shape=pltpu.HBM((2, ROWS, hc * HEAD), BF16),
        compiler_params=PARAMS,
        name="pack",
    )(k, v)


def near_swap(x):
    return lax.ppermute(x, "ctx", [(i, i ^ 1) for i in range(lax.axis_size("ctx"))])


def far_swap(x):
    count = lax.axis_size("ctx")
    return lax.ppermute(x, "ctx", [(i, (i + 2 * (i % 2) - 1) % count) for i in range(count)])


def swap(x):
    return lax.ppermute(x, "section", [(0, 1), (1, 0)])


def split_heads(sizes):
    return [(sum(sizes[:n]), size) for n, size in enumerate(sizes)]


def on_device(queries, key_states, value_states, out_grad, tile_mask):
    position = lax.axis_index("ctx")
    side = lax.axis_index("section").astype(jnp.int32).reshape(1)
    own_mask = lax.dynamic_slice_in_dim(tile_mask, position * 2, 2, 0)
    bias = jnp.where(jnp.repeat(own_mask.T, TILE, axis=1) > 0, 0.0, DEAD).astype(jnp.float32)
    before, own, after = bias[0:2], bias[2:4], bias[4:6]
    odd = position % 2 == 1
    near = jnp.where(odd, before, after)
    far = jnp.where(odd, after, before)
    bias = jnp.concatenate([near, own, far, jnp.zeros((2, ROWS), jnp.float32)], axis=0)

    spans = split_heads(CHUNKS)
    count = len(spans)
    near_k, near_v = near_swap(key_states), near_swap(value_states)
    packs, source = [pack(key_states, value_states, *spans[0])], key_states
    source, near_k = lax.optimization_barrier((source, near_k))
    for h0, hc in spans[1:]:
        packs.append(pack(source, value_states, h0, hc))
        source, packs[-1] = lax.optimization_barrier((source, packs[-1]))
    fars = [far_swap(packs[0]), far_swap(packs[1])]
    bias, *_ = lax.optimization_barrier((bias, *packs))

    out_q, out_kv = None, None
    q_parts, kv_parts, owns, from_far, from_near = [], [], [], [], []

    def finish(n, own):
        nonlocal out_kv
        h0, hc = spans[n]
        *out_kv, send = combine(side, own, from_near[n], from_far[n], out_kv, h0, hc)
        kv_parts.append(swap(send))

    def after(arrived, *values):
        held = lax.optimization_barrier((*values, *(where[i] for where, i in arrived)))
        for (where, i), value in zip(arrived, held[len(values) :]):
            where[i] = value
        return held[: len(values)]

    nears = []
    for n, (h0, hc) in enumerate(spans):
        if n >= 1:
            arrived = [(fars, n)] + ([(from_far, n - 2)] if n >= 2 else [])
            (near_part,) = after(arrived, nears[n - 1])
            from_near.append(near_swap(near_part))
            if n >= 2:
                finish(n - 2, owns[n - 2])
        out_q, send_q, own, near_part, far_part = attn_chunk(
            side, queries, out_grad, key_states, value_states, near_k, near_v, fars[n], bias,
            out_q, h0, hc,
        )
        arrived = []
        if n >= 1:
            arrived += [(q_parts, n - 1), (from_near, n - 1)]
        if 2 <= n < count - 1:
            arrived.append((kv_parts, n - 2))
        if n + 2 < count:
            arrived.append((packs, n + 2))
        send_q, own, near_part, far_part = after(arrived, send_q, own, near_part, far_part)
        from_far.append(far_swap(far_part))
        if n + 2 < count:
            fars.append(far_swap(packs[n + 2]))
        q_parts.append(swap(send_q))
        nears.append(near_part)
        owns.append(own)
    from_near.append(near_swap(nears[-1]))
    for n in range(max(count - 2, 0), count):
        finish(n, owns[n])
    for (h0, hc), part in zip(spans, q_parts):
        (out_q,) = place(side, part, [out_q], h0, hc)
    for (h0, hc), part in zip(spans, kv_parts):
        out_kv = place(side, part, out_kv, h0, hc)
    return (out_q, *out_kv)


def solution(mesh):
    placed = P("ctx", "section")
    out = P(("ctx", "section"), None)
    return jax.shard_map(
        on_device,
        mesh=mesh,
        in_specs=(placed, placed, placed, placed, P()),
        out_specs=(out, out, out),
        check_vma=False,
    )
```

time: 210 us -> 166 us (0.79)
  the two profiles are of different devices: /device:TPU:24 before, /device:TPU:230 now
where the time goes in v1:
time: 166 us; the launch traced here: 163 us
  Pallas kernels  85.6 us (52%)
  waiting for transfers between devices  37.8 us (23%)
  starting transfers between devices  32.6 us (20%)
  local copies, waits for them, and re-layouts  4.96 us (3%)
    ppermute x8, waiting for transfers between devices, swap(): return lax.ppermute(x, 'section', [(0, 1), (1, 0)])  37.8 us
    pallas_call x4, Pallas kernels, attn_chunk(): pl.pallas_call(attn_kernel, grid_spec=pltpu.PrefetchScalarGridSpec(num_sc...  30.2 us
    pallas_call x8, Pallas kernels, place(): pl.pallas_call(place_kernel, grid_spec=pltpu.PrefetchScalarGridSpec(num_s...  24.7 us
    pallas_call x4, Pallas kernels, combine(): pl.pallas_call(combine_kernel, grid_spec=pltpu.PrefetchScalarGridSpec(num...  16.7 us
    ppermute x8, starting transfers between devices, swap(): return lax.ppermute(x, 'section', [(0, 1), (1, 0)])  16.2 us
    ppermute x8, starting transfers between devices, far_swap(): lax.ppermute(x, 'ctx', [(i, (i + 2 * (i % 2) - 1) % count) for i in range...  15.5 us
    pallas_call x4, Pallas kernels, pack(): pl.pallas_call(pack_kernel, grid=(hc,), in_specs=[block] * 2, out_specs=p...  14 us
    unnamed x25, local copies, waits for them, and re-layouts  4.88 us
  transfers between devices with their start and end apart: 22, of which 3 were waited for; matrix products, arithmetic and copies ran while one was open for 1% of the time, Pallas kernels for 51%

profile of v1, /device:TPU:230, one launch (start us, length us, event | category | flops | bytes accessed | tf_op | source)
XLA Modules:
  0.0 162.5 jit_solution(17882142476194328856)
XLA Ops:
  1.2 3.5 %pack.4 = bf16[2,256,640]{2,1,0:T(8,128)(2,1)} custom-call(bf16[256,2560]{1,0:T(8,128)(2,1)} %k_ref.12, bf16[256,2560]{1,0:T(8,128)(2,1)} %v_ref.15), custom_call_target="tpu_custom_call" | custom-call | tf_op jit(solution)/shard_map/pack/pallas_call | solution.py:185
  4.7 3.2 %collective-permute-start.2 = (bf16[2,256,640]{2,1,0:T(8,128)(2,1)}, bf16[2,256,640]{2,1,0:T(8,128)(2,1)S(1)}, u32[]{:S(2)}, u32[]{:S(2)}) collective-permute-start(bf16[2,256,640]{2,1,0:T(8,128)(2,1)} %pack.4), channel_id=1, source_target_pairs={{0,254},{2,4},{4,2},{6,8},{8,6},{10,12},{12,10},{14,16},{16,14},{1... | collective-permute-start | bytes 1966088 | tf_op jit(solution)/shard_map/ppermute | solution.py:202
  8.0 3.5 %pack.5 = bf16[2,256,640]{2,1,0:T(8,128)(2,1)} custom-call(bf16[256,2560]{1,0:T(8,128)(2,1)} %k_ref.12, bf16[256,2560]{1,0:T(8,128)(2,1)} %v_ref.15), custom_call_target="tpu_custom_call" | custom-call | tf_op jit(solution)/shard_map/pack/pallas_call | solution.py:185
  13.1 3.5 %pack.6 = bf16[2,256,640]{2,1,0:T(8,128)(2,1)} custom-call(bf16[256,2560]{1,0:T(8,128)(2,1)} %k_ref.12, bf16[256,2560]{1,0:T(8,128)(2,1)} %v_ref.15), custom_call_target="tpu_custom_call" | custom-call | tf_op jit(solution)/shard_map/pack/pallas_call | solution.py:185
  16.6 3.5 %pack.7 = bf16[2,256,640]{2,1,0:T(8,128)(2,1)} custom-call(bf16[256,2560]{1,0:T(8,128)(2,1)} %k_ref.12, bf16[256,2560]{1,0:T(8,128)(2,1)} %v_ref.15), custom_call_target="tpu_custom_call" | custom-call | tf_op jit(solution)/shard_map/pack/pallas_call | solution.py:185
  20.9 7.6 %attn.4 = (bf16[128,5120]{1,0:T(8,128)(2,1)}, bf16[128,640]{1,0:T(8,128)(2,1)}, bf16[2,256,640]{2,1,0:T(8,128)(2,1)}, bf16[2,256,640]{2,1,0:T(8,128)(2,1)}, bf16[2,256,640]{2,1,0:T(8,128)(2,1)}) custom-call(s32[1]{0:T(128)} %bitcast.side_ref, bf16[256,2560]{1,0:T(8,128)(2,1)} %q_ref.7, bf16[256,2560]{1,0:T(8,128)(2,1)} %do_ref.7, bf16[256,2560]{1,0:T(8,128)(2,1)} %k_ref.12, ...), custom_call_target="tpu_custom_call" | custom-call | tf_op jit(solution)/shard_map/attn/pallas_call | solution.py:96
  28.7 3.3 %collective-permute-start.6 = (bf16[2,256,640]{2,1,0:T(8,128)(2,1)}, bf16[2,256,640]{2,1,0:T(8,128)(2,1)S(1)}, u32[]{:S(2)}, u32[]{:S(2)}) collective-permute-start(bf16[2,256,640]{2,1,0:T(8,128)(2,1)} %pack.6), channel_id=1, source_target_pairs={{0,254},{2,4},{4,2},{6,8},{8,6},{10,12},{12,10},{14,16},{16,14},{1... | collective-permute-start | bytes 1966088 | tf_op jit(solution)/shard_map/ppermute | solution.py:202
  32.6 1.4 collective-permute-start.4
  34.0 7.5 %attn.5 = (bf16[128,5120]{1,0:T(8,128)(2,1)}, bf16[128,640]{1,0:T(8,128)(2,1)}, bf16[2,256,640]{2,1,0:T(8,128)(2,1)}, bf16[2,256,640]{2,1,0:T(8,128)(2,1)}, bf16[2,256,640]{2,1,0:T(8,128)(2,1)}) custom-call(s32[1]{0:T(128)} %bitcast.side_ref, bf16[256,2560]{1,0:T(8,128)(2,1)} %q_ref.7, bf16[256,2560]{1,0:T(8,128)(2,1)} %do_ref.7, ...), custom_call_target="tpu_custom_call", output_to_operand_aliasing={{0}: (9, {})} | custom-call | tf_op jit(solution)/shard_map/attn/pallas_call | solution.py:96
  41.5 12.1 %collective-permute-done.4.src_ref = bf16[128,640]{1,0:T(8,128)(2,1)S(1)} collective-permute-done((bf16[128,640]{1,0:T(8,128)(2,1)}, bf16[128,640]{1,0:T(8,128)(2,1)S(1)}, u32[]{:S(2)}, u32[]{:S(2)}) %collective-permute-start.4) | collective-permute-done | bytes 163872 | tf_op jit(solution)/shard_map/ppermute | solution.py:206
  54.6 3.9 %collective-permute-start.12 = (bf16[2,256,640]{2,1,0:T(8,128)(2,1)}, bf16[2,256,640]{2,1,0:T(8,128)(2,1)}, u32[]{:S(2)}, u32[]{:S(2)}) collective-permute-start(bf16[2,256,640]{2,1,0:T(8,128)(2,1)} %get-tuple-element.122), channel_id=1, source_target_pairs={{0,254},{2,4},{4,2},{6,8},{8,6},{10,12},{12,10},{14,16},{16,14},{1... | collective-permute-start | bytes 1966088 | tf_op jit(solution)/shard_map/ppermute | solution.py:202
  58.4 4.2 %combine.4 = (bf16[128,5120]{1,0:T(8,128)(2,1)}, bf16[128,5120]{1,0:T(8,128)(2,1)}, bf16[256,640]{1,0:T(8,128)(2,1)}) custom-call(s32[1]{0:T(128)} %bitcast.side_ref, bf16[2,256,640]{2,1,0:T(8,128)(2,1)} %get-tuple-element.116.own_ref, bf16[2,256,640]{2,1,0:T(8,128)(2,1)} %collective-permute-done.5.fn_ref, bf16[2,256,640]{2,1,0:T(8,128)(2,1)} %collective-permute-done.7.fp_ref), custom_call_target="tpu_custom_call" | custom-call | tf_op jit(solution)/shard_map/combine/pallas_call | solution.py:137
  62.7 3.5 %collective-permute-start.8 = (bf16[128,640]{1,0:T(8,128)(2,1)}, bf16[128,640]{1,0:T(8,128)(2,1)}, u32[]{:S(2)}, u32[]{:S(2)}) collective-permute-start(bf16[128,640]{1,0:T(8,128)(2,1)} %get-tuple-element.114), channel_id=1, source_target_pairs={{0,1},{1,0},{2,3},{3,2},{4,5},{5,4},{6,7},{7,6},{8,9},{9,8},{10,11... | collective-permute-start | bytes 491528 | tf_op jit(solution)/shard_map/ppermute | solution.py:206
  66.2 7.5 %attn.6 = (bf16[128,5120]{1,0:T(8,128)(2,1)}, bf16[128,640]{1,0:T(8,128)(2,1)}, bf16[2,256,640]{2,1,0:T(8,128)(2,1)}, bf16[2,256,640]{2,1,0:T(8,128)(2,1)}, bf16[2,256,640]{2,1,0:T(8,128)(2,1)}) custom-call(s32[1]{0:T(128)} %bitcast.side_ref, bf16[256,2560]{1,0:T(8,128)(2,1)} %q_ref.7, bf16[256,2560]{1,0:T(8,128)(2,1)} %do_ref.7, ...), custom_call_target="tpu_custom_call", output_to_operand_aliasing={{0}: (9, {})} | custom-call | tf_op jit(solution)/shard_map/attn/pallas_call | solution.py:96
  73.7 23.8 %collective-permute-done.8.src_ref = bf16[128,640]{1,0:T(8,128)(2,1)} collective-permute-done((bf16[128,640]{1,0:T(8,128)(2,1)}, bf16[128,640]{1,0:T(8,128)(2,1)}, u32[]{:S(2)}, u32[]{:S(2)}) %collective-permute-start.8) | collective-permute-done | bytes 163872 | tf_op jit(solution)/shard_map/ppermute | solution.py:206
  97.7 4.1 %collective-permute-start.13 = (bf16[128,640]{1,0:T(8,128)(2,1)}, bf16[128,640]{1,0:T(8,128)(2,1)}, u32[]{:S(2)}, u32[]{:S(2)}) collective-permute-start(bf16[128,640]{1,0:T(8,128)(2,1)} %get-tuple-element.129), channel_id=1, source_target_pairs={{0,1},{1,0},{2,3},{3,2},{4,5},{5,4},{6,7},{7,6},{8,9},{9,8},{10,11... | collective-permute-start | bytes 491528 | tf_op jit(solution)/shard_map/ppermute | solution.py:206
  101.8 7.5 %attn.7 = (bf16[128,5120]{1,0:T(8,128)(2,1)}, bf16[128,640]{1,0:T(8,128)(2,1)}, bf16[2,256,640]{2,1,0:T(8,128)(2,1)}, bf16[2,256,640]{2,1,0:T(8,128)(2,1)}, bf16[2,256,640]{2,1,0:T(8,128)(2,1)}) custom-call(s32[1]{0:T(128)} %bitcast.side_ref, bf16[256,2560]{1,0:T(8,128)(2,1)} %q_ref.7, bf16[256,2560]{1,0:T(8,128)(2,1)} %do_ref.7, ...), custom_call_target="tpu_custom_call", output_to_operand_aliasing={{0}: (9, {})} | custom-call | tf_op jit(solution)/shard_map/attn/pallas_call | solution.py:96
  109.6 3.8 %collective-permute-start.17 = (bf16[2,256,640]{2,1,0:T(8,128)(2,1)}, bf16[2,256,640]{2,1,0:T(8,128)(2,1)}, u32[]{:S(2)}, u32[]{:S(2)}) collective-permute-start(bf16[2,256,640]{2,1,0:T(8,128)(2,1)} %get-tuple-element.138), channel_id=1, source_target_pairs={{0,254},{2,4},{4,2},{6,8},{8,6},{10,12},{12,10},{14,16},{16,14},{1... | collective-permute-start | bytes 1966088 | tf_op jit(solution)/shard_map/ppermute | solution.py:202
  113.4 4.2 %combine.5 = (bf16[128,5120]{1,0:T(8,128)(2,1)}, bf16[128,5120]{1,0:T(8,128)(2,1)}, bf16[256,640]{1,0:T(8,128)(2,1)}) custom-call(s32[1]{0:T(128)} %bitcast.side_ref, bf16[2,256,640]{2,1,0:T(8,128)(2,1)} %get-tuple-element.142.own_ref, bf16[2,256,640]{2,1,0:T(8,128)(2,1)} %collective-permute-done.9.fn_ref, ...), custom_call_target="tpu_custom_call", output_to_operand_aliasing={{0}: (4, {}), {1}: (5, {})} | custom-call | tf_op jit(solution)/shard_map/combine/pallas_call | solution.py:137
  117.8 4.2 %combine.6 = (bf16[128,5120]{1,0:T(8,128)(2,1)}, bf16[128,5120]{1,0:T(8,128)(2,1)}, bf16[256,640]{1,0:T(8,128)(2,1)}) custom-call(s32[1]{0:T(128)} %bitcast.side_ref, bf16[2,256,640]{2,1,0:T(8,128)(2,1)} %get-tuple-element.139.own_ref, bf16[2,256,640]{2,1,0:T(8,128)(2,1)} %collective-permute-done.14.fn_ref, ...), custom_call_target="tpu_custom_call", output_to_operand_aliasing={{0}: (4, {}), {1}: (5, {})} | custom-call | tf_op jit(solution)/shard_map/combine/pallas_call | solution.py:137
  122.0 3.2 %collective-permute-start.20 = (bf16[256,640]{1,0:T(8,128)(2,1)}, bf16[256,640]{1,0:T(8,128)(2,1)}, u32[]{:S(2)}, u32[]{:S(2)}) collective-permute-start(bf16[256,640]{1,0:T(8,128)(2,1)} %get-tuple-element.152), channel_id=1, source_target_pairs={{0,1},{1,0},{2,3},{3,2},{4,5},{5,4},{6,7},{7,6},{8,9},{9,8},{10,11... | collective-permute-start | bytes 983048 | tf_op jit(solution)/shard_map/ppermute | solution.py:206
  126.2 4.2 %combine.7 = (bf16[128,5120]{1,0:T(8,128)(2,1)}, bf16[128,5120]{1,0:T(8,128)(2,1)}, bf16[256,640]{1,0:T(8,128)(2,1)}) custom-call(s32[1]{0:T(128)} %bitcast.side_ref, bf16[2,256,640]{2,1,0:T(8,128)(2,1)} %get-tuple-element.136.own_ref, bf16[2,256,640]{2,1,0:T(8,128)(2,1)} %copy-done.3, ...), custom_call_target="tpu_custom_call", output_to_operand_aliasing={{0}: (4, {}), {1}: (5, {})} | custom-call | tf_op jit(solution)/shard_map/combine/pallas_call | solution.py:137
  130.6 3.2 %collective-permute-start.15 = (bf16[128,640]{1,0:T(8,128)(2,1)}, bf16[128,640]{1,0:T(8,128)(2,1)S(1)}, u32[]{:S(2)}, u32[]{:S(2)}) collective-permute-start(bf16[128,640]{1,0:T(8,128)(2,1)} %get-tuple-element.131), channel_id=1, source_target_pairs={{0,1},{1,0},{2,3},{3,2},{4,5},{5,4},{6,7},{7,6},{8,9},{9,8},{10,11... | collective-permute-start | bytes 491528 | tf_op jit(solution)/shard_map/ppermute | solution.py:206
  133.8 2.9 %place.8.refs_0_ = bf16[128,5120]{1,0:T(8,128)(2,1)} custom-call(s32[1]{0:T(128)} %bitcast.side_ref, bf16[128,640]{1,0:T(8,128)(2,1)} %copy-done.7, bf16[128,5120]{1,0:T(8,128)(2,1)} %get-tuple-element.135.refs_0_), custom_call_target="tpu_custom_call", output_to_operand_aliasing={{}: (2, {})} | custom-call | tf_op jit(solution)/shard_map/place/pallas_call | solution.py:162
  136.8 2.9 %place.9.refs_0_ = bf16[128,5120]{1,0:T(8,128)(2,1)} custom-call(s32[1]{0:T(128)} %bitcast.side_ref, bf16[128,640]{1,0:T(8,128)(2,1)} %collective-permute-done.8.src_ref, bf16[128,5120]{1,0:T(8,128)(2,1)} %place.8.refs_0_), custom_call_target="tpu_custom_call", output_to_operand_aliasing={{}: (2, {})} | custom-call | tf_op jit(solution)/shard_map/place/pallas_call | solution.py:162
  139.7 2.9 %place.10.refs_0_ = bf16[128,5120]{1,0:T(8,128)(2,1)} custom-call(s32[1]{0:T(128)} %bitcast.side_ref, bf16[128,640]{1,0:T(8,128)(2,1)} %collective-permute-done.13.src_ref, bf16[128,5120]{1,0:T(8,128)(2,1)} %place.9.refs_0_), custom_call_target="tpu_custom_call", output_to_operand_aliasing={{}: (2, {})} | custom-call | tf_op jit(solution)/shard_map/place/pallas_call | solution.py:162
  142.7 1.8 %collective-permute-done.15.src_ref = bf16[128,640]{1,0:T(8,128)(2,1)S(1)} collective-permute-done((bf16[128,640]{1,0:T(8,128)(2,1)}, bf16[128,640]{1,0:T(8,128)(2,1)S(1)}, u32[]{:S(2)}, u32[]{:S(2)}) %collective-permute-start.15) | collective-permute-done | bytes 163872 | tf_op jit(solution)/shard_map/ppermute | solution.py:206
  145.1 2.9 %place.11 = bf16[128,5120]{1,0:T(8,128)(2,1)} custom-call(s32[1]{0:T(128)} %bitcast.side_ref, bf16[128,640]{1,0:T(8,128)(2,1)} %copy-done.8, bf16[128,5120]{1,0:T(8,128)(2,1)} %place.10.refs_0_), custom_call_target="tpu_custom_call", output_to_operand_aliasing={{}: (2, {})} | custom-call | tf_op jit(solution)/shard_map/place/pallas_call | solution.py:162
  148.1 3.2 %place.12 = (bf16[128,5120]{1,0:T(8,128)(2,1)}, bf16[128,5120]{1,0:T(8,128)(2,1)}) custom-call(s32[1]{0:T(128)} %bitcast.side_ref, bf16[256,640]{1,0:T(8,128)(2,1)} %copy-done.4, bf16[128,5120]{1,0:T(8,128)(2,1)} %get-tuple-element.155.refs_0_, bf16[128,5120]{1,0:T(8,128)(2,1)} %get-tuple-element.156.refs_1_), custom_call_target="tpu_custom_call", output_to_operand_aliasing={{0}: (2, {}), {1}: (3, {})} | custom-call | tf_op jit(solution)/shard_map/place/pallas_call | solution.py:162
  152.1 3.2 %place.13 = (bf16[128,5120]{1,0:T(8,128)(2,1)}, bf16[128,5120]{1,0:T(8,128)(2,1)}) custom-call(s32[1]{0:T(128)} %bitcast.side_ref, bf16[256,640]{1,0:T(8,128)(2,1)} %copy-done.5, bf16[128,5120]{1,0:T(8,128)(2,1)} %get-tuple-element.157.refs_0_, bf16[128,5120]{1,0:T(8,128)(2,1)} %get-tuple-element.158.refs_1_), custom_call_target="tpu_custom_call", output_to_operand_aliasing={{0}: (2, {}), {1}: (3, {})} | custom-call | tf_op jit(solution)/shard_map/place/pallas_call | solution.py:162
  155.3 3.2 %place.14 = (bf16[128,5120]{1,0:T(8,128)(2,1)}, bf16[128,5120]{1,0:T(8,128)(2,1)}) custom-call(s32[1]{0:T(128)} %bitcast.side_ref, bf16[256,640]{1,0:T(8,128)(2,1)} %collective-permute-done.20.src_ref, bf16[128,5120]{1,0:T(8,128)(2,1)} %get-tuple-element.159.refs_0_, ...), custom_call_target="tpu_custom_call", output_to_operand_aliasing={{0}: (2, {}), {1}: (3, {})} | custom-call | tf_op jit(solution)/shard_map/place/pallas_call | solution.py:162
  159.3 3.2 %place.15 = (bf16[128,5120]{1,0:T(8,128)(2,1)}, bf16[128,5120]{1,0:T(8,128)(2,1)}) custom-call(s32[1]{0:T(128)} %bitcast.side_ref, bf16[256,640]{1,0:T(8,128)(2,1)} %copy-done.6, bf16[128,5120]{1,0:T(8,128)(2,1)} %get-tuple-element.161.refs_0_, bf16[128,5120]{1,0:T(8,128)(2,1)} %get-tuple-element.162.refs_1_), custom_call_target="tpu_custom_call", output_to_operand_aliasing={{0}: (2, {}), {1}: (3, {})} | custom-call | tf_op jit(solution)/shard_map/place/pallas_call | solution.py:162
  (62 shorter events, 8.8 us)
Async XLA Ops:
  0.6 7.3 %copy-start.9 = (s32[256,6]{0,1:T(8,128)S(1)}, s32[256,6]{0,1:T(8,128)}, u32[]{:S(2)}) copy-start(s32[256,6]{0,1:T(8,128)} %param.9) | copy-start | bytes 18436
  0.6 7.3 %collective-permute-start = (bf16[256,2560]{1,0:T(8,128)(2,1)}, bf16[256,2560]{1,0:T(8,128)(2,1)}, u32[]{:S(2)}, u32[]{:S(2)}) collective-permute-start(bf16[256,2560]{1,0:T(8,128)(2,1)} %k_ref.12), channel_id=1, source_target_pairs={{0,2},{2,0},{4,6},{6,4},{8,10},{10,8},{12,14},{14,12},{16,18},{18,... | collective-permute-start | bytes 3932168 | tf_op jit(solution)/shard_map/ppermute | solution.py:197
  0.7 19.4 %collective-permute-start.1 = (bf16[256,2560]{1,0:T(8,128)(2,1)}, bf16[256,2560]{1,0:T(8,128)(2,1)}, u32[]{:S(2)}, u32[]{:S(2)}) collective-permute-start(bf16[256,2560]{1,0:T(8,128)(2,1)} %v_ref.15), channel_id=1, source_target_pairs={{0,2},{2,0},{4,6},{6,4},{8,10},{10,8},{12,14},{14,12},{16,18},{18,... | collective-permute-start | bytes 3932168 | tf_op jit(solution)/shard_map/ppermute | solution.py:197
  4.7 15.4 %collective-permute-start.2 = (bf16[2,256,640]{2,1,0:T(8,128)(2,1)}, bf16[2,256,640]{2,1,0:T(8,128)(2,1)S(1)}, u32[]{:S(2)}, u32[]{:S(2)}) collective-permute-start(bf16[2,256,640]{2,1,0:T(8,128)(2,1)} %pack.4), channel_id=1, source_target_pairs={{0,254},{2,4},{4,2},{6,8},{8,6},{10,12},{12,10},{14,16},{16,14},{1... | collective-permute-start | bytes 1966088 | tf_op jit(solution)/shard_map/ppermute | solution.py:202
  11.5 17.1 %collective-permute-start.3 = (bf16[2,256,640]{2,1,0:T(8,128)(2,1)}, bf16[2,256,640]{2,1,0:T(8,128)(2,1)}, u32[]{:S(2)}, u32[]{:S(2)}) collective-permute-start(bf16[2,256,640]{2,1,0:T(8,128)(2,1)} %pack.5), channel_id=1, source_target_pairs={{0,254},{2,4},{4,2},{6,8},{8,6},{10,12},{12,10},{14,16},{16,14},{1... | collective-permute-start | bytes 1966088 | tf_op jit(solution)/shard_map/ppermute | solution.py:202
  20.1 0.8 copy-start
  28.6 25.1 %collective-permute-start.5 = (bf16[2,256,640]{2,1,0:T(8,128)(2,1)}, bf16[2,256,640]{2,1,0:T(8,128)(2,1)}, u32[]{:S(2)}, u32[]{:S(2)}) collective-permute-start(bf16[2,256,640]{2,1,0:T(8,128)(2,1)} %get-tuple-element.104), channel_id=1, source_target_pairs={{0,2},{2,0},{4,6},{6,4},{8,10},{10,8},{12,14},{14,12},{16,18},{18,... | collective-permute-start | bytes 1966088 | tf_op jit(solution)/shard_map/ppermute | solution.py:197
  28.7 25.0 %collective-permute-start.6 = (bf16[2,256,640]{2,1,0:T(8,128)(2,1)}, bf16[2,256,640]{2,1,0:T(8,128)(2,1)S(1)}, u32[]{:S(2)}, u32[]{:S(2)}) collective-permute-start(bf16[2,256,640]{2,1,0:T(8,128)(2,1)} %pack.6), channel_id=1, source_target_pairs={{0,254},{2,4},{4,2},{6,8},{8,6},{10,12},{12,10},{14,16},{16,14},{1... | collective-permute-start | bytes 1966088 | tf_op jit(solution)/shard_map/ppermute | solution.py:202
  31.9 21.8 %collective-permute-start.7 = (bf16[2,256,640]{2,1,0:T(8,128)(2,1)}, bf16[2,256,640]{2,1,0:T(8,128)(2,1)}, u32[]{:S(2)}, u32[]{:S(2)}) collective-permute-start(bf16[2,256,640]{2,1,0:T(8,128)(2,1)} %get-tuple-element.107), channel_id=1, source_target_pairs={{0,254},{2,4},{4,2},{6,8},{8,6},{10,12},{12,10},{14,16},{16,14},{1... | collective-permute-start | bytes 1966088 | tf_op jit(solution)/shard_map/ppermute | solution.py:202
  32.6 21.1 %collective-permute-start.4 = (bf16[128,640]{1,0:T(8,128)(2,1)}, bf16[128,640]{1,0:T(8,128)(2,1)S(1)}, u32[]{:S(2)}, u32[]{:S(2)}) collective-permute-start(bf16[128,640]{1,0:T(8,128)(2,1)} %get-tuple-element.103), channel_id=1, source_target_pairs={{0,1},{1,0},{2,3},{3,2},{4,5},{5,4},{6,7},{7,6},{8,9},{9,8},{10,11... | collective-permute-start | bytes 491528 | tf_op jit(solution)/shard_map/ppermute | solution.py:206
  53.7 8.9 %copy-start.7 = (bf16[128,640]{1,0:T(8,128)(2,1)}, bf16[128,640]{1,0:T(8,128)(2,1)S(1)}, u32[]{:S(2)}) copy-start(bf16[128,640]{1,0:T(8,128)(2,1)S(1)} %collective-permute-done.4.src_ref) | copy-start | bytes 491524
  53.7 0.9 copy-start.2
  54.6 43.0 %collective-permute-start.9 = (bf16[2,256,640]{2,1,0:T(8,128)(2,1)}, bf16[2,256,640]{2,1,0:T(8,128)(2,1)}, u32[]{:S(2)}, u32[]{:S(2)}) collective-permute-start(bf16[2,256,640]{2,1,0:T(8,128)(2,1)} %get-tuple-element.115), channel_id=1, source_target_pairs={{0,2},{2,0},{4,6},{6,4},{8,10},{10,8},{12,14},{14,12},{16,18},{18,... | collective-permute-start | bytes 1966088 | tf_op jit(solution)/shard_map/ppermute | solution.py:197
  54.6 43.0 %collective-permute-start.11 = (bf16[2,256,640]{2,1,0:T(8,128)(2,1)}, bf16[2,256,640]{2,1,0:T(8,128)(2,1)S(1)}, u32[]{:S(2)}, u32[]{:S(2)}) collective-permute-start(bf16[2,256,640]{2,1,0:T(8,128)(2,1)} %pack.7), channel_id=1, source_target_pairs={{0,254},{2,4},{4,2},{6,8},{8,6},{10,12},{12,10},{14,16},{16,14},{1... | collective-permute-start | bytes 1966088 | tf_op jit(solution)/shard_map/ppermute | solution.py:202
  54.6 43.0 %collective-permute-start.12 = (bf16[2,256,640]{2,1,0:T(8,128)(2,1)}, bf16[2,256,640]{2,1,0:T(8,128)(2,1)}, u32[]{:S(2)}, u32[]{:S(2)}) collective-permute-start(bf16[2,256,640]{2,1,0:T(8,128)(2,1)} %get-tuple-element.122), channel_id=1, source_target_pairs={{0,254},{2,4},{4,2},{6,8},{8,6},{10,12},{12,10},{14,16},{16,14},{1... | collective-permute-start | bytes 1966088 | tf_op jit(solution)/shard_map/ppermute | solution.py:202
  62.6 34.9 %collective-permute-start.10 = (bf16[256,640]{1,0:T(8,128)(2,1)}, bf16[256,640]{1,0:T(8,128)(2,1)S(1)}, u32[]{:S(2)}, u32[]{:S(2)}) collective-permute-start(bf16[256,640]{1,0:T(8,128)(2,1)} %get-tuple-element.119), channel_id=1, source_target_pairs={{0,1},{1,0},{2,3},{3,2},{4,5},{5,4},{6,7},{7,6},{8,9},{9,8},{10,11... | collective-permute-start | bytes 983048 | tf_op jit(solution)/shard_map/ppermute | solution.py:206
  62.7 34.9 %collective-permute-start.8 = (bf16[128,640]{1,0:T(8,128)(2,1)}, bf16[128,640]{1,0:T(8,128)(2,1)}, u32[]{:S(2)}, u32[]{:S(2)}) collective-permute-start(bf16[128,640]{1,0:T(8,128)(2,1)} %get-tuple-element.114), channel_id=1, source_target_pairs={{0,1},{1,0},{2,3},{3,2},{4,5},{5,4},{6,7},{7,6},{8,9},{9,8},{10,11... | collective-permute-start | bytes 491528 | tf_op jit(solution)/shard_map/ppermute | solution.py:206
  97.6 11.7 %copy-start.4 = (bf16[256,640]{1,0:T(8,128)(2,1)}, bf16[256,640]{1,0:T(8,128)(2,1)S(1)}, u32[]{:S(2)}) copy-start(bf16[256,640]{1,0:T(8,128)(2,1)S(1)} %collective-permute-done.10.src_ref) | copy-start | bytes 983044
  97.6 4.2 %copy-start.1 = (bf16[2,256,640]{2,1,0:T(8,128)(2,1)}, bf16[2,256,640]{2,1,0:T(8,128)(2,1)S(1)}, u32[]{:S(2)}) copy-start(bf16[2,256,640]{2,1,0:T(8,128)(2,1)S(1)} %collective-permute-done.11.far_ref) | copy-start | bytes 1966084
  97.6 11.7 %collective-permute-start.14 = (bf16[2,256,640]{2,1,0:T(8,128)(2,1)}, bf16[2,256,640]{2,1,0:T(8,128)(2,1)}, u32[]{:S(2)}, u32[]{:S(2)}) collective-permute-start(bf16[2,256,640]{2,1,0:T(8,128)(2,1)} %get-tuple-element.130), channel_id=1, source_target_pairs={{0,2},{2,0},{4,6},{6,4},{8,10},{10,8},{12,14},{14,12},{16,18},{18,... | collective-permute-start | bytes 1966088 | tf_op jit(solution)/shard_map/ppermute | solution.py:197
  97.7 11.6 %collective-permute-start.13 = (bf16[128,640]{1,0:T(8,128)(2,1)}, bf16[128,640]{1,0:T(8,128)(2,1)}, u32[]{:S(2)}, u32[]{:S(2)}) collective-permute-start(bf16[128,640]{1,0:T(8,128)(2,1)} %get-tuple-element.129), channel_id=1, source_target_pairs={{0,1},{1,0},{2,3},{3,2},{4,5},{5,4},{6,7},{7,6},{8,9},{9,8},{10,11... | collective-permute-start | bytes 491528 | tf_op jit(solution)/shard_map/ppermute | solution.py:206
  101.8 16.1 %collective-permute-start.18 = (bf16[2,256,640]{2,1,0:T(8,128)(2,1)}, bf16[2,256,640]{2,1,0:T(8,128)(2,1)}, u32[]{:S(2)}, u32[]{:S(2)}) collective-permute-start(bf16[2,256,640]{2,1,0:T(8,128)(2,1)} %get-tuple-element.141), channel_id=1, source_target_pairs={{0,254},{2,4},{4,2},{6,8},{8,6},{10,12},{12,10},{14,16},{16,14},{1... | collective-permute-start | bytes 1966088 | tf_op jit(solution)/shard_map/ppermute | solution.py:202
  109.3 15.9 %collective-permute-start.16 = (bf16[2,256,640]{2,1,0:T(8,128)(2,1)}, bf16[2,256,640]{2,1,0:T(8,128)(2,1)S(1)}, u32[]{:S(2)}, u32[]{:S(2)}) collective-permute-start(bf16[2,256,640]{2,1,0:T(8,128)(2,1)} %get-tuple-element.137), channel_id=1, source_target_pairs={{0,2},{2,0},{4,6},{6,4},{8,10},{10,8},{12,14},{14,12},{16,18},{18,... | collective-permute-start | bytes 1966088 | tf_op jit(solution)/shard_map/ppermute | solution.py:197
  109.6 15.7 %collective-permute-start.17 = (bf16[2,256,640]{2,1,0:T(8,128)(2,1)}, bf16[2,256,640]{2,1,0:T(8,128)(2,1)}, u32[]{:S(2)}, u32[]{:S(2)}) collective-permute-start(bf16[2,256,640]{2,1,0:T(8,128)(2,1)} %get-tuple-element.138), channel_id=1, source_target_pairs={{0,254},{2,4},{4,2},{6,8},{8,6},{10,12},{12,10},{14,16},{16,14},{1... | collective-permute-start | bytes 1966088 | tf_op jit(solution)/shard_map/ppermute | solution.py:202
  117.5 33.8 %collective-permute-start.21 = (bf16[256,640]{1,0:T(8,128)(2,1)}, bf16[256,640]{1,0:T(8,128)(2,1)S(1)}, u32[]{:S(2)}, u32[]{:S(2)}) collective-permute-start(bf16[256,640]{1,0:T(8,128)(2,1)} %get-tuple-element.153), channel_id=1, source_target_pairs={{0,1},{1,0},{2,3},{3,2},{4,5},{5,4},{6,7},{7,6},{8,9},{9,8},{10,11... | collective-permute-start | bytes 983048 | tf_op jit(solution)/shard_map/ppermute | solution.py:206
  122.0 33.3 %collective-permute-start.20 = (bf16[256,640]{1,0:T(8,128)(2,1)}, bf16[256,640]{1,0:T(8,128)(2,1)}, u32[]{:S(2)}, u32[]{:S(2)}) collective-permute-start(bf16[256,640]{1,0:T(8,128)(2,1)} %get-tuple-element.152), channel_id=1, source_target_pairs={{0,1},{1,0},{2,3},{3,2},{4,5},{5,4},{6,7},{7,6},{8,9},{9,8},{10,11... | collective-permute-start | bytes 983048 | tf_op jit(solution)/shard_map/ppermute | solution.py:206
  125.3 0.9 copy-start.3
  130.3 28.2 %collective-permute-start.19 = (bf16[256,640]{1,0:T(8,128)(2,1)}, bf16[256,640]{1,0:T(8,128)(2,1)S(1)}, u32[]{:S(2)}, u32[]{:S(2)}) collective-permute-start(bf16[256,640]{1,0:T(8,128)(2,1)} %get-tuple-element.151), channel_id=1, source_target_pairs={{0,1},{1,0},{2,3},{3,2},{4,5},{5,4},{6,7},{7,6},{8,9},{9,8},{10,11... | collective-permute-start | bytes 983048 | tf_op jit(solution)/shard_map/ppermute | solution.py:206
  130.6 13.8 %collective-permute-start.15 = (bf16[128,640]{1,0:T(8,128)(2,1)}, bf16[128,640]{1,0:T(8,128)(2,1)S(1)}, u32[]{:S(2)}, u32[]{:S(2)}) collective-permute-start(bf16[128,640]{1,0:T(8,128)(2,1)} %get-tuple-element.131), channel_id=1, source_target_pairs={{0,1},{1,0},{2,3},{3,2},{4,5},{5,4},{6,7},{7,6},{8,9},{9,8},{10,11... | collective-permute-start | bytes 491528 | tf_op jit(solution)/shard_map/ppermute | solution.py:206
  144.5 0.7 copy-start.8
  151.3 0.7 copy-start.5
  158.5 0.7 copy-start.6

commit v2 on v1

--- a/solution.py
+++ b/solution.py
@@ -12,7 +12,7 @@
 H = 20
 TILE = 128
 ROWS = 256
-CHUNKS = (5, 5, 5, 5)
+CHUNKS = (7, 7, 6)
 SCALE = 1.0 / math.sqrt(HEAD)
 LOG2E = math.log2(math.e)
 DEAD = -1e30
@@ -118,76 +118,145 @@
     )(side, *args)
 
 
-def combine_kernel(side_ref, own_ref, fn_ref, fp_ref, *refs):
-    keep_k, keep_v, send_ref = refs[-3:]
-    f32 = jnp.float32
+def columns(side, h0, hc):
+    return pl.ds(pl.multiple_of(side * (H * HEAD) + h0 * HEAD, HEAD), hc * HEAD)
+
+
+def run_all(copies):
+    for copy in copies:
+        copy.start()
+    for copy in copies:
+        copy.wait()
+
+
+def combine_kernel(h0, hc, side_ref, own_ref, near_ref, far_ref, *refs):
+    keep_k, keep_v, send_ref, parts, kept, sent, in_sems, out_sems = refs[-8:]
+    f32, side = jnp.float32, side_ref[0]
+    fetches = [
+        [
+            pltpu.make_async_copy(src.at[j], parts.at[j, n], in_sems.at[j, n])
+            for n, src in enumerate((own_ref, near_ref, far_ref))
+        ]
+        for j in range(2)
+    ]
+    for copy in fetches[0] + fetches[1]:
+        copy.start()
+    leaving = []
     for j, keep in enumerate((keep_k, keep_v)):
-        total = own_ref[j].astype(f32) + fn_ref[j].astype(f32) + fp_ref[j].astype(f32)
-        split_rows(side_ref[0], total.astype(BF16), keep, send_ref.at[pl.ds(j * TILE, TILE)])
+        for copy in fetches[j]:
+            copy.wait()
+        total = parts[j, 0].astype(f32) + parts[j, 1].astype(f32) + parts[j, 2].astype(f32)
+        split_rows(side, total.astype(BF16), kept.at[j], sent.at[j])
+        leaving += [
+            pltpu.make_async_copy(
+                sent.at[j], send_ref.at[pl.ds(j * TILE, TILE)], out_sems.at[j, 0]
+            ),
+            pltpu.make_async_copy(
+                kept.at[j], keep.at[:, columns(side, h0, hc)], out_sems.at[j, 1]
+            ),
+        ]
+        for copy in leaving[-2:]:
+            copy.start()
+    for copy in leaving:
+        copy.wait()
 
 
 def combine(side, own, from_near, from_far, outs, h0, hc):
-    pair = pl.BlockSpec((2, ROWS, HEAD), lambda i, s: (0, 0, i))
-    specs, args, alias = [pair] * 3, [own, from_near, from_far], {}
+    width = hc * HEAD
+    anywhere = pl.BlockSpec(memory_space=pl.ANY)
+    args, alias = [own, from_near, from_far], {}
     if outs is not None:
-        specs += [pl.BlockSpec(memory_space=pl.ANY)] * 2
         args += list(outs)
         alias = {4: 0, 5: 1}
-    keep = pl.BlockSpec((TILE, HEAD), lambda i, s: (0, s[0] * H + h0 + i))
     return pl.pallas_call(
-        combine_kernel,
+        functools.partial(combine_kernel, h0, hc),
         grid_spec=pltpu.PrefetchScalarGridSpec(
             num_scalar_prefetch=1,
-            grid=(hc,),
-            in_specs=specs,
-            out_specs=[keep, keep, pl.BlockSpec((2 * TILE, HEAD), lambda i, s: (0, i))],
+            grid=(1,),
+            in_specs=[anywhere] * len(args),
+            out_specs=[anywhere] * 3,
+            scratch_shapes=[
+                pltpu.VMEM((2, 3, ROWS, width), BF16),
+                pltpu.VMEM((2, TILE, width), BF16),
+                pltpu.VMEM((2, TILE, width), BF16),
+                pltpu.SemaphoreType.DMA((2, 3)),
+                pltpu.SemaphoreType.DMA((2, 2)),
+            ],
         ),
         out_shape=[pltpu.HBM((TILE, 2 * H * HEAD), BF16)] * 2
-        + [pltpu.HBM((2 * TILE, hc * HEAD), BF16)],
+        + [pltpu.HBM((2 * TILE, width), BF16)],
         input_output_aliases=alias,
         compiler_params=PARAMS,
         name="combine",
     )(side, *args)
 
 
-def place_kernel(side_ref, src_ref, *refs):
-    outs = refs[len(refs) // 2 :]
-    for j, out in enumerate(outs):
-        out[...] = src_ref[j * TILE : (j + 1) * TILE]
-
-
-def place(side, part, outs, h0, hc):
-    n = len(outs)
-    dest = pl.BlockSpec((TILE, HEAD), lambda i, s: (0, (1 - s[0]) * H + h0 + i))
+def place_kernel(moves, side_ref, *refs):
+    sems = refs[-1]
+    outs = refs[len(refs) - 1 - max(o for _, _, o, _, _ in moves) - 1 : -1]
+    copies = [
+        pltpu.make_async_copy(
+            refs[part].at[pl.ds(row, TILE)],
+            outs[o].at[:, columns(1 - side_ref[0], h0, hc)],
+            sems.at[n],
+        )
+        for n, (part, row, o, h0, hc) in enumerate(moves)
+    ]
+    run_all(copies)
+
+
+def place(side, parts, outs, spans):
+    moves = [
+        (p, o * TILE, o, h0, hc) for p, (h0, hc) in enumerate(spans) for o in range(len(outs))
+    ]
     return pl.pallas_call(
-        place_kernel,
+        functools.partial(place_kernel, moves),
         grid_spec=pltpu.PrefetchScalarGridSpec(
             num_scalar_prefetch=1,
-            grid=(hc,),
-            in_specs=[pl.BlockSpec((n * TILE, HEAD), lambda i, s: (0, i))]
-            + [pl.BlockSpec(memory_space=pl.ANY)] * n,
-            out_specs=[dest] * n,
+            grid=(1,),
+            in_specs=[pl.BlockSpec(part.shape, lambda i, s: (0, 0)) for part in parts]
+            + [pl.BlockSpec(memory_space=pl.ANY)] * len(outs),
+            out_specs=[pl.BlockSpec(memory_space=pl.ANY)] * len(outs),
+            scratch_shapes=[pltpu.SemaphoreType.DMA((len(moves),))],
         ),
-        out_shape=[pltpu.HBM((TILE, 2 * H * HEAD), BF16)] * n,
-        input_output_aliases={2 + j: j for j in range(n)},
+        out_shape=[pltpu.HBM((TILE, 2 * H * HEAD), BF16)] * len(outs),
+        input_output_aliases={1 + len(parts) + j: j for j in range(len(outs))},
         compiler_params=PARAMS,
         name="place",
-    )(side, part, *outs)
-
-
-def pack_kernel(k_ref, v_ref, out_ref):
-    out_ref[0] = k_ref[...]
-    out_ref[1] = v_ref[...]
-
-
-def pack(k, v, h0, hc):
-    block = pl.BlockSpec((ROWS, HEAD), lambda i: (0, h0 + i))
+    )(side, *parts, *outs)
+
+
+def pack_kernel(spans, k_ref, v_ref, *refs):
+    count = len(spans)
+    outs, stages, sems = refs[:count], refs[count : 2 * count], refs[-1]
+    moves = []
+    for n, (h0, hc) in enumerate(spans):
+        for j, src in enumerate((k_ref, v_ref)):
+            cols = pl.ds(h0 * HEAD, hc * HEAD)
+            moves.append(
+                (
+                    pltpu.make_async_copy(src.at[:, cols], stages[n].at[j], sems.at[n, j, 0]),
+                    pltpu.make_async_copy(stages[n].at[j], outs[n].at[j], sems.at[n, j, 1]),
+                )
+            )
+    for fetch, _ in moves:
+        fetch.start()
+    for fetch, store in moves:
+        fetch.wait()
+        store.start()
+    for _, store in moves:
+        store.wait()
+
+
+def pack(k, v, spans):
     return pl.pallas_call(
-        pack_kernel,
-        grid=(hc,),
-        in_specs=[block] * 2,
-        out_specs=pl.BlockSpec((2, ROWS, HEAD), lambda i: (0, 0, i)),
-        out_shape=pltpu.HBM((2, ROWS, hc * HEAD), BF16),
+        functools.partial(pack_kernel, spans),
+        grid=(1,),
+        in_specs=[pl.BlockSpec(memory_space=pl.ANY)] * 2,
+        out_specs=[pl.BlockSpec(memory_space=pl.ANY)] * len(spans),
+        out_shape=[pltpu.HBM((2, ROWS, hc * HEAD), BF16) for _, hc in spans],
+        scratch_shapes=[pltpu.VMEM((2, ROWS, hc * HEAD), BF16) for _, hc in spans]
+        + [pltpu.SemaphoreType.DMA((len(spans), 2, 2))],
         compiler_params=PARAMS,
         name="pack",
     )(k, v)
@@ -224,11 +293,9 @@
     spans = split_heads(CHUNKS)
     count = len(spans)
     near_k, near_v = near_swap(key_states), near_swap(value_states)
-    packs, source = [pack(key_states, value_states, *spans[0])], key_states
-    source, near_k = lax.optimization_barrier((source, near_k))
-    for h0, hc in spans[1:]:
-        packs.append(pack(source, value_states, h0, hc))
-        source, packs[-1] = lax.optimization_barrier((source, packs[-1]))
+    packs = list(pack(key_states, value_states, spans[:1]))
+    later_keys, near_k = lax.optimization_barrier((key_states, near_k))
+    packs += pack(later_keys, value_states, spans[1:])
     fars = [far_swap(packs[0]), far_swap(packs[1])]
     bias, *_ = lax.optimization_barrier((bias, *packs))
 
@@ -276,10 +343,9 @@
     from_near.append(near_swap(nears[-1]))
     for n in range(max(count - 2, 0), count):
         finish(n, owns[n])
-    for (h0, hc), part in zip(spans, q_parts):
-        (out_q,) = place(side, part, [out_q], h0, hc)
-    for (h0, hc), part in zip(spans, kv_parts):
-        out_kv = place(side, part, out_kv, h0, hc)
+    (out_q,) = place(side, q_parts, [out_q], spans)
+    out_kv = place(side, kv_parts[:-1], out_kv, spans[:-1])
+    out_kv = place(side, kv_parts[-1:], out_kv, spans[-1:])
     return (out_q, *out_kv)
 
 

time: 166 us -> 135 us (0.81)
  the two profiles are of different devices: /device:TPU:230 before, /device:TPU:225 now
where the time goes in v2:
time: 135 us; the launch traced here: 133 us
  waiting for transfers between devices  54.3 us (40%)
  Pallas kernels  46.9 us (35%)
  starting transfers between devices  29.4 us (22%)
    ppermute x6, waiting for transfers between devices, swap(): return lax.ppermute(x, 'section', [(0, 1), (1, 0)])  36.3 us
    pallas_call x3, Pallas kernels, attn_chunk(): pl.pallas_call(attn_kernel, grid_spec=pltpu.PrefetchScalarGridSpec(num_sc...  28.3 us
    ppermute x6, waiting for transfers between devices, far_swap(): lax.ppermute(x, 'ctx', [(i, (i + 2 * (i % 2) - 1) % count) for i in range...  18 us
    ppermute x6, starting transfers between devices, swap(): return lax.ppermute(x, 'section', [(0, 1), (1, 0)])  13 us
    ppermute x5, starting transfers between devices, near_swap(): lax.ppermute(x, 'ctx', [(i, i ^ 1) for i in range(lax.axis_size('ctx'))])  12.1 us
    pallas_call x3, Pallas kernels, combine(): pl.pallas_call(functools.partial(combine_kernel, h0, hc), grid_spec=pltpu...  8.55 us
    pallas_call x3, Pallas kernels, place(): pl.pallas_call(functools.partial(place_kernel, moves), grid_spec=pltpu.Pr...  5.86 us
    ppermute x6, starting transfers between devices, far_swap(): lax.ppermute(x, 'ctx', [(i, (i + 2 * (i % 2) - 1) % count) for i in range...  4.3 us
  transfers between devices with their start and end apart: 17, of which 5 were waited for; matrix products, arithmetic and copies ran while one was open for 1% of the time, Pallas kernels for 34%

profile of v2, /device:TPU:225, one launch (start us, length us, event | category | flops | bytes accessed | tf_op | source)
XLA Modules:
  0.0 133.5 jit_solution(14816773076615916556)
XLA Ops:
  0.6 0.8 collective-permute-start
  1.4 0.1 collective-permute-start.1
  1.5 2.0 %pack.2 = bf16[2,256,896]{2,1,0:T(8,128)(2,1)} custom-call(bf16[256,2560]{1,0:T(8,128)(2,1)} %k_ref.8, bf16[256,2560]{1,0:T(8,128)(2,1)} %v_ref.9), custom_call_target="tpu_custom_call" | custom-call | tf_op jit(solution)/shard_map/pack/pallas_call | solution.py:252
  3.5 1.7 %collective-permute-start.2 = (bf16[2,256,896]{2,1,0:T(8,128)(2,1)}, bf16[2,256,896]{2,1,0:T(8,128)(2,1)}, u32[]{:S(2)}, u32[]{:S(2)}) collective-permute-start(bf16[2,256,896]{2,1,0:T(8,128)(2,1)} %pack.2), channel_id=1, source_target_pairs={{0,254},{2,4},{4,2},{6,8},{8,6},{10,12},{12,10},{14,16},{16,14},{1... | collective-permute-start | bytes 2752520 | tf_op jit(solution)/shard_map/ppermute | solution.py:271
  5.2 2.3 %pack.3 = (bf16[2,256,896]{2,1,0:T(8,128)(2,1)}, bf16[2,256,768]{2,1,0:T(8,128)(2,1)}) custom-call(bf16[256,2560]{1,0:T(8,128)(2,1)} %k_ref.8, bf16[256,2560]{1,0:T(8,128)(2,1)} %v_ref.9), custom_call_target="tpu_custom_call" | custom-call | tf_op jit(solution)/shard_map/pack/pallas_call | solution.py:252
  7.5 0.9 collective-permute-start.3
  8.7 0.7 maximum_maximum_fusion.bias_ref
  9.3 7.7 %collective-permute-done.2.far_ref = bf16[2,256,896]{2,1,0:T(8,128)(2,1)} collective-permute-done((bf16[2,256,896]{2,1,0:T(8,128)(2,1)}, bf16[2,256,896]{2,1,0:T(8,128)(2,1)}, u32[]{:S(2)}, u32[]{:S(2)}) %collective-permute-start.2) | collective-permute-done | bytes 917536 | tf_op jit(solution)/shard_map/ppermute | solution.py:271
  17.0 9.8 %attn.3 = (bf16[128,5120]{1,0:T(8,128)(2,1)}, bf16[128,896]{1,0:T(8,128)(2,1)}, bf16[2,256,896]{2,1,0:T(8,128)(2,1)}, bf16[2,256,896]{2,1,0:T(8,128)(2,1)}, bf16[2,256,896]{2,1,0:T(8,128)(2,1)}) custom-call(s32[1]{0:T(128)} %bitcast.side_ref, bf16[256,2560]{1,0:T(8,128)(2,1)} %q_ref.5, bf16[256,2560]{1,0:T(8,128)(2,1)} %do_ref.5, bf16[256,2560]{1,0:T(8,128)(2,1)} %k_ref.8, ...), custom_call_target="tpu_custom_call" | custom-call | tf_op jit(solution)/shard_map/attn/pallas_call | solution.py:96
  26.8 2.3 %collective-permute-start.5 = (bf16[2,256,896]{2,1,0:T(8,128)(2,1)}, bf16[2,256,896]{2,1,0:T(8,128)(2,1)}, u32[]{:S(2)}, u32[]{:S(2)}) collective-permute-start(bf16[2,256,896]{2,1,0:T(8,128)(2,1)} %get-tuple-element.75), channel_id=1, source_target_pairs={{0,2},{2,0},{4,6},{6,4},{8,10},{10,8},{12,14},{14,12},{16,18},{18,... | collective-permute-start | bytes 2752520 | tf_op jit(solution)/shard_map/ppermute | solution.py:266
  29.1 1.7 %collective-permute-start.6 = (bf16[2,256,768]{2,1,0:T(8,128)(2,1)}, bf16[2,256,768]{2,1,0:T(8,128)(2,1)}, u32[]{:S(2)}, u32[]{:S(2)}) collective-permute-start(bf16[2,256,768]{2,1,0:T(8,128)(2,1)} %get-tuple-element.78), channel_id=1, source_target_pairs={{0,254},{2,4},{4,2},{6,8},{8,6},{10,12},{12,10},{14,16},{16,14},{1... | collective-permute-start | bytes 2359304 | tf_op jit(solution)/shard_map/ppermute | solution.py:271
  30.9 2.8 %collective-permute-start.4 = (bf16[128,896]{1,0:T(8,128)(2,1)}, bf16[128,896]{1,0:T(8,128)(2,1)}, u32[]{:S(2)}, u32[]{:S(2)}) collective-permute-start(bf16[128,896]{1,0:T(8,128)(2,1)} %get-tuple-element.74), channel_id=1, source_target_pairs={{0,1},{1,0},{2,3},{3,2},{4,5},{5,4},{6,7},{7,6},{8,9},{9,8},{10,11... | collective-permute-start | bytes 688136 | tf_op jit(solution)/shard_map/ppermute | solution.py:275
  33.6 9.8 %attn.4 = (bf16[128,5120]{1,0:T(8,128)(2,1)}, bf16[128,896]{1,0:T(8,128)(2,1)}, bf16[2,256,896]{2,1,0:T(8,128)(2,1)}, bf16[2,256,896]{2,1,0:T(8,128)(2,1)}, bf16[2,256,896]{2,1,0:T(8,128)(2,1)}) custom-call(s32[1]{0:T(128)} %bitcast.side_ref, bf16[256,2560]{1,0:T(8,128)(2,1)} %q_ref.5, bf16[256,2560]{1,0:T(8,128)(2,1)} %do_ref.5, ...), custom_call_target="tpu_custom_call", output_to_operand_aliasing={{0}: (9, {})} | custom-call | tf_op jit(solution)/shard_map/attn/pallas_call | solution.py:96
  43.5 7.5 %collective-permute-done.6.far_ref = bf16[2,256,768]{2,1,0:T(8,128)(2,1)} collective-permute-done((bf16[2,256,768]{2,1,0:T(8,128)(2,1)}, bf16[2,256,768]{2,1,0:T(8,128)(2,1)}, u32[]{:S(2)}, u32[]{:S(2)}) %collective-permute-start.6) | collective-permute-done | bytes 786464 | tf_op jit(solution)/shard_map/ppermute | solution.py:271
  51.0 7.3 %collective-permute-start.9 = (bf16[2,256,896]{2,1,0:T(8,128)(2,1)}, bf16[2,256,896]{2,1,0:T(8,128)(2,1)S(1)}, u32[]{:S(2)}, u32[]{:S(2)}) collective-permute-start(bf16[2,256,896]{2,1,0:T(8,128)(2,1)} %get-tuple-element.87), channel_id=1, source_target_pairs={{0,2},{2,0},{4,6},{6,4},{8,10},{10,8},{12,14},{14,12},{16,18},{18,... | collective-permute-start | bytes 2752520 | tf_op jit(solution)/shard_map/ppermute | solution.py:266
  58.3 3.7 %collective-permute-start.8 = (bf16[128,896]{1,0:T(8,128)(2,1)}, bf16[128,896]{1,0:T(8,128)(2,1)}, u32[]{:S(2)}, u32[]{:S(2)}) collective-permute-start(bf16[128,896]{1,0:T(8,128)(2,1)} %get-tuple-element.86), channel_id=1, source_target_pairs={{0,1},{1,0},{2,3},{3,2},{4,5},{5,4},{6,7},{7,6},{8,9},{9,8},{10,11... | collective-permute-start | bytes 688136 | tf_op jit(solution)/shard_map/ppermute | solution.py:275
  62.0 8.6 %attn.5 = (bf16[128,5120]{1,0:T(8,128)(2,1)}, bf16[128,768]{1,0:T(8,128)(2,1)}, bf16[2,256,768]{2,1,0:T(8,128)(2,1)}, bf16[2,256,768]{2,1,0:T(8,128)(2,1)}, bf16[2,256,768]{2,1,0:T(8,128)(2,1)}) custom-call(s32[1]{0:T(128)} %bitcast.side_ref, bf16[256,2560]{1,0:T(8,128)(2,1)} %q_ref.5, bf16[256,2560]{1,0:T(8,128)(2,1)} %do_ref.5, ...), custom_call_target="tpu_custom_call", output_to_operand_aliasing={{0}: (9, {})} | custom-call | tf_op jit(solution)/shard_map/attn/pallas_call | solution.py:96
  70.7 14.9 %collective-permute-done.8.refs_1_ = bf16[128,896]{1,0:T(8,128)(2,1)} collective-permute-done((bf16[128,896]{1,0:T(8,128)(2,1)}, bf16[128,896]{1,0:T(8,128)(2,1)}, u32[]{:S(2)}, u32[]{:S(2)}) %collective-permute-start.8) | collective-permute-done | bytes 229408 | tf_op jit(solution)/shard_map/ppermute | solution.py:275
  85.6 1.6 %collective-permute-start.11 = (bf16[2,256,768]{2,1,0:T(8,128)(2,1)}, bf16[2,256,768]{2,1,0:T(8,128)(2,1)}, u32[]{:S(2)}, u32[]{:S(2)}) collective-permute-start(bf16[2,256,768]{2,1,0:T(8,128)(2,1)} %get-tuple-element.92), channel_id=1, source_target_pairs={{0,2},{2,0},{4,6},{6,4},{8,10},{10,8},{12,14},{14,12},{16,18},{18,... | collective-permute-start | bytes 2359304 | tf_op jit(solution)/shard_map/ppermute | solution.py:266
  87.2 2.9 %combine.3 = (bf16[128,5120]{1,0:T(8,128)(2,1)}, bf16[128,5120]{1,0:T(8,128)(2,1)}, bf16[256,896]{1,0:T(8,128)(2,1)}) custom-call(s32[1]{0:T(128)} %bitcast.side_ref, bf16[2,256,896]{2,1,0:T(8,128)(2,1)} %get-tuple-element.97.own_ref, bf16[2,256,896]{2,1,0:T(8,128)(2,1)} %collective-permute-done.5.near_ref, bf16[2,256,896]{2,1,0:T(8,128)(2,1)} %collective-permute-done.7.far_ref), custom_call_target="tpu_custom_call" | custom-call | tf_op jit(solution)/shard_map/combine/pallas_call | solution.py:171
  90.1 3.3 %collective-permute-start.15 = (bf16[256,896]{1,0:T(8,128)(2,1)}, bf16[256,896]{1,0:T(8,128)(2,1)S(1)}, u32[]{:S(2)}, u32[]{:S(2)}) collective-permute-start(bf16[256,896]{1,0:T(8,128)(2,1)} %get-tuple-element.105), channel_id=1, source_target_pairs={{0,1},{1,0},{2,3},{3,2},{4,5},{5,4},{6,7},{7,6},{8,9},{9,8},{10,11... | collective-permute-start | bytes 1376264 | tf_op jit(solution)/shard_map/ppermute | solution.py:275
  93.4 2.9 %combine.4 = (bf16[128,5120]{1,0:T(8,128)(2,1)}, bf16[128,5120]{1,0:T(8,128)(2,1)}, bf16[256,896]{1,0:T(8,128)(2,1)}) custom-call(s32[1]{0:T(128)} %bitcast.side_ref, bf16[2,256,896]{2,1,0:T(8,128)(2,1)} %get-tuple-element.94.own_ref, bf16[2,256,896]{2,1,0:T(8,128)(2,1)} %copy-done.1, ...), custom_call_target="tpu_custom_call", output_to_operand_aliasing={{0}: (4, {}), {1}: (5, {})} | custom-call | tf_op jit(solution)/shard_map/combine/pallas_call | solution.py:171
  96.3 0.1 collective-permute-start.16
  96.4 2.8 %collective-permute-done.12.far_ref = bf16[2,256,768]{2,1,0:T(8,128)(2,1)} collective-permute-done((bf16[2,256,768]{2,1,0:T(8,128)(2,1)}, bf16[2,256,768]{2,1,0:T(8,128)(2,1)}, u32[]{:S(2)}, u32[]{:S(2)}) %collective-permute-start.12) | collective-permute-done | bytes 786464 | tf_op jit(solution)/shard_map/ppermute | solution.py:271
  99.2 2.7 %combine.5 = (bf16[128,5120]{1,0:T(8,128)(2,1)}, bf16[128,5120]{1,0:T(8,128)(2,1)}, bf16[256,768]{1,0:T(8,128)(2,1)}) custom-call(s32[1]{0:T(128)} %bitcast.side_ref, bf16[2,256,768]{2,1,0:T(8,128)(2,1)} %get-tuple-element.91.own_ref, bf16[2,256,768]{2,1,0:T(8,128)(2,1)} %collective-permute-done.11.near_ref, ...), custom_call_target="tpu_custom_call", output_to_operand_aliasing={{0}: (4, {}), {1}: (5, {})} | custom-call | tf_op jit(solution)/shard_map/combine/pallas_call | solution.py:171
  101.9 3.1 %collective-permute-start.14 = (bf16[256,768]{1,0:T(8,128)(2,1)}, bf16[256,768]{1,0:T(8,128)(2,1)}, u32[]{:S(2)}, u32[]{:S(2)}) collective-permute-start(bf16[256,768]{1,0:T(8,128)(2,1)} %get-tuple-element.104), channel_id=1, source_target_pairs={{0,1},{1,0},{2,3},{3,2},{4,5},{5,4},{6,7},{7,6},{8,9},{9,8},{10,11... | collective-permute-start | bytes 1179656 | tf_op jit(solution)/shard_map/ppermute | solution.py:275
  105.1 21.4 %collective-permute-done.10.refs_2_ = bf16[128,768]{1,0:T(8,128)(2,1)} collective-permute-done((bf16[128,768]{1,0:T(8,128)(2,1)}, bf16[128,768]{1,0:T(8,128)(2,1)}, u32[]{:S(2)}, u32[]{:S(2)}) %collective-permute-start.10) | collective-permute-done | bytes 196640 | tf_op jit(solution)/shard_map/ppermute | solution.py:275
  126.5 2.0 %place.3 = bf16[128,5120]{1,0:T(8,128)(2,1)} custom-call(s32[1]{0:T(128)} %bitcast.side_ref, bf16[128,896]{1,0:T(8,128)(2,1)} %collective-permute-done.4.refs_0_, bf16[128,896]{1,0:T(8,128)(2,1)} %collective-permute-done.8.refs_1_, bf16[128,768]{1,0:T(8,128)(2,1)} %collective-permute-done.10.refs_2_, ...), custom_call_target="tpu_custom_call", output_to_operand_aliasing={{}: (4, {})} | custom-call | tf_op jit(solution)/shard_map/place/pallas_call | solution.py:212
  128.5 0.7 copy-done.2
  129.3 0.2 copy-done.3
  129.4 2.1 %place.4 = (bf16[128,5120]{1,0:T(8,128)(2,1)}, bf16[128,5120]{1,0:T(8,128)(2,1)}) custom-call(s32[1]{0:T(128)} %bitcast.side_ref, bf16[256,896]{1,0:T(8,128)(2,1)} %copy-done.2, bf16[256,896]{1,0:T(8,128)(2,1)} %copy-done.3, bf16[128,5120]{1,0:T(8,128)(2,1)} %get-tuple-element.107.refs_2_, ...), custom_call_target="tpu_custom_call", output_to_operand_aliasing={{0}: (3, {}), {1}: (4, {})} | custom-call | tf_op jit(solution)/shard_map/place/pallas_call | solution.py:212
  131.6 1.8 %place.5 = (bf16[128,5120]{1,0:T(8,128)(2,1)}, bf16[128,5120]{1,0:T(8,128)(2,1)}) custom-call(s32[1]{0:T(128)} %bitcast.side_ref, bf16[256,768]{1,0:T(8,128)(2,1)} %collective-permute-done.14.refs_0_, bf16[128,5120]{1,0:T(8,128)(2,1)} %get-tuple-element.109.refs_1_, ...), custom_call_target="tpu_custom_call", output_to_operand_aliasing={{0}: (2, {}), {1}: (3, {})} | custom-call | tf_op jit(solution)/shard_map/place/pallas_call | solution.py:212
  (33 shorter events, 0.5 us)
Async XLA Ops:
  0.6 4.5 %collective-permute-start = (bf16[256,2560]{1,0:T(8,128)(2,1)}, bf16[256,2560]{1,0:T(8,128)(2,1)}, u32[]{:S(2)}, u32[]{:S(2)}) collective-permute-start(bf16[256,2560]{1,0:T(8,128)(2,1)} %k_ref.8), channel_id=1, source_target_pairs={{0,2},{2,0},{4,6},{6,4},{8,10},{10,8},{12,14},{14,12},{16,18},{18,... | collective-permute-start | bytes 3932168 | tf_op jit(solution)/shard_map/ppermute | solution.py:266
  1.4 15.6 %collective-permute-start.1 = (bf16[256,2560]{1,0:T(8,128)(2,1)}, bf16[256,2560]{1,0:T(8,128)(2,1)}, u32[]{:S(2)}, u32[]{:S(2)}) collective-permute-start(bf16[256,2560]{1,0:T(8,128)(2,1)} %v_ref.9), channel_id=1, source_target_pairs={{0,2},{2,0},{4,6},{6,4},{8,10},{10,8},{12,14},{14,12},{16,18},{18,... | collective-permute-start | bytes 3932168 | tf_op jit(solution)/shard_map/ppermute | solution.py:266
  3.5 13.5 %collective-permute-start.2 = (bf16[2,256,896]{2,1,0:T(8,128)(2,1)}, bf16[2,256,896]{2,1,0:T(8,128)(2,1)}, u32[]{:S(2)}, u32[]{:S(2)}) collective-permute-start(bf16[2,256,896]{2,1,0:T(8,128)(2,1)} %pack.2), channel_id=1, source_target_pairs={{0,254},{2,4},{4,2},{6,8},{8,6},{10,12},{12,10},{14,16},{16,14},{1... | collective-permute-start | bytes 2752520 | tf_op jit(solution)/shard_map/ppermute | solution.py:271
  5.1 3.2 %copy-start.4 = (s32[256,6]{0,1:T(8,128)S(1)}, s32[256,6]{0,1:T(8,128)}, u32[]{:S(2)}) copy-start(s32[256,6]{0,1:T(8,128)} %param.9) | copy-start | bytes 18436
  7.5 19.3 %collective-permute-start.3 = (bf16[2,256,896]{2,1,0:T(8,128)(2,1)}, bf16[2,256,896]{2,1,0:T(8,128)(2,1)S(1)}, u32[]{:S(2)}, u32[]{:S(2)}) collective-permute-start(bf16[2,256,896]{2,1,0:T(8,128)(2,1)} %get-tuple-element.60), channel_id=1, source_target_pairs={{0,254},{2,4},{4,2},{6,8},{8,6},{10,12},{12,10},{14,16},{16,14},{1... | collective-permute-start | bytes 2752520 | tf_op jit(solution)/shard_map/ppermute | solution.py:271
  26.8 6.8 %copy-start = (bf16[2,256,896]{2,1,0:T(8,128)(2,1)}, bf16[2,256,896]{2,1,0:T(8,128)(2,1)S(1)}, u32[]{:S(2)}) copy-start(bf16[2,256,896]{2,1,0:T(8,128)(2,1)S(1)} %collective-permute-done.3.far_ref) | copy-start | bytes 2752516
  26.8 16.7 %collective-permute-start.5 = (bf16[2,256,896]{2,1,0:T(8,128)(2,1)}, bf16[2,256,896]{2,1,0:T(8,128)(2,1)}, u32[]{:S(2)}, u32[]{:S(2)}) collective-permute-start(bf16[2,256,896]{2,1,0:T(8,128)(2,1)} %get-tuple-element.75), channel_id=1, source_target_pairs={{0,2},{2,0},{4,6},{6,4},{8,10},{10,8},{12,14},{14,12},{16,18},{18,... | collective-permute-start | bytes 2752520 | tf_op jit(solution)/shard_map/ppermute | solution.py:266
  29.1 21.9 %collective-permute-start.7 = (bf16[2,256,896]{2,1,0:T(8,128)(2,1)}, bf16[2,256,896]{2,1,0:T(8,128)(2,1)}, u32[]{:S(2)}, u32[]{:S(2)}) collective-permute-start(bf16[2,256,896]{2,1,0:T(8,128)(2,1)} %get-tuple-element.79), channel_id=1, source_target_pairs={{0,254},{2,4},{4,2},{6,8},{8,6},{10,12},{12,10},{14,16},{16,14},{1... | collective-permute-start | bytes 2752520 | tf_op jit(solution)/shard_map/ppermute | solution.py:271
  29.1 21.9 %collective-permute-start.6 = (bf16[2,256,768]{2,1,0:T(8,128)(2,1)}, bf16[2,256,768]{2,1,0:T(8,128)(2,1)}, u32[]{:S(2)}, u32[]{:S(2)}) collective-permute-start(bf16[2,256,768]{2,1,0:T(8,128)(2,1)} %get-tuple-element.78), channel_id=1, source_target_pairs={{0,254},{2,4},{4,2},{6,8},{8,6},{10,12},{12,10},{14,16},{16,14},{1... | collective-permute-start | bytes 2359304 | tf_op jit(solution)/shard_map/ppermute | solution.py:271
  30.9 12.6 %collective-permute-start.4 = (bf16[128,896]{1,0:T(8,128)(2,1)}, bf16[128,896]{1,0:T(8,128)(2,1)}, u32[]{:S(2)}, u32[]{:S(2)}) collective-permute-start(bf16[128,896]{1,0:T(8,128)(2,1)} %get-tuple-element.74), channel_id=1, source_target_pairs={{0,1},{1,0},{2,3},{3,2},{4,5},{5,4},{6,7},{7,6},{8,9},{9,8},{10,11... | collective-permute-start | bytes 688136 | tf_op jit(solution)/shard_map/ppermute | solution.py:275
  51.0 34.6 %collective-permute-start.9 = (bf16[2,256,896]{2,1,0:T(8,128)(2,1)}, bf16[2,256,896]{2,1,0:T(8,128)(2,1)S(1)}, u32[]{:S(2)}, u32[]{:S(2)}) collective-permute-start(bf16[2,256,896]{2,1,0:T(8,128)(2,1)} %get-tuple-element.87), channel_id=1, source_target_pairs={{0,2},{2,0},{4,6},{6,4},{8,10},{10,8},{12,14},{14,12},{16,18},{18,... | collective-permute-start | bytes 2752520 | tf_op jit(solution)/shard_map/ppermute | solution.py:266
  58.3 27.2 %collective-permute-start.8 = (bf16[128,896]{1,0:T(8,128)(2,1)}, bf16[128,896]{1,0:T(8,128)(2,1)}, u32[]{:S(2)}, u32[]{:S(2)}) collective-permute-start(bf16[128,896]{1,0:T(8,128)(2,1)} %get-tuple-element.86), channel_id=1, source_target_pairs={{0,1},{1,0},{2,3},{3,2},{4,5},{5,4},{6,7},{7,6},{8,9},{9,8},{10,11... | collective-permute-start | bytes 688136 | tf_op jit(solution)/shard_map/ppermute | solution.py:275
  62.0 31.3 %collective-permute-start.13 = (bf16[2,256,896]{2,1,0:T(8,128)(2,1)}, bf16[2,256,896]{2,1,0:T(8,128)(2,1)}, u32[]{:S(2)}, u32[]{:S(2)}) collective-permute-start(bf16[2,256,896]{2,1,0:T(8,128)(2,1)} %get-tuple-element.96), channel_id=1, source_target_pairs={{0,254},{2,4},{4,2},{6,8},{8,6},{10,12},{12,10},{14,16},{16,14},{1... | collective-permute-start | bytes 2752520 | tf_op jit(solution)/shard_map/ppermute | solution.py:271
  85.6 4.5 %copy-start.1 = (bf16[2,256,896]{2,1,0:T(8,128)(2,1)}, bf16[2,256,896]{2,1,0:T(8,128)(2,1)S(1)}, u32[]{:S(2)}) copy-start(bf16[2,256,896]{2,1,0:T(8,128)(2,1)S(1)} %collective-permute-done.9.near_ref) | copy-start | bytes 2752516
  85.6 10.8 %collective-permute-start.11 = (bf16[2,256,768]{2,1,0:T(8,128)(2,1)}, bf16[2,256,768]{2,1,0:T(8,128)(2,1)}, u32[]{:S(2)}, u32[]{:S(2)}) collective-permute-start(bf16[2,256,768]{2,1,0:T(8,128)(2,1)} %get-tuple-element.92), channel_id=1, source_target_pairs={{0,2},{2,0},{4,6},{6,4},{8,10},{10,8},{12,14},{14,12},{16,18},{18,... | collective-permute-start | bytes 2359304 | tf_op jit(solution)/shard_map/ppermute | solution.py:266
  87.2 12.0 %collective-permute-start.12 = (bf16[2,256,768]{2,1,0:T(8,128)(2,1)}, bf16[2,256,768]{2,1,0:T(8,128)(2,1)}, u32[]{:S(2)}, u32[]{:S(2)}) collective-permute-start(bf16[2,256,768]{2,1,0:T(8,128)(2,1)} %get-tuple-element.93), channel_id=1, source_target_pairs={{0,254},{2,4},{4,2},{6,8},{8,6},{10,12},{12,10},{14,16},{16,14},{1... | collective-permute-start | bytes 2359304 | tf_op jit(solution)/shard_map/ppermute | solution.py:271
  90.1 38.4 %collective-permute-start.15 = (bf16[256,896]{1,0:T(8,128)(2,1)}, bf16[256,896]{1,0:T(8,128)(2,1)S(1)}, u32[]{:S(2)}, u32[]{:S(2)}) collective-permute-start(bf16[256,896]{1,0:T(8,128)(2,1)} %get-tuple-element.105), channel_id=1, source_target_pairs={{0,1},{1,0},{2,3},{3,2},{4,5},{5,4},{6,7},{7,6},{8,9},{9,8},{10,11... | collective-permute-start | bytes 1376264 | tf_op jit(solution)/shard_map/ppermute | solution.py:275
  96.3 32.2 %collective-permute-start.16 = (bf16[256,896]{1,0:T(8,128)(2,1)}, bf16[256,896]{1,0:T(8,128)(2,1)S(1)}, u32[]{:S(2)}, u32[]{:S(2)}) collective-permute-start(bf16[256,896]{1,0:T(8,128)(2,1)} %get-tuple-element.106), channel_id=1, source_target_pairs={{0,1},{1,0},{2,3},{3,2},{4,5},{5,4},{6,7},{7,6},{8,9},{9,8},{10,11... | collective-permute-start | bytes 1376264 | tf_op jit(solution)/shard_map/ppermute | solution.py:275
  101.9 29.6 %collective-permute-start.14 = (bf16[256,768]{1,0:T(8,128)(2,1)}, bf16[256,768]{1,0:T(8,128)(2,1)}, u32[]{:S(2)}, u32[]{:S(2)}) collective-permute-start(bf16[256,768]{1,0:T(8,128)(2,1)} %get-tuple-element.104), channel_id=1, source_target_pairs={{0,1},{1,0},{2,3},{3,2},{4,5},{5,4},{6,7},{7,6},{8,9},{9,8},{10,11... | collective-permute-start | bytes 1179656 | tf_op jit(solution)/shard_map/ppermute | solution.py:275
  105.0 21.5 %collective-permute-start.10 = (bf16[128,768]{1,0:T(8,128)(2,1)}, bf16[128,768]{1,0:T(8,128)(2,1)}, u32[]{:S(2)}, u32[]{:S(2)}) collective-permute-start(bf16[128,768]{1,0:T(8,128)(2,1)} %get-tuple-element.89), channel_id=1, source_target_pairs={{0,1},{1,0},{2,3},{3,2},{4,5},{5,4},{6,7},{7,6},{8,9},{9,8},{10,11... | collective-permute-start | bytes 589832 | tf_op jit(solution)/shard_map/ppermute | solution.py:275
  128.5 0.8 copy-start.2
  128.5 0.9 copy-start.3

commit v3 on v2

--- a/solution.py
+++ b/solution.py
@@ -13,11 +13,13 @@
 TILE = 128
 ROWS = 256
 CHUNKS = (7, 7, 6)
+RELAYED = (1,)
 SCALE = 1.0 / math.sqrt(HEAD)
 LOG2E = math.log2(math.e)
 DEAD = -1e30
 BF16 = jnp.bfloat16
-PARAMS = pltpu.CompilerParams(vmem_limit_bytes=66_000_000)
+COST = pl.CostEstimate(flops=1000, transcendentals=0, bytes_accessed=1000)
+PARAMS = pltpu.CompilerParams(vmem_limit_bytes=67_000_000)
 
 NT = (((1,), (1,)), ((), ()))
 NN = (((1,), (0,)), ((), ()))
@@ -114,6 +116,7 @@
         + [pltpu.HBM((2, ROWS, hc * HEAD), BF16)] * 3,
         input_output_aliases=alias,
         compiler_params=PARAMS,
+        cost_estimate=COST,
         name="attn",
     )(side, *args)
 
@@ -129,27 +132,48 @@
         copy.wait()
 
 
-def combine_kernel(h0, hc, side_ref, own_ref, near_ref, far_ref, *refs):
-    keep_k, keep_v, send_ref, parts, kept, sent, in_sems, out_sems = refs[-8:]
+def combine_kernel(h0, hc, relayed, extra, moves, n_in, side_ref, *refs):
     f32, side = jnp.float32, side_ref[0]
+    ins, outs = refs[:n_in], refs[n_in : n_in + 4]
+    parts, kept, sent, in_sems, out_sems, carry_sems, *stages = refs[n_in + 4 :]
+    keep_k, keep_v, send_ref, out_q = outs
     fetches = [
         [
-            pltpu.make_async_copy(src.at[j], parts.at[j, n], in_sems.at[j, n])
-            for n, src in enumerate((own_ref, near_ref, far_ref))
+            pltpu.make_async_copy(ins[n].at[j], parts.at[j, n], in_sems.at[j, n])
+            for n in range(3 + relayed)
         ]
         for j in range(2)
     ]
-    for copy in fetches[0] + fetches[1]:
+    carries, at = [], 3 + relayed
+    if extra:
+        carries.append((ins[at], send_ref.at[pl.ds(2 * TILE, TILE), pl.ds(0, extra * HEAD)]))
+        at += 1
+    for part, row, out, o0, oc in moves:
+        source = ins[at + part].at[pl.ds(row, TILE), pl.ds(0, oc * HEAD)]
+        carries.append((source, (out_q, keep_k, keep_v)[out].at[:, columns(1 - side, o0, oc)]))
+    carries = [
+        (
+            pltpu.make_async_copy(source, stages[n], carry_sems.at[n, 0]),
+            pltpu.make_async_copy(stages[n], target, carry_sems.at[n, 1]),
+        )
+        for n, (source, target) in enumerate(carries)
+    ]
+    for copy in fetches[0] + fetches[1] + [fetch for fetch, _ in carries]:
         copy.start()
     leaving = []
     for j, keep in enumerate((keep_k, keep_v)):
         for copy in fetches[j]:
             copy.wait()
-        total = parts[j, 0].astype(f32) + parts[j, 1].astype(f32) + parts[j, 2].astype(f32)
+        far = parts[j, 2]
+        if relayed:
+            far = jnp.where(side_ref[1] == 1, parts[j, 3], far)
+        total = parts[j, 0].astype(f32) + parts[j, 1].astype(f32) + far.astype(f32)
         split_rows(side, total.astype(BF16), kept.at[j], sent.at[j])
         leaving += [
             pltpu.make_async_copy(
-                sent.at[j], send_ref.at[pl.ds(j * TILE, TILE)], out_sems.at[j, 0]
+                sent.at[j],
+                send_ref.at[pl.ds(j * TILE, TILE), pl.ds(0, hc * HEAD)],
+                out_sems.at[j, 0],
             ),
             pltpu.make_async_copy(
                 kept.at[j], keep.at[:, columns(side, h0, hc)], out_sems.at[j, 1]
@@ -157,73 +181,83 @@
         ]
         for copy in leaving[-2:]:
             copy.start()
+    for fetch, store in carries:
+        fetch.wait()
+        store.start()
+        leaving.append(store)
     for copy in leaving:
         copy.wait()
 
 
-def combine(side, own, from_near, from_far, outs, h0, hc):
-    width = hc * HEAD
+def combine(side, own, from_near, from_far, out_q, out_kv, send_q, extra, arrived, moves, h0, hc):
+    width, relayed = hc * HEAD, len(from_far) - 1
     anywhere = pl.BlockSpec(memory_space=pl.ANY)
-    args, alias = [own, from_near, from_far], {}
-    if outs is not None:
-        args += list(outs)
-        alias = {4: 0, 5: 1}
+    args = [own, from_near, *from_far, *([send_q] if extra else []), *arrived]
+    alias = {1 + len(args): 3}
+    args.append(out_q)
+    if out_kv is not None:
+        alias |= {1 + len(args): 0, 2 + len(args): 1}
+        args += list(out_kv)
+    send_shape = (3 * TILE, max(hc, extra) * HEAD) if extra else (2 * TILE, width)
+    stages = ([(TILE, extra * HEAD)] if extra else []) + [(TILE, m[4] * HEAD) for m in moves]
+    whole = pltpu.HBM((TILE, 2 * H * HEAD), BF16)
     return pl.pallas_call(
-        functools.partial(combine_kernel, h0, hc),
+        functools.partial(combine_kernel, h0, hc, relayed, extra, moves, len(args)),
         grid_spec=pltpu.PrefetchScalarGridSpec(
             num_scalar_prefetch=1,
             grid=(1,),
             in_specs=[anywhere] * len(args),
-            out_specs=[anywhere] * 3,
+            out_specs=[anywhere] * 4,
             scratch_shapes=[
-                pltpu.VMEM((2, 3, ROWS, width), BF16),
+                pltpu.VMEM((2, 3 + relayed, ROWS, width), BF16),
                 pltpu.VMEM((2, TILE, width), BF16),
                 pltpu.VMEM((2, TILE, width), BF16),
-                pltpu.SemaphoreType.DMA((2, 3)),
+                pltpu.SemaphoreType.DMA((2, 3 + relayed)),
                 pltpu.SemaphoreType.DMA((2, 2)),
-            ],
+                pltpu.SemaphoreType.DMA((max(len(stages), 1), 2)),
+            ]
+            + [pltpu.VMEM(shape, BF16) for shape in stages],
         ),
-        out_shape=[pltpu.HBM((TILE, 2 * H * HEAD), BF16)] * 2
-        + [pltpu.HBM((2 * TILE, width), BF16)],
+        out_shape=[whole, whole, pltpu.HBM(send_shape, BF16), whole],
         input_output_aliases=alias,
         compiler_params=PARAMS,
+        cost_estimate=COST,
         name="combine",
     )(side, *args)
 
 
 def place_kernel(moves, side_ref, *refs):
     sems = refs[-1]
-    outs = refs[len(refs) - 1 - max(o for _, _, o, _, _ in moves) - 1 : -1]
-    copies = [
-        pltpu.make_async_copy(
-            refs[part].at[pl.ds(row, TILE)],
-            outs[o].at[:, columns(1 - side_ref[0], h0, hc)],
-            sems.at[n],
-        )
-        for n, (part, row, o, h0, hc) in enumerate(moves)
-    ]
-    run_all(copies)
-
-
-def place(side, parts, outs, spans):
-    moves = [
-        (p, o * TILE, o, h0, hc) for p, (h0, hc) in enumerate(spans) for o in range(len(outs))
-    ]
+    outs = refs[-4:-1]
+    run_all(
+        [
+            pltpu.make_async_copy(
+                refs[0].at[pl.ds(row, TILE), pl.ds(0, oc * HEAD)],
+                outs[out].at[:, columns(1 - side_ref[0], o0, oc)],
+                sems.at[n],
+            )
+            for n, (row, out, o0, oc) in enumerate(moves)
+        ]
+    )
+
+
+def place(side, part, outs, moves):
+    anywhere = pl.BlockSpec(memory_space=pl.ANY)
     return pl.pallas_call(
         functools.partial(place_kernel, moves),
         grid_spec=pltpu.PrefetchScalarGridSpec(
             num_scalar_prefetch=1,
             grid=(1,),
-            in_specs=[pl.BlockSpec(part.shape, lambda i, s: (0, 0)) for part in parts]
-            + [pl.BlockSpec(memory_space=pl.ANY)] * len(outs),
-            out_specs=[pl.BlockSpec(memory_space=pl.ANY)] * len(outs),
+            in_specs=[pl.BlockSpec(part.shape, lambda i, s: (0, 0))] + [anywhere] * 3,
+            out_specs=[anywhere] * 3,
             scratch_shapes=[pltpu.SemaphoreType.DMA((len(moves),))],
         ),
-        out_shape=[pltpu.HBM((TILE, 2 * H * HEAD), BF16)] * len(outs),
-        input_output_aliases={1 + len(parts) + j: j for j in range(len(outs))},
+        out_shape=[pltpu.HBM((TILE, 2 * H * HEAD), BF16)] * 3,
+        input_output_aliases={2 + j: j for j in range(3)},
         compiler_params=PARAMS,
+        cost_estimate=COST,
         name="place",
-    )(side, *parts, *outs)
+    )(side, part, *outs)
 
 
 def pack_kernel(spans, k_ref, v_ref, *refs):
@@ -258,6 +292,7 @@
         scratch_shapes=[pltpu.VMEM((2, ROWS, hc * HEAD), BF16) for _, hc in spans]
         + [pltpu.SemaphoreType.DMA((len(spans), 2, 2))],
         compiler_params=PARAMS,
+        cost_estimate=COST,
         name="pack",
     )(k, v)
 
@@ -266,9 +301,25 @@
     return lax.ppermute(x, "ctx", [(i, i ^ 1) for i in range(lax.axis_size("ctx"))])
 
 
-def far_swap(x):
+def corners():
     count = lax.axis_size("ctx")
-    return lax.ppermute(x, "ctx", [(i, (i + 2 * (i % 2) - 1) % count) for i in range(count)])
+    return (0, count // 2 - 1, count // 2, count - 1)
+
+
+def far_pairs():
+    count = lax.axis_size("ctx")
+    return [(i, (i + 2 * (i % 2) - 1) % count) for i in range(count)]
+
+
+def far_swap(x, in_legs=False):
+    half = lax.axis_size("ctx") // 2
+    pairs = [(i, j ^ half if in_legs and i in corners() else j) for i, j in far_pairs()]
+    return lax.ppermute(x, "ctx", pairs)
+
+
+def across_x(x):
+    half = lax.axis_size("ctx") // 2
+    return lax.ppermute(x, "ctx", [(i, i ^ half) for i in corners()])
 
 
 def swap(x):
@@ -281,7 +332,8 @@
 
 def on_device(queries, key_states, value_states, out_grad, tile_mask):
     position = lax.axis_index("ctx")
-    side = lax.axis_index("section").astype(jnp.int32).reshape(1)
+    at_corner = functools.reduce(jnp.logical_or, [position == i for i in corners()])
+    side = jnp.stack([lax.axis_index("section").astype(jnp.int32), at_corner.astype(jnp.int32)])
     own_mask = lax.dynamic_slice_in_dim(tile_mask, position * 2, 2, 0)
     bias = jnp.where(jnp.repeat(own_mask.T, TILE, axis=1) > 0, 0.0, DEAD).astype(jnp.float32)
     before, own, after = bias[0:2], bias[2:4], bias[4:6]
@@ -300,12 +352,28 @@
     bias, *_ = lax.optimization_barrier((bias, *packs))
 
     out_q, out_kv = None, None
-    q_parts, kv_parts, owns, from_far, from_near = [], [], [], [], []
-
-    def finish(n, own):
-        nonlocal out_kv
-        h0, hc = spans[n]
-        *out_kv, send = combine(side, own, from_near[n], from_far[n], out_kv, h0, hc)
+    sends, kv_parts, owns, from_far, from_near = [], [], [], [], []
+    first_q = None
+
+    def arrivals(n):
+        moves = [(0, 1, *spans[n]), (TILE, 2, *spans[n])]
+        return moves + ([(2 * TILE, 0, *spans[n + 1])] if n + 1 < count else [])
+
+    def finish(n):
+        nonlocal out_q, out_kv
+        legs = [from_far[n]]
+        if n in RELAYED:
+            legs.append(across_x(from_far[n]))
+        last = n + 1 == count
+        arrived, moves = [], []
+        if n == 1:
+            arrived, moves = [first_q], [(0, 0, 0, *spans[0])]
+        if n >= 2:
+            arrived, moves = [kv_parts[n - 2]], [(0, *move) for move in arrivals(n - 2)]
+        *out_kv, send, out_q = combine(
+            side, owns[n], from_near[n], legs, out_q, out_kv,
+            None if last else sends[n + 1], 0 if last else spans[n + 1][1], arrived, moves, *spans[n],
+        )
         kv_parts.append(swap(send))
 
     def after(arrived, *values):
@@ -321,31 +389,36 @@
             (near_part,) = after(arrived, nears[n - 1])
             from_near.append(near_swap(near_part))
             if n >= 2:
-                finish(n - 2, owns[n - 2])
+                finish(n - 2)
+                fars[n], out_kv[0] = lax.optimization_barrier((fars[n], out_kv[0]))
         out_q, send_q, own, near_part, far_part = attn_chunk(
             side, queries, out_grad, key_states, value_states, near_k, near_v, fars[n], bias,
             out_q, h0, hc,
         )
-        arrived = []
-        if n >= 1:
-            arrived += [(q_parts, n - 1), (from_near, n - 1)]
-        if 2 <= n < count - 1:
+        arrived = [(from_near, n - 1)] if n >= 1 else []
+        if n >= 2:
             arrived.append((kv_parts, n - 2))
         if n + 2 < count:
             arrived.append((packs, n + 2))
-        send_q, own, near_part, far_part = after(arrived, send_q, own, near_part, far_part)
-        from_far.append(far_swap(far_part))
+        values = (send_q, own, near_part, far_part)
+        if n == 1:
+            *values, first_q = after(arrived, *values, first_q)
+        else:
+            values = after(arrived, *values)
+        send_q, own, near_part, far_part = values
+        from_far.append(far_swap(far_part, n in RELAYED))
         if n + 2 < count:
             fars.append(far_swap(packs[n + 2]))
-        q_parts.append(swap(send_q))
+        if n == 0:
+            first_q = swap(send_q)
+        sends.append(send_q)
         nears.append(near_part)
         owns.append(own)
     from_near.append(near_swap(nears[-1]))
     for n in range(max(count - 2, 0), count):
-        finish(n, owns[n])
-    (out_q,) = place(side, q_parts, [out_q], spans)
-    out_kv = place(side, kv_parts[:-1], out_kv, spans[:-1])
-    out_kv = place(side, kv_parts[-1:], out_kv, spans[-1:])
+        finish(n)
+    for n in range(max(count - 2, 0), count):
+        out_q, *out_kv = place(side, kv_parts[n], (out_q, *out_kv), arrivals(n))
     return (out_q, *out_kv)
 
 

time: 135 us -> 128 us (0.948)
  waiting for transfers between devices: 54.3 us -> 39.6 us
  Pallas kernels: 46.9 us -> 51.3 us
  starting transfers between devices: 29.4 us -> 33.5 us
    ppermute x6 -> x4, waiting for transfers between devices: 36.3 us -> 21.9 us  [swap(): return lax.ppermute(x, 'section', [(0, 1), (1, 0)])]
    pallas_call x3, Pallas kernels: 8.55 us -> 11.6 us  [combine(): pl.pallas_call(functools.partial(combine_kernel, h0, hc, relayed, extra,...]
    pallas_call x3, Pallas kernels: 28.3 us -> 30.4 us  [attn_chunk(): pl.pallas_call(attn_kernel, grid_spec=pltpu.PrefetchScalarGridSpec(num_sc...]
    ppermute x6 -> x7, starting transfers between devices: 4.3 us -> 6.23 us  [the longest x6 4.64 us: far_swap(): return lax.ppermute(x, 'ctx', pairs)]
    ppermute x6 -> x4, starting transfers between devices: 13 us -> 14.1 us  [swap(): return lax.ppermute(x, 'section', [(0, 1), (1, 0)])]
    pallas_call x3 -> x2, Pallas kernels: 5.86 us -> 5.03 us  [place(): pl.pallas_call(functools.partial(place_kernel, moves), grid_spec=pltpu.Pr...]
    ppermute x6 -> x7, waiting for transfers between devices: 18 us -> 17.7 us  [the longest x6 17.7 us: far_swap(): return lax.ppermute(x, 'ctx', pairs)]
  transfers between devices with their start and end apart: 17 -> 16, of which waited for: 5 -> 6; matrix products, arithmetic and copies ran while one was open for 1% -> 1% of each run, Pallas kernels for 34% -> 39%
where the time goes in v3:
time: 128 us; the launch traced here: 127 us
  Pallas kernels  51.3 us (40%)
  waiting for transfers between devices  39.6 us (31%)
  starting transfers between devices  33.5 us (26%)
  other arithmetic  1.34 us (1%)
    pallas_call x3, Pallas kernels, attn_chunk(): pl.pallas_call(attn_kernel, grid_spec=pltpu.PrefetchScalarGridSpec(num_sc...  30.4 us
    ppermute x4, waiting for transfers between devices, swap(): return lax.ppermute(x, 'section', [(0, 1), (1, 0)])  21.9 us
    ppermute x6, waiting for transfers between devices, far_swap(): return lax.ppermute(x, 'ctx', pairs)  17.7 us
    ppermute x4, starting transfers between devices, swap(): return lax.ppermute(x, 'section', [(0, 1), (1, 0)])  14.1 us
    ppermute x5, starting transfers between devices, near_swap(): lax.ppermute(x, 'ctx', [(i, i ^ 1) for i in range(lax.axis_size('ctx'))])  13.2 us
    pallas_call x3, Pallas kernels, combine(): pl.pallas_call(functools.partial(combine_kernel, h0, hc, relayed, extra,...  11.6 us
    pallas_call x2, Pallas kernels, place(): pl.pallas_call(functools.partial(place_kernel, moves), grid_spec=pltpu.Pr...  5.03 us
    ppermute x6, starting transfers between devices, far_swap(): return lax.ppermute(x, 'ctx', pairs)  4.64 us
  transfers between devices with their start and end apart: 16, of which 6 were waited for; matrix products, arithmetic and copies ran while one was open for 1% of the time, Pallas kernels for 39%

profile of v3, /device:TPU:225, one launch (start us, length us, event | category | flops | bytes accessed | tf_op | source)
XLA Modules:
  0.0 126.8 jit_solution(11840085983264579249)
XLA Ops:
  0.6 0.8 collective-permute-start
  1.4 0.1 collective-permute-start.1
  1.5 2.0 %pack.2 = bf16[2,256,896]{2,1,0:T(8,128)(2,1)} custom-call(bf16[256,2560]{1,0:T(8,128)(2,1)} %k_ref.8, bf16[256,2560]{1,0:T(8,128)(2,1)} %v_ref.9), custom_call_target="tpu_custom_call" | custom-call | flops 1000 | bytes 1000 | tf_op jit(solution)/shard_map/pack/pallas_call | solution.py:286
  3.5 1.7 %collective-permute-start.2 = (bf16[2,256,896]{2,1,0:T(8,128)(2,1)}, bf16[2,256,896]{2,1,0:T(8,128)(2,1)}, u32[]{:S(2)}, u32[]{:S(2)}) collective-permute-start(bf16[2,256,896]{2,1,0:T(8,128)(2,1)} %pack.2), channel_id=1, source_target_pairs={{0,254},{2,4},{4,2},{6,8},{8,6},{10,12},{12,10},{14,16},{16,14},{1... | collective-permute-start | bytes 2752520 | tf_op jit(solution)/shard_map/ppermute | solution.py:317
  5.2 2.3 %pack.3 = (bf16[2,256,896]{2,1,0:T(8,128)(2,1)}, bf16[2,256,768]{2,1,0:T(8,128)(2,1)}) custom-call(bf16[256,2560]{1,0:T(8,128)(2,1)} %k_ref.8, bf16[256,2560]{1,0:T(8,128)(2,1)} %v_ref.9), custom_call_target="tpu_custom_call" | custom-call | flops 1000 | bytes 1000 | tf_op jit(solution)/shard_map/pack/pallas_call | solution.py:286
  7.5 0.8 collective-permute-start.3
  8.6 0.6 pad_add_fusion.side_ref
  9.2 0.7 maximum_maximum_fusion.bias_ref
  9.8 7.2 %collective-permute-done.2.far_ref = bf16[2,256,896]{2,1,0:T(8,128)(2,1)} collective-permute-done((bf16[2,256,896]{2,1,0:T(8,128)(2,1)}, bf16[2,256,896]{2,1,0:T(8,128)(2,1)}, u32[]{:S(2)}, u32[]{:S(2)}) %collective-permute-start.2) | collective-permute-done | bytes 917536 | tf_op jit(solution)/shard_map/ppermute | solution.py:317
  17.0 10.5 %attn.3 = (bf16[128,5120]{1,0:T(8,128)(2,1)}, bf16[128,896]{1,0:T(8,128)(2,1)}, bf16[2,256,896]{2,1,0:T(8,128)(2,1)}, bf16[2,256,896]{2,1,0:T(8,128)(2,1)}, bf16[2,256,896]{2,1,0:T(8,128)(2,1)}) custom-call(s32[2]{0:T(128)} %pad_add_fusion.side_ref, bf16[256,2560]{1,0:T(8,128)(2,1)} %q_ref.5, bf16[256,2560]{1,0:T(8,128)(2,1)} %do_ref.5, ...), custom_call_target="tpu_custom_call" | custom-call | flops 1000 | bytes 1000 | tf_op jit(solution)/shard_map/attn/pallas_call | solution.py:98
  27.5 2.3 %collective-permute-start.5 = (bf16[2,256,896]{2,1,0:T(8,128)(2,1)}, bf16[2,256,896]{2,1,0:T(8,128)(2,1)}, u32[]{:S(2)}, u32[]{:S(2)}) collective-permute-start(bf16[2,256,896]{2,1,0:T(8,128)(2,1)} %get-tuple-element.79), channel_id=1, source_target_pairs={{0,2},{2,0},{4,6},{6,4},{8,10},{10,8},{12,14},{14,12},{16,18},{18,... | collective-permute-start | bytes 2752520 | tf_op jit(solution)/shard_map/ppermute | solution.py:301
  29.8 1.7 %collective-permute-start.6 = (bf16[2,256,768]{2,1,0:T(8,128)(2,1)}, bf16[2,256,768]{2,1,0:T(8,128)(2,1)}, u32[]{:S(2)}, u32[]{:S(2)}) collective-permute-start(bf16[2,256,768]{2,1,0:T(8,128)(2,1)} %get-tuple-element.81), channel_id=1, source_target_pairs={{0,254},{2,4},{4,2},{6,8},{8,6},{10,12},{12,10},{14,16},{16,14},{1... | collective-permute-start | bytes 2359304 | tf_op jit(solution)/shard_map/ppermute | solution.py:317
  31.5 2.8 %collective-permute-start.4 = (bf16[128,896]{1,0:T(8,128)(2,1)}, bf16[128,896]{1,0:T(8,128)(2,1)}, u32[]{:S(2)}, u32[]{:S(2)}) collective-permute-start(bf16[128,896]{1,0:T(8,128)(2,1)} %get-tuple-element.78), channel_id=1, source_target_pairs={{0,1},{1,0},{2,3},{3,2},{4,5},{5,4},{6,7},{7,6},{8,9},{9,8},{10,11... | collective-permute-start | bytes 688136 | tf_op jit(solution)/shard_map/ppermute | solution.py:326
  34.3 10.5 %attn.4 = (bf16[128,5120]{1,0:T(8,128)(2,1)}, bf16[128,896]{1,0:T(8,128)(2,1)}, bf16[2,256,896]{2,1,0:T(8,128)(2,1)}, bf16[2,256,896]{2,1,0:T(8,128)(2,1)}, bf16[2,256,896]{2,1,0:T(8,128)(2,1)}) custom-call(s32[2]{0:T(128)} %pad_add_fusion.side_ref, bf16[256,2560]{1,0:T(8,128)(2,1)} %q_ref.5, ...), custom_call_target="tpu_custom_call", output_to_operand_aliasing={{0}: (9, {})} | custom-call | flops 1000 | bytes 1000 | tf_op jit(solution)/shard_map/attn/pallas_call | solution.py:98
  44.8 0.4 collective-permute-start.12
  45.3 6.4 %collective-permute-done.6.far_ref = bf16[2,256,768]{2,1,0:T(8,128)(2,1)} collective-permute-done((bf16[2,256,768]{2,1,0:T(8,128)(2,1)}, bf16[2,256,768]{2,1,0:T(8,128)(2,1)}, u32[]{:S(2)}, u32[]{:S(2)}) %collective-permute-start.6) | collective-permute-done | bytes 786464 | tf_op jit(solution)/shard_map/ppermute | solution.py:317
  51.7 7.4 %collective-permute-start.8 = (bf16[2,256,896]{2,1,0:T(8,128)(2,1)}, bf16[2,256,896]{2,1,0:T(8,128)(2,1)}, u32[]{:S(2)}, u32[]{:S(2)}) collective-permute-start(bf16[2,256,896]{2,1,0:T(8,128)(2,1)} %get-tuple-element.96), channel_id=1, source_target_pairs={{0,2},{2,0},{4,6},{6,4},{8,10},{10,8},{12,14},{14,12},{16,18},{18,... | collective-permute-start | bytes 2752520 | tf_op jit(solution)/shard_map/ppermute | solution.py:301
  59.0 3.7 %combine.3 = (bf16[128,5120]{1,0:T(8,128)(2,1)}, bf16[128,5120]{1,0:T(8,128)(2,1)}, bf16[384,896]{1,0:T(8,128)(2,1)}, bf16[128,5120]{1,0:T(8,128)(2,1)}) custom-call(s32[2]{0:T(128)} %pad_add_fusion.side_ref, bf16[2,256,896]{2,1,0:T(8,128)(2,1)} %get-tuple-element.84.refs_0_, ...), custom_call_target="tpu_custom_call", output_to_operand_aliasing={{3}: (5, {})} | custom-call | flops 1000 | bytes 1000 | tf_op jit(solution)/shard_map/combine/pallas_call | solution.py:204
  62.7 3.8 %collective-permute-start.9 = (bf16[384,896]{1,0:T(8,128)(2,1)}, bf16[384,896]{1,0:T(8,128)(2,1)}, u32[]{:S(2)}, u32[]{:S(2)}) collective-permute-start(bf16[384,896]{1,0:T(8,128)(2,1)} %get-tuple-element.97), channel_id=1, source_target_pairs={{0,1},{1,0},{2,3},{3,2},{4,5},{5,4},{6,7},{7,6},{8,9},{9,8},{10,11... | collective-permute-start | bytes 2064392 | tf_op jit(solution)/shard_map/ppermute | solution.py:326
  66.5 1.6 %collective-permute-start.13 = (bf16[2,256,896]{2,1,0:T(8,128)(2,1)}, bf16[2,256,896]{2,1,0:T(8,128)(2,1)}, u32[]{:S(2)}, u32[]{:S(2)}) collective-permute-start(bf16[2,256,896]{2,1,0:T(8,128)(2,1)} %collective-permute-done.12.refs_2_), channel_id=1, source_target_pairs={{0,128},{126,254},{128,0},{254,126},{1,129},{127,255},{129,1},{255... | collective-permute-start | bytes 2752520 | tf_op jit(solution)/shard_map/ppermute | solution.py:322
  68.1 9.4 %attn.5 = (bf16[128,5120]{1,0:T(8,128)(2,1)}, bf16[128,768]{1,0:T(8,128)(2,1)}, bf16[2,256,768]{2,1,0:T(8,128)(2,1)}, bf16[2,256,768]{2,1,0:T(8,128)(2,1)}, bf16[2,256,768]{2,1,0:T(8,128)(2,1)}) custom-call(s32[2]{0:T(128)} %pad_add_fusion.side_ref, bf16[256,2560]{1,0:T(8,128)(2,1)} %q_ref.5, ...), custom_call_target="tpu_custom_call", output_to_operand_aliasing={{0}: (9, {})} | custom-call | flops 1000 | bytes 1000 | tf_op jit(solution)/shard_map/attn/pallas_call | solution.py:98
  77.5 5.1 %collective-permute-done.9.refs_3_ = bf16[384,896]{1,0:T(8,128)(2,1)} collective-permute-done((bf16[384,896]{1,0:T(8,128)(2,1)}, bf16[384,896]{1,0:T(8,128)(2,1)}, u32[]{:S(2)}, u32[]{:S(2)}) %collective-permute-start.9) | collective-permute-done | bytes 688160 | tf_op jit(solution)/shard_map/ppermute | solution.py:326
  82.6 2.6 %collective-permute-start.10 = (bf16[2,256,768]{2,1,0:T(8,128)(2,1)}, bf16[2,256,768]{2,1,0:T(8,128)(2,1)}, u32[]{:S(2)}, u32[]{:S(2)}) collective-permute-start(bf16[2,256,768]{2,1,0:T(8,128)(2,1)} %get-tuple-element.99), channel_id=1, source_target_pairs={{0,2},{2,0},{4,6},{6,4},{8,10},{10,8},{12,14},{14,12},{16,18},{18,... | collective-permute-start | bytes 2359304 | tf_op jit(solution)/shard_map/ppermute | solution.py:301
  85.3 4.1 %combine.4 = (bf16[128,5120]{1,0:T(8,128)(2,1)}, bf16[128,5120]{1,0:T(8,128)(2,1)}, bf16[384,896]{1,0:T(8,128)(2,1)}, bf16[128,5120]{1,0:T(8,128)(2,1)}) custom-call(s32[2]{0:T(128)} %pad_add_fusion.side_ref, bf16[2,256,896]{2,1,0:T(8,128)(2,1)} %get-tuple-element.102.refs_0_, ...), custom_call_target="tpu_custom_call", output_to_operand_aliasing={{3}: (7, {}), {0}: (8, {}), {1}: (9, {})} | custom-call | flops 1000 | bytes 1000 | tf_op jit(solution)/shard_map/combine/pallas_call | solution.py:204
  89.4 3.8 %collective-permute-start.15 = (bf16[384,896]{1,0:T(8,128)(2,1)}, bf16[384,896]{1,0:T(8,128)(2,1)}, u32[]{:S(2)}, u32[]{:S(2)}) collective-permute-start(bf16[384,896]{1,0:T(8,128)(2,1)} %get-tuple-element.114), channel_id=1, source_target_pairs={{0,1},{1,0},{2,3},{3,2},{4,5},{5,4},{6,7},{7,6},{8,9},{9,8},{10,11... | collective-permute-start | bytes 2064392 | tf_op jit(solution)/shard_map/ppermute | solution.py:326
  93.2 4.1 %collective-permute-done.11.refs_2_ = bf16[2,256,768]{2,1,0:T(8,128)(2,1)} collective-permute-done((bf16[2,256,768]{2,1,0:T(8,128)(2,1)}, bf16[2,256,768]{2,1,0:T(8,128)(2,1)}, u32[]{:S(2)}, u32[]{:S(2)}) %collective-permute-start.11) | collective-permute-done | bytes 786464 | tf_op jit(solution)/shard_map/ppermute | solution.py:317
  97.3 3.8 %combine.5 = (bf16[128,5120]{1,0:T(8,128)(2,1)}, bf16[128,5120]{1,0:T(8,128)(2,1)}, bf16[256,768]{1,0:T(8,128)(2,1)}, bf16[128,5120]{1,0:T(8,128)(2,1)}) custom-call(s32[2]{0:T(128)} %pad_add_fusion.side_ref, bf16[2,256,768]{2,1,0:T(8,128)(2,1)} %get-tuple-element.98.refs_0_, ...), custom_call_target="tpu_custom_call", output_to_operand_aliasing={{3}: (5, {}), {0}: (6, {}), {1}: (7, {})} | custom-call | flops 1000 | bytes 1000 | tf_op jit(solution)/shard_map/combine/pallas_call | solution.py:204
  101.1 3.8 %collective-permute-start.14 = (bf16[256,768]{1,0:T(8,128)(2,1)}, bf16[256,768]{1,0:T(8,128)(2,1)}, u32[]{:S(2)}, u32[]{:S(2)}) collective-permute-start(bf16[256,768]{1,0:T(8,128)(2,1)} %get-tuple-element.113), channel_id=1, source_target_pairs={{0,1},{1,0},{2,3},{3,2},{4,5},{5,4},{6,7},{7,6},{8,9},{9,8},{10,11... | collective-permute-start | bytes 1179656 | tf_op jit(solution)/shard_map/ppermute | solution.py:326
  104.9 11.0 %collective-permute-done.15.refs_0_ = bf16[384,896]{1,0:T(8,128)(2,1)} collective-permute-done((bf16[384,896]{1,0:T(8,128)(2,1)}, bf16[384,896]{1,0:T(8,128)(2,1)}, u32[]{:S(2)}, u32[]{:S(2)}) %collective-permute-start.15) | collective-permute-done | bytes 688160 | tf_op jit(solution)/shard_map/ppermute | solution.py:326
  115.8 2.6 %place.2 = (bf16[128,5120]{1,0:T(8,128)(2,1)}, bf16[128,5120]{1,0:T(8,128)(2,1)}, bf16[128,5120]{1,0:T(8,128)(2,1)}) custom-call(s32[2]{0:T(128)} %pad_add_fusion.side_ref, bf16[384,896]{1,0:T(8,128)(2,1)} %collective-permute-done.15.refs_0_, ...), custom_call_target="tpu_custom_call", output_to_operand_aliasing={{0}: (2, {}), {1}: (3, {}), {2}: (4, {})} | custom-call | flops 1000 | bytes 1000 | tf_op jit(solution)/shard_map/place/pallas_call | solution.py:246
  118.4 5.8 %collective-permute-done.14.refs_0_ = bf16[256,768]{1,0:T(8,128)(2,1)} collective-permute-done((bf16[256,768]{1,0:T(8,128)(2,1)}, bf16[256,768]{1,0:T(8,128)(2,1)}, u32[]{:S(2)}, u32[]{:S(2)}) %collective-permute-start.14) | collective-permute-done | bytes 393248 | tf_op jit(solution)/shard_map/ppermute | solution.py:326
  124.3 2.4 %place.3 = (bf16[128,5120]{1,0:T(8,128)(2,1)}, bf16[128,5120]{1,0:T(8,128)(2,1)}, bf16[128,5120]{1,0:T(8,128)(2,1)}) custom-call(s32[2]{0:T(128)} %pad_add_fusion.side_ref, bf16[256,768]{1,0:T(8,128)(2,1)} %collective-permute-done.14.refs_0_, ...), custom_call_target="tpu_custom_call", output_to_operand_aliasing={{0}: (2, {}), {1}: (3, {}), {2}: (4, {})} | custom-call | flops 1000 | bytes 1000 | tf_op jit(solution)/shard_map/place/pallas_call | solution.py:246
  (23 shorter events, 0.3 us)
Async XLA Ops:
  0.6 4.5 %copy-start = (s32[256,6]{0,1:T(8,128)S(1)}, s32[256,6]{0,1:T(8,128)}, u32[]{:S(2)}) copy-start(s32[256,6]{0,1:T(8,128)} %param.9) | copy-start | bytes 18436
  0.6 4.6 %collective-permute-start = (bf16[256,2560]{1,0:T(8,128)(2,1)}, bf16[256,2560]{1,0:T(8,128)(2,1)}, u32[]{:S(2)}, u32[]{:S(2)}) collective-permute-start(bf16[256,2560]{1,0:T(8,128)(2,1)} %k_ref.8), channel_id=1, source_target_pairs={{0,2},{2,0},{4,6},{6,4},{8,10},{10,8},{12,14},{14,12},{16,18},{18,... | collective-permute-start | bytes 3932168 | tf_op jit(solution)/shard_map/ppermute | solution.py:301
  1.4 15.6 %collective-permute-start.1 = (bf16[256,2560]{1,0:T(8,128)(2,1)}, bf16[256,2560]{1,0:T(8,128)(2,1)}, u32[]{:S(2)}, u32[]{:S(2)}) collective-permute-start(bf16[256,2560]{1,0:T(8,128)(2,1)} %v_ref.9), channel_id=1, source_target_pairs={{0,2},{2,0},{4,6},{6,4},{8,10},{10,8},{12,14},{14,12},{16,18},{18,... | collective-permute-start | bytes 3932168 | tf_op jit(solution)/shard_map/ppermute | solution.py:301
  3.5 13.5 %collective-permute-start.2 = (bf16[2,256,896]{2,1,0:T(8,128)(2,1)}, bf16[2,256,896]{2,1,0:T(8,128)(2,1)}, u32[]{:S(2)}, u32[]{:S(2)}) collective-permute-start(bf16[2,256,896]{2,1,0:T(8,128)(2,1)} %pack.2), channel_id=1, source_target_pairs={{0,254},{2,4},{4,2},{6,8},{8,6},{10,12},{12,10},{14,16},{16,14},{1... | collective-permute-start | bytes 2752520 | tf_op jit(solution)/shard_map/ppermute | solution.py:317
  7.5 20.0 %collective-permute-start.3 = (bf16[2,256,896]{2,1,0:T(8,128)(2,1)}, bf16[2,256,896]{2,1,0:T(8,128)(2,1)}, u32[]{:S(2)}, u32[]{:S(2)}) collective-permute-start(bf16[2,256,896]{2,1,0:T(8,128)(2,1)} %get-tuple-element.64), channel_id=1, source_target_pairs={{0,254},{2,4},{4,2},{6,8},{8,6},{10,12},{12,10},{14,16},{16,14},{1... | collective-permute-start | bytes 2752520 | tf_op jit(solution)/shard_map/ppermute | solution.py:317
  27.5 17.3 %collective-permute-start.5 = (bf16[2,256,896]{2,1,0:T(8,128)(2,1)}, bf16[2,256,896]{2,1,0:T(8,128)(2,1)}, u32[]{:S(2)}, u32[]{:S(2)}) collective-permute-start(bf16[2,256,896]{2,1,0:T(8,128)(2,1)} %get-tuple-element.79), channel_id=1, source_target_pairs={{0,2},{2,0},{4,6},{6,4},{8,10},{10,8},{12,14},{14,12},{16,18},{18,... | collective-permute-start | bytes 2752520 | tf_op jit(solution)/shard_map/ppermute | solution.py:301
  29.8 21.9 %collective-permute-start.7 = (bf16[2,256,896]{2,1,0:T(8,128)(2,1)}, bf16[2,256,896]{2,1,0:T(8,128)(2,1)}, u32[]{:S(2)}, u32[]{:S(2)}) collective-permute-start(bf16[2,256,896]{2,1,0:T(8,128)(2,1)} %get-tuple-element.82), channel_id=1, source_target_pairs={{0,254},{2,4},{4,2},{6,8},{8,6},{10,12},{12,10},{14,16},{16,14},{1... | collective-permute-start | bytes 2752520 | tf_op jit(solution)/shard_map/ppermute | solution.py:317
  29.8 21.9 %collective-permute-start.6 = (bf16[2,256,768]{2,1,0:T(8,128)(2,1)}, bf16[2,256,768]{2,1,0:T(8,128)(2,1)}, u32[]{:S(2)}, u32[]{:S(2)}) collective-permute-start(bf16[2,256,768]{2,1,0:T(8,128)(2,1)} %get-tuple-element.81), channel_id=1, source_target_pairs={{0,254},{2,4},{4,2},{6,8},{8,6},{10,12},{12,10},{14,16},{16,14},{1... | collective-permute-start | bytes 2359304 | tf_op jit(solution)/shard_map/ppermute | solution.py:317
  31.5 13.3 %collective-permute-start.4 = (bf16[128,896]{1,0:T(8,128)(2,1)}, bf16[128,896]{1,0:T(8,128)(2,1)}, u32[]{:S(2)}, u32[]{:S(2)}) collective-permute-start(bf16[128,896]{1,0:T(8,128)(2,1)} %get-tuple-element.78), channel_id=1, source_target_pairs={{0,1},{1,0},{2,3},{3,2},{4,5},{5,4},{6,7},{7,6},{8,9},{9,8},{10,11... | collective-permute-start | bytes 688136 | tf_op jit(solution)/shard_map/ppermute | solution.py:326
  44.8 21.7 %collective-permute-start.12 = (bf16[2,256,896]{2,1,0:T(8,128)(2,1)}, bf16[2,256,896]{2,1,0:T(8,128)(2,1)}, u32[]{:S(2)}, u32[]{:S(2)}) collective-permute-start(bf16[2,256,896]{2,1,0:T(8,128)(2,1)} %get-tuple-element.104), channel_id=1, source_target_pairs={{0,126},{2,4},{4,2},{6,8},{8,6},{10,12},{12,10},{14,16},{16,14},{1... | collective-permute-start | bytes 2752520 | tf_op jit(solution)/shard_map/ppermute | solution.py:317
  51.7 31.0 %collective-permute-start.8 = (bf16[2,256,896]{2,1,0:T(8,128)(2,1)}, bf16[2,256,896]{2,1,0:T(8,128)(2,1)}, u32[]{:S(2)}, u32[]{:S(2)}) collective-permute-start(bf16[2,256,896]{2,1,0:T(8,128)(2,1)} %get-tuple-element.96), channel_id=1, source_target_pairs={{0,2},{2,0},{4,6},{6,4},{8,10},{10,8},{12,14},{14,12},{16,18},{18,... | collective-permute-start | bytes 2752520 | tf_op jit(solution)/shard_map/ppermute | solution.py:301
  62.7 19.9 %collective-permute-start.9 = (bf16[384,896]{1,0:T(8,128)(2,1)}, bf16[384,896]{1,0:T(8,128)(2,1)}, u32[]{:S(2)}, u32[]{:S(2)}) collective-permute-start(bf16[384,896]{1,0:T(8,128)(2,1)} %get-tuple-element.97), channel_id=1, source_target_pairs={{0,1},{1,0},{2,3},{3,2},{4,5},{5,4},{6,7},{7,6},{8,9},{9,8},{10,11... | collective-permute-start | bytes 2064392 | tf_op jit(solution)/shard_map/ppermute | solution.py:326
  66.5 18.8 %collective-permute-start.13 = (bf16[2,256,896]{2,1,0:T(8,128)(2,1)}, bf16[2,256,896]{2,1,0:T(8,128)(2,1)}, u32[]{:S(2)}, u32[]{:S(2)}) collective-permute-start(bf16[2,256,896]{2,1,0:T(8,128)(2,1)} %collective-permute-done.12.refs_2_), channel_id=1, source_target_pairs={{0,128},{126,254},{128,0},{254,126},{1,129},{127,255},{129,1},{255... | collective-permute-start | bytes 2752520 | tf_op jit(solution)/shard_map/ppermute | solution.py:322
  82.6 10.6 %collective-permute-start.10 = (bf16[2,256,768]{2,1,0:T(8,128)(2,1)}, bf16[2,256,768]{2,1,0:T(8,128)(2,1)}, u32[]{:S(2)}, u32[]{:S(2)}) collective-permute-start(bf16[2,256,768]{2,1,0:T(8,128)(2,1)} %get-tuple-element.99), channel_id=1, source_target_pairs={{0,2},{2,0},{4,6},{6,4},{8,10},{10,8},{12,14},{14,12},{16,18},{18,... | collective-permute-start | bytes 2359304 | tf_op jit(solution)/shard_map/ppermute | solution.py:301
  85.3 12.0 %collective-permute-start.11 = (bf16[2,256,768]{2,1,0:T(8,128)(2,1)}, bf16[2,256,768]{2,1,0:T(8,128)(2,1)}, u32[]{:S(2)}, u32[]{:S(2)}) collective-permute-start(bf16[2,256,768]{2,1,0:T(8,128)(2,1)} %get-tuple-element.100), channel_id=1, source_target_pairs={{0,254},{2,4},{4,2},{6,8},{8,6},{10,12},{12,10},{14,16},{16,14},{1... | collective-permute-start | bytes 2359304 | tf_op jit(solution)/shard_map/ppermute | solution.py:317
  89.4 26.4 %collective-permute-start.15 = (bf16[384,896]{1,0:T(8,128)(2,1)}, bf16[384,896]{1,0:T(8,128)(2,1)}, u32[]{:S(2)}, u32[]{:S(2)}) collective-permute-start(bf16[384,896]{1,0:T(8,128)(2,1)} %get-tuple-element.114), channel_id=1, source_target_pairs={{0,1},{1,0},{2,3},{3,2},{4,5},{5,4},{6,7},{7,6},{8,9},{9,8},{10,11... | collective-permute-start | bytes 2064392 | tf_op jit(solution)/shard_map/ppermute | solution.py:326
  101.1 23.2 %collective-permute-start.14 = (bf16[256,768]{1,0:T(8,128)(2,1)}, bf16[256,768]{1,0:T(8,128)(2,1)}, u32[]{:S(2)}, u32[]{:S(2)}) collective-permute-start(bf16[256,768]{1,0:T(8,128)(2,1)} %get-tuple-element.113), channel_id=1, source_target_pairs={{0,1},{1,0},{2,3},{3,2},{4,5},{5,4},{6,7},{7,6},{8,9},{9,8},{10,11... | collective-permute-start | bytes 1179656 | tf_op jit(solution)/shard_map/ppermute | solution.py:326

commit v4 on v3

--- a/solution.py
+++ b/solution.py
@@ -12,7 +12,7 @@
 H = 20
 TILE = 128
 ROWS = 256
-CHUNKS = (7, 7, 6)
+CHUNKS = (6, 7, 7)
 RELAYED = (1,)
 SCALE = 1.0 / math.sqrt(HEAD)
 LOG2E = math.log2(math.e)
@@ -132,7 +132,7 @@
         copy.wait()
 
 
-def combine_kernel(h0, hc, relayed, extra, moves, n_in, side_ref, *refs):
+def combine_kernel(h0, hc, relayed, extra, moves, n_in, side_ref, corner_ref, *refs):
     f32, side = jnp.float32, side_ref[0]
     ins, outs = refs[:n_in], refs[n_in : n_in + 4]
     parts, kept, sent, in_sems, out_sems, carry_sems, *stages = refs[n_in + 4 :]
@@ -166,7 +166,7 @@
             copy.wait()
         far = parts[j, 2]
         if relayed:
-            far = jnp.where(side_ref[1] == 1, parts[j, 3], far)
+            far = jnp.where(corner_ref[0] == 1, parts[j, 3], far)
         total = parts[j, 0].astype(f32) + parts[j, 1].astype(f32) + far.astype(f32)
         split_rows(side, total.astype(BF16), kept.at[j], sent.at[j])
         leaving += [
@@ -189,14 +189,14 @@
         copy.wait()
 
 
-def combine(side, own, from_near, from_far, out_q, out_kv, send_q, extra, arrived, moves, h0, hc):
+def combine(side, corner, own, from_near, from_far, out_q, out_kv, send_q, extra, arrived, moves, h0, hc):
     width, relayed = hc * HEAD, len(from_far) - 1
     anywhere = pl.BlockSpec(memory_space=pl.ANY)
     args = [own, from_near, *from_far, *([send_q] if extra else []), *arrived]
-    alias = {1 + len(args): 3}
+    alias = {2 + len(args): 3}
     args.append(out_q)
     if out_kv is not None:
-        alias |= {1 + len(args): 0, 2 + len(args): 1}
+        alias |= {2 + len(args): 0, 3 + len(args): 1}
         args += list(out_kv)
     send_shape = (3 * TILE, max(hc, extra) * HEAD) if extra else (2 * TILE, width)
     stages = ([(TILE, extra * HEAD)] if extra else []) + [(TILE, m[4] * HEAD) for m in moves]
@@ -204,7 +204,7 @@
     return pl.pallas_call(
         functools.partial(combine_kernel, h0, hc, relayed, extra, moves, len(args)),
         grid_spec=pltpu.PrefetchScalarGridSpec(
-            num_scalar_prefetch=1,
+            num_scalar_prefetch=2,
             grid=(1,),
             in_specs=[anywhere] * len(args),
             out_specs=[anywhere] * 4,
@@ -223,7 +223,7 @@
         compiler_params=PARAMS,
         cost_estimate=COST,
         name="combine",
-    )(side, *args)
+    )(side, corner, *args)
 
 
 def place_kernel(moves, side_ref, *refs):
@@ -333,7 +333,8 @@
 def on_device(queries, key_states, value_states, out_grad, tile_mask):
     position = lax.axis_index("ctx")
     at_corner = functools.reduce(jnp.logical_or, [position == i for i in corners()])
-    side = jnp.stack([lax.axis_index("section").astype(jnp.int32), at_corner.astype(jnp.int32)])
+    at_corner = at_corner.astype(jnp.int32).reshape(1)
+    side = lax.axis_index("section").astype(jnp.int32).reshape(1)
     own_mask = lax.dynamic_slice_in_dim(tile_mask, position * 2, 2, 0)
     bias = jnp.where(jnp.repeat(own_mask.T, TILE, axis=1) > 0, 0.0, DEAD).astype(jnp.float32)
     before, own, after = bias[0:2], bias[2:4], bias[4:6]
@@ -348,7 +349,7 @@
     packs = list(pack(key_states, value_states, spans[:1]))
     later_keys, near_k = lax.optimization_barrier((key_states, near_k))
     packs += pack(later_keys, value_states, spans[1:])
-    fars = [far_swap(packs[0]), far_swap(packs[1])]
+    fars = [far_swap(x) for x in packs]
     bias, *_ = lax.optimization_barrier((bias, *packs))
 
     out_q, out_kv = None, None
@@ -363,7 +364,8 @@
         nonlocal out_q, out_kv
         legs = [from_far[n]]
         if n in RELAYED:
-            legs.append(across_x(from_far[n]))
+            (first_leg,) = after([(owns, n + 1)], from_far[n])
+            legs.append(across_x(first_leg))
         last = n + 1 == count
         arrived, moves = [], []
         if n == 1:
@@ -371,7 +373,7 @@
         if n >= 2:
             arrived, moves = [kv_parts[n - 2]], [(0, *move) for move in arrivals(n - 2)]
         *out_kv, send, out_q = combine(
-            side, owns[n], from_near[n], legs, out_q, out_kv,
+            side, at_corner, owns[n], from_near[n], legs, out_q, out_kv,
             None if last else sends[n + 1], 0 if last else spans[n + 1][1], arrived, moves, *spans[n],
         )
         kv_parts.append(swap(send))
@@ -398,8 +400,8 @@
         arrived = [(from_near, n - 1)] if n >= 1 else []
         if n >= 2:
             arrived.append((kv_parts, n - 2))
-        if n + 2 < count:
-            arrived.append((packs, n + 2))
+        if n >= 1 and n + 1 < count:
+            arrived.append((fars, n + 1))
         values = (send_q, own, near_part, far_part)
         if n == 1:
             *values, first_q = after(arrived, *values, first_q)
@@ -407,8 +409,6 @@
             values = after(arrived, *values)
         send_q, own, near_part, far_part = values
         from_far.append(far_swap(far_part, n in RELAYED))
-        if n + 2 < count:
-            fars.append(far_swap(packs[n + 2]))
         if n == 0:
             first_q = swap(send_q)
         sends.append(send_q)

time: 128 us -> 120 us (0.938)
  starting transfers between devices: 33.5 us -> 14.3 us
  waiting for transfers between devices: 39.6 us -> 56.4 us
  Pallas kernels: 51.3 us -> 46 us
    ppermute x4, waiting for transfers between devices: 21.9 us -> 40.5 us  [swap(): return lax.ppermute(x, 'section', [(0, 1), (1, 0)])]
    ppermute x4, starting transfers between devices: 14.1 us -> 4.57 us  [swap(): return lax.ppermute(x, 'section', [(0, 1), (1, 0)])]
    ppermute x5, starting transfers between devices: 13.2 us -> 4.61 us  [near_swap(): lax.ppermute(x, 'ctx', [(i, i ^ 1) for i in range(lax.axis_size('ctx'))])]
    pallas_call x3, Pallas kernels: 11.6 us -> 9.58 us  [combine(): pl.pallas_call(functools.partial(combine_kernel, h0, hc, relayed, extra,...]
    pallas_call x3, Pallas kernels: 30.4 us -> 28.4 us  [attn_chunk(): pl.pallas_call(attn_kernel, grid_spec=pltpu.PrefetchScalarGridSpec(num_sc...]
    ppermute x6, waiting for transfers between devices: 17.7 us -> 15.8 us  [far_swap(): return lax.ppermute(x, 'ctx', pairs)]
  transfers between devices with their start and end apart: 16 -> 16, of which waited for: 6 -> 7; matrix products, arithmetic and copies ran while one was open for 1% -> 1% of each run, Pallas kernels for 39% -> 37%
where the time goes in v4:
time: 120 us; the launch traced here: 119 us
  waiting for transfers between devices  56.4 us (47%)
  Pallas kernels  46 us (38%)
  starting transfers between devices  14.3 us (12%)
    ppermute x4, waiting for transfers between devices, swap(): return lax.ppermute(x, 'section', [(0, 1), (1, 0)])  40.5 us
    pallas_call x3, Pallas kernels, attn_chunk(): pl.pallas_call(attn_kernel, grid_spec=pltpu.PrefetchScalarGridSpec(num_sc...  28.4 us
    ppermute x6, waiting for transfers between devices, far_swap(): return lax.ppermute(x, 'ctx', pairs)  15.8 us
    pallas_call x3, Pallas kernels, combine(): pl.pallas_call(functools.partial(combine_kernel, h0, hc, relayed, extra,...  9.58 us
    ppermute x5, starting transfers between devices, near_swap(): lax.ppermute(x, 'ctx', [(i, i ^ 1) for i in range(lax.axis_size('ctx'))])  4.61 us
    ppermute x4, starting transfers between devices, swap(): return lax.ppermute(x, 'section', [(0, 1), (1, 0)])  4.57 us
    pallas_call x2, Pallas kernels, pack(): pl.pallas_call(functools.partial(pack_kernel, spans), grid=(1,), in_specs...  4.22 us
    pallas_call x2, Pallas kernels, place(): pl.pallas_call(functools.partial(place_kernel, moves), grid_spec=pltpu.Pr...  3.76 us
  transfers between devices with their start and end apart: 16, of which 7 were waited for; matrix products, arithmetic and copies ran while one was open for 1% of the time, Pallas kernels for 37%

profile of v4, /device:TPU:225, one launch (start us, length us, event | category | flops | bytes accessed | tf_op | source)
XLA Modules:
  0.0 118.5 jit_solution(6529640121388621110)
XLA Ops:
  0.6 0.8 collective-permute-start
  1.4 0.1 collective-permute-start.1
  1.5 1.9 %pack.2 = bf16[2,256,768]{2,1,0:T(8,128)(2,1)} custom-call(bf16[256,2560]{1,0:T(8,128)(2,1)} %k_ref.8, bf16[256,2560]{1,0:T(8,128)(2,1)} %v_ref.9), custom_call_target="tpu_custom_call" | custom-call | flops 1000 | bytes 1000 | tf_op jit(solution)/shard_map/pack/pallas_call | solution.py:286
  3.4 1.7 %collective-permute-start.2 = (bf16[2,256,768]{2,1,0:T(8,128)(2,1)}, bf16[2,256,768]{2,1,0:T(8,128)(2,1)}, u32[]{:S(2)}, u32[]{:S(2)}) collective-permute-start(bf16[2,256,768]{2,1,0:T(8,128)(2,1)} %pack.2), channel_id=1, source_target_pairs={{0,254},{2,4},{4,2},{6,8},{8,6},{10,12},{12,10},{14,16},{16,14},{1... | collective-permute-start | bytes 2359304 | tf_op jit(solution)/shard_map/ppermute | solution.py:317
  5.1 2.3 %pack.3 = (bf16[2,256,896]{2,1,0:T(8,128)(2,1)}, bf16[2,256,896]{2,1,0:T(8,128)(2,1)}) custom-call(bf16[256,2560]{1,0:T(8,128)(2,1)} %k_ref.8, bf16[256,2560]{1,0:T(8,128)(2,1)} %v_ref.9), custom_call_target="tpu_custom_call" | custom-call | flops 1000 | bytes 1000 | tf_op jit(solution)/shard_map/pack/pallas_call | solution.py:286
  7.4 0.9 collective-permute-start.3
  8.6 0.1 pad.3.clone
  8.7 0.9 collective-permute-start.6
  9.6 0.7 maximum_maximum_fusion.bias_ref
  10.2 5.3 %collective-permute-done.2.far_ref = bf16[2,256,768]{2,1,0:T(8,128)(2,1)} collective-permute-done((bf16[2,256,768]{2,1,0:T(8,128)(2,1)}, bf16[2,256,768]{2,1,0:T(8,128)(2,1)}, u32[]{:S(2)}, u32[]{:S(2)}) %collective-permute-start.2) | collective-permute-done | bytes 786464 | tf_op jit(solution)/shard_map/ppermute | solution.py:317
  15.5 8.6 %attn.3 = (bf16[128,5120]{1,0:T(8,128)(2,1)}, bf16[128,768]{1,0:T(8,128)(2,1)}, bf16[2,256,768]{2,1,0:T(8,128)(2,1)}, bf16[2,256,768]{2,1,0:T(8,128)(2,1)}, bf16[2,256,768]{2,1,0:T(8,128)(2,1)}) custom-call(s32[1]{0:T(128)} %bitcast.side_ref, bf16[256,2560]{1,0:T(8,128)(2,1)} %q_ref.5, bf16[256,2560]{1,0:T(8,128)(2,1)} %do_ref.5, bf16[256,2560]{1,0:T(8,128)(2,1)} %k_ref.8, ...), custom_call_target="tpu_custom_call" | custom-call | flops 1000 | bytes 1000 | tf_op jit(solution)/shard_map/attn/pallas_call | solution.py:98
  24.1 1.2 %collective-permute-done.3.far_ref = bf16[2,256,896]{2,1,0:T(8,128)(2,1)} collective-permute-done((bf16[2,256,896]{2,1,0:T(8,128)(2,1)}, bf16[2,256,896]{2,1,0:T(8,128)(2,1)}, u32[]{:S(2)}, u32[]{:S(2)}) %collective-permute-start.3) | collective-permute-done | bytes 917536 | tf_op jit(solution)/shard_map/ppermute | solution.py:317
  25.3 2.2 %collective-permute-start.5 = (bf16[2,256,768]{2,1,0:T(8,128)(2,1)}, bf16[2,256,768]{2,1,0:T(8,128)(2,1)}, u32[]{:S(2)}, u32[]{:S(2)}) collective-permute-start(bf16[2,256,768]{2,1,0:T(8,128)(2,1)} %get-tuple-element.81), channel_id=1, source_target_pairs={{0,2},{2,0},{4,6},{6,4},{8,10},{10,8},{12,14},{14,12},{16,18},{18,... | collective-permute-start | bytes 2359304 | tf_op jit(solution)/shard_map/ppermute | solution.py:301
  27.6 2.7 %collective-permute-start.4 = (bf16[128,768]{1,0:T(8,128)(2,1)}, bf16[128,768]{1,0:T(8,128)(2,1)}, u32[]{:S(2)}, u32[]{:S(2)}) collective-permute-start(bf16[128,768]{1,0:T(8,128)(2,1)} %get-tuple-element.80), channel_id=1, source_target_pairs={{0,1},{1,0},{2,3},{3,2},{4,5},{5,4},{6,7},{7,6},{8,9},{9,8},{10,11... | collective-permute-start | bytes 589832 | tf_op jit(solution)/shard_map/ppermute | solution.py:326
  30.3 9.9 %attn.4 = (bf16[128,5120]{1,0:T(8,128)(2,1)}, bf16[128,896]{1,0:T(8,128)(2,1)}, bf16[2,256,896]{2,1,0:T(8,128)(2,1)}, bf16[2,256,896]{2,1,0:T(8,128)(2,1)}, bf16[2,256,896]{2,1,0:T(8,128)(2,1)}) custom-call(s32[1]{0:T(128)} %bitcast.side_ref, bf16[256,2560]{1,0:T(8,128)(2,1)} %q_ref.5, bf16[256,2560]{1,0:T(8,128)(2,1)} %do_ref.5, ...), custom_call_target="tpu_custom_call", output_to_operand_aliasing={{0}: (9, {})} | custom-call | flops 1000 | bytes 1000 | tf_op jit(solution)/shard_map/attn/pallas_call | solution.py:98
  40.2 14.3 %collective-permute-done.4.refs_5_ = bf16[128,768]{1,0:T(8,128)(2,1)} collective-permute-done((bf16[128,768]{1,0:T(8,128)(2,1)}, bf16[128,768]{1,0:T(8,128)(2,1)}, u32[]{:S(2)}, u32[]{:S(2)}) %collective-permute-start.4) | collective-permute-done | bytes 196640 | tf_op jit(solution)/shard_map/ppermute | solution.py:326
  54.5 0.6 collective-permute-start.9
  55.1 2.8 %combine.3 = (bf16[128,5120]{1,0:T(8,128)(2,1)}, bf16[128,5120]{1,0:T(8,128)(2,1)}, bf16[384,896]{1,0:T(8,128)(2,1)}, bf16[128,5120]{1,0:T(8,128)(2,1)}) custom-call(s32[1]{0:T(128)} %bitcast.side_ref, s32[1]{0:T(128)} %bitcast.1.corner_ref, bf16[2,256,768]{2,1,0:T(8,128)(2,1)} %get-tuple-element.87.refs_0_, ...), custom_call_target="tpu_custom_call", output_to_operand_aliasing={{3}: (6, {})} | custom-call | flops 1000 | bytes 1000 | tf_op jit(solution)/shard_map/combine/pallas_call | solution.py:204
  57.9 0.6 collective-permute-start.10
  58.5 9.9 %attn.5 = (bf16[128,5120]{1,0:T(8,128)(2,1)}, bf16[128,896]{1,0:T(8,128)(2,1)}, bf16[2,256,896]{2,1,0:T(8,128)(2,1)}, bf16[2,256,896]{2,1,0:T(8,128)(2,1)}, bf16[2,256,896]{2,1,0:T(8,128)(2,1)}) custom-call(s32[1]{0:T(128)} %bitcast.side_ref, bf16[256,2560]{1,0:T(8,128)(2,1)} %q_ref.5, bf16[256,2560]{1,0:T(8,128)(2,1)} %do_ref.5, ...), custom_call_target="tpu_custom_call", output_to_operand_aliasing={{0}: (9, {})} | custom-call | flops 1000 | bytes 1000 | tf_op jit(solution)/shard_map/attn/pallas_call | solution.py:98
  68.4 8.3 %collective-permute-done.10.refs_3_ = bf16[384,896]{1,0:T(8,128)(2,1)} collective-permute-done((bf16[384,896]{1,0:T(8,128)(2,1)}, bf16[384,896]{1,0:T(8,128)(2,1)}, u32[]{:S(2)}, u32[]{:S(2)}) %collective-permute-start.10) | collective-permute-done | bytes 688160 | tf_op jit(solution)/shard_map/ppermute | solution.py:326
  76.7 1.6 %collective-permute-start.13 = (bf16[2,256,896]{2,1,0:T(8,128)(2,1)}, bf16[2,256,896]{2,1,0:T(8,128)(2,1)}, u32[]{:S(2)}, u32[]{:S(2)}) collective-permute-start(bf16[2,256,896]{2,1,0:T(8,128)(2,1)} %collective-permute-done.7.refs_2_), channel_id=1, source_target_pairs={{0,128},{126,254},{128,0},{254,126},{1,129},{127,255},{129,1},{255... | collective-permute-start | bytes 2752520 | tf_op jit(solution)/shard_map/ppermute | solution.py:322
  78.3 0.9 collective-permute-start.11
  79.3 3.5 %combine.4 = (bf16[128,5120]{1,0:T(8,128)(2,1)}, bf16[128,5120]{1,0:T(8,128)(2,1)}, bf16[384,896]{1,0:T(8,128)(2,1)}, bf16[128,5120]{1,0:T(8,128)(2,1)}) custom-call(s32[1]{0:T(128)} %bitcast.side_ref, s32[1]{0:T(128)} %bitcast.1.corner_ref, ...), custom_call_target="tpu_custom_call", output_to_operand_aliasing={{3}: (8, {}), {0}: (9, {}), {1}: (10, {})} | custom-call | flops 1000 | bytes 1000 | tf_op jit(solution)/shard_map/combine/pallas_call | solution.py:204
  82.8 0.6 collective-permute-start.15
  83.4 9.3 %collective-permute-done.12.refs_2_ = bf16[2,256,896]{2,1,0:T(8,128)(2,1)} collective-permute-done((bf16[2,256,896]{2,1,0:T(8,128)(2,1)}, bf16[2,256,896]{2,1,0:T(8,128)(2,1)}, u32[]{:S(2)}, u32[]{:S(2)}) %collective-permute-start.12) | collective-permute-done | bytes 917536 | tf_op jit(solution)/shard_map/ppermute | solution.py:317
  92.7 3.3 %combine.5 = (bf16[128,5120]{1,0:T(8,128)(2,1)}, bf16[128,5120]{1,0:T(8,128)(2,1)}, bf16[256,896]{1,0:T(8,128)(2,1)}, bf16[128,5120]{1,0:T(8,128)(2,1)}) custom-call(s32[1]{0:T(128)} %bitcast.side_ref, s32[1]{0:T(128)} %bitcast.1.corner_ref, ...), custom_call_target="tpu_custom_call", output_to_operand_aliasing={{3}: (6, {}), {0}: (7, {}), {1}: (8, {})} | custom-call | flops 1000 | bytes 1000 | tf_op jit(solution)/shard_map/combine/pallas_call | solution.py:204
  96.0 0.6 collective-permute-start.14
  96.6 10.1 %collective-permute-done.15.refs_0_ = bf16[384,896]{1,0:T(8,128)(2,1)} collective-permute-done((bf16[384,896]{1,0:T(8,128)(2,1)}, bf16[384,896]{1,0:T(8,128)(2,1)}, u32[]{:S(2)}, u32[]{:S(2)}) %collective-permute-start.15) | collective-permute-done | bytes 688160 | tf_op jit(solution)/shard_map/ppermute | solution.py:326
  106.7 2.0 %place.2 = (bf16[128,5120]{1,0:T(8,128)(2,1)}, bf16[128,5120]{1,0:T(8,128)(2,1)}, bf16[128,5120]{1,0:T(8,128)(2,1)}) custom-call(s32[1]{0:T(128)} %bitcast.side_ref, bf16[384,896]{1,0:T(8,128)(2,1)} %collective-permute-done.15.refs_0_, bf16[128,5120]{1,0:T(8,128)(2,1)} %get-tuple-element.119.refs_1_, ...), custom_call_target="tpu_custom_call", output_to_operand_aliasing={{0}: (2, {}), {1}: (3, {}), {2}: (4, {})} | custom-call | flops 1000 | bytes 1000 | tf_op jit(solution)/shard_map/place/pallas_call | solution.py:246
  108.7 7.9 %collective-permute-done.14.refs_0_ = bf16[256,896]{1,0:T(8,128)(2,1)} collective-permute-done((bf16[256,896]{1,0:T(8,128)(2,1)}, bf16[256,896]{1,0:T(8,128)(2,1)}, u32[]{:S(2)}, u32[]{:S(2)}) %collective-permute-start.14) | collective-permute-done | bytes 458784 | tf_op jit(solution)/shard_map/ppermute | solution.py:326
  116.5 1.8 %place.3 = (bf16[128,5120]{1,0:T(8,128)(2,1)}, bf16[128,5120]{1,0:T(8,128)(2,1)}, bf16[128,5120]{1,0:T(8,128)(2,1)}) custom-call(s32[1]{0:T(128)} %bitcast.side_ref, bf16[256,896]{1,0:T(8,128)(2,1)} %collective-permute-done.14.refs_0_, bf16[128,5120]{1,0:T(8,128)(2,1)} %get-tuple-element.122.refs_1_, ...), custom_call_target="tpu_custom_call", output_to_operand_aliasing={{0}: (2, {}), {1}: (3, {}), {2}: (4, {})} | custom-call | flops 1000 | bytes 1000 | tf_op jit(solution)/shard_map/place/pallas_call | solution.py:246
  (22 shorter events, 0.3 us)
Async XLA Ops:
  0.6 4.5 %collective-permute-start = (bf16[256,2560]{1,0:T(8,128)(2,1)}, bf16[256,2560]{1,0:T(8,128)(2,1)}, u32[]{:S(2)}, u32[]{:S(2)}) collective-permute-start(bf16[256,2560]{1,0:T(8,128)(2,1)} %k_ref.8), channel_id=1, source_target_pairs={{0,2},{2,0},{4,6},{6,4},{8,10},{10,8},{12,14},{14,12},{16,18},{18,... | collective-permute-start | bytes 3932168 | tf_op jit(solution)/shard_map/ppermute | solution.py:301
  1.4 14.1 %collective-permute-start.1 = (bf16[256,2560]{1,0:T(8,128)(2,1)}, bf16[256,2560]{1,0:T(8,128)(2,1)}, u32[]{:S(2)}, u32[]{:S(2)}) collective-permute-start(bf16[256,2560]{1,0:T(8,128)(2,1)} %v_ref.9), channel_id=1, source_target_pairs={{0,2},{2,0},{4,6},{6,4},{8,10},{10,8},{12,14},{14,12},{16,18},{18,... | collective-permute-start | bytes 3932168 | tf_op jit(solution)/shard_map/ppermute | solution.py:301
  3.4 12.1 %collective-permute-start.2 = (bf16[2,256,768]{2,1,0:T(8,128)(2,1)}, bf16[2,256,768]{2,1,0:T(8,128)(2,1)}, u32[]{:S(2)}, u32[]{:S(2)}) collective-permute-start(bf16[2,256,768]{2,1,0:T(8,128)(2,1)} %pack.2), channel_id=1, source_target_pairs={{0,254},{2,4},{4,2},{6,8},{8,6},{10,12},{12,10},{14,16},{16,14},{1... | collective-permute-start | bytes 2359304 | tf_op jit(solution)/shard_map/ppermute | solution.py:317
  5.1 3.3 %copy-start = (s32[256,6]{0,1:T(8,128)S(1)}, s32[256,6]{0,1:T(8,128)}, u32[]{:S(2)}) copy-start(s32[256,6]{0,1:T(8,128)} %param.9) | copy-start | bytes 18436
  7.4 17.9 %collective-permute-start.3 = (bf16[2,256,896]{2,1,0:T(8,128)(2,1)}, bf16[2,256,896]{2,1,0:T(8,128)(2,1)}, u32[]{:S(2)}, u32[]{:S(2)}) collective-permute-start(bf16[2,256,896]{2,1,0:T(8,128)(2,1)} %get-tuple-element.66), channel_id=1, source_target_pairs={{0,254},{2,4},{4,2},{6,8},{8,6},{10,12},{12,10},{14,16},{16,14},{1... | collective-permute-start | bytes 2752520 | tf_op jit(solution)/shard_map/ppermute | solution.py:317
  8.7 45.8 %collective-permute-start.6 = (bf16[2,256,896]{2,1,0:T(8,128)(2,1)}, bf16[2,256,896]{2,1,0:T(8,128)(2,1)}, u32[]{:S(2)}, u32[]{:S(2)}) collective-permute-start(bf16[2,256,896]{2,1,0:T(8,128)(2,1)} %get-tuple-element.67), channel_id=1, source_target_pairs={{0,254},{2,4},{4,2},{6,8},{8,6},{10,12},{12,10},{14,16},{16,14},{1... | collective-permute-start | bytes 2752520 | tf_op jit(solution)/shard_map/ppermute | solution.py:317
  25.3 29.1 %collective-permute-start.5 = (bf16[2,256,768]{2,1,0:T(8,128)(2,1)}, bf16[2,256,768]{2,1,0:T(8,128)(2,1)}, u32[]{:S(2)}, u32[]{:S(2)}) collective-permute-start(bf16[2,256,768]{2,1,0:T(8,128)(2,1)} %get-tuple-element.81), channel_id=1, source_target_pairs={{0,2},{2,0},{4,6},{6,4},{8,10},{10,8},{12,14},{14,12},{16,18},{18,... | collective-permute-start | bytes 2359304 | tf_op jit(solution)/shard_map/ppermute | solution.py:301
  27.6 26.9 %collective-permute-start.8 = (bf16[2,256,768]{2,1,0:T(8,128)(2,1)}, bf16[2,256,768]{2,1,0:T(8,128)(2,1)}, u32[]{:S(2)}, u32[]{:S(2)}) collective-permute-start(bf16[2,256,768]{2,1,0:T(8,128)(2,1)} %get-tuple-element.85), channel_id=1, source_target_pairs={{0,254},{2,4},{4,2},{6,8},{8,6},{10,12},{12,10},{14,16},{16,14},{1... | collective-permute-start | bytes 2359304 | tf_op jit(solution)/shard_map/ppermute | solution.py:317
  27.6 26.9 %collective-permute-start.4 = (bf16[128,768]{1,0:T(8,128)(2,1)}, bf16[128,768]{1,0:T(8,128)(2,1)}, u32[]{:S(2)}, u32[]{:S(2)}) collective-permute-start(bf16[128,768]{1,0:T(8,128)(2,1)} %get-tuple-element.80), channel_id=1, source_target_pairs={{0,1},{1,0},{2,3},{3,2},{4,5},{5,4},{6,7},{7,6},{8,9},{9,8},{10,11... | collective-permute-start | bytes 589832 | tf_op jit(solution)/shard_map/ppermute | solution.py:326
  54.5 22.2 %collective-permute-start.9 = (bf16[2,256,896]{2,1,0:T(8,128)(2,1)}, bf16[2,256,896]{2,1,0:T(8,128)(2,1)}, u32[]{:S(2)}, u32[]{:S(2)}) collective-permute-start(bf16[2,256,896]{2,1,0:T(8,128)(2,1)} %get-tuple-element.99), channel_id=1, source_target_pairs={{0,2},{2,0},{4,6},{6,4},{8,10},{10,8},{12,14},{14,12},{16,18},{18,... | collective-permute-start | bytes 2752520 | tf_op jit(solution)/shard_map/ppermute | solution.py:301
  55.1 21.6 %collective-permute-start.7 = (bf16[2,256,896]{2,1,0:T(8,128)(2,1)}, bf16[2,256,896]{2,1,0:T(8,128)(2,1)}, u32[]{:S(2)}, u32[]{:S(2)}) collective-permute-start(bf16[2,256,896]{2,1,0:T(8,128)(2,1)} %get-tuple-element.82), channel_id=1, source_target_pairs={{0,126},{2,4},{4,2},{6,8},{8,6},{10,12},{12,10},{14,16},{16,14},{1... | collective-permute-start | bytes 2752520 | tf_op jit(solution)/shard_map/ppermute | solution.py:317
  57.9 18.8 %collective-permute-start.10 = (bf16[384,896]{1,0:T(8,128)(2,1)}, bf16[384,896]{1,0:T(8,128)(2,1)}, u32[]{:S(2)}, u32[]{:S(2)}) collective-permute-start(bf16[384,896]{1,0:T(8,128)(2,1)} %get-tuple-element.100), channel_id=1, source_target_pairs={{0,1},{1,0},{2,3},{3,2},{4,5},{5,4},{6,7},{7,6},{8,9},{9,8},{10,11... | collective-permute-start | bytes 2064392 | tf_op jit(solution)/shard_map/ppermute | solution.py:326
  76.7 2.6 %collective-permute-start.13 = (bf16[2,256,896]{2,1,0:T(8,128)(2,1)}, bf16[2,256,896]{2,1,0:T(8,128)(2,1)}, u32[]{:S(2)}, u32[]{:S(2)}) collective-permute-start(bf16[2,256,896]{2,1,0:T(8,128)(2,1)} %collective-permute-done.7.refs_2_), channel_id=1, source_target_pairs={{0,128},{126,254},{128,0},{254,126},{1,129},{127,255},{129,1},{255... | collective-permute-start | bytes 2752520 | tf_op jit(solution)/shard_map/ppermute | solution.py:322
  78.3 5.1 %collective-permute-start.11 = (bf16[2,256,896]{2,1,0:T(8,128)(2,1)}, bf16[2,256,896]{2,1,0:T(8,128)(2,1)}, u32[]{:S(2)}, u32[]{:S(2)}) collective-permute-start(bf16[2,256,896]{2,1,0:T(8,128)(2,1)} %get-tuple-element.103), channel_id=1, source_target_pairs={{0,2},{2,0},{4,6},{6,4},{8,10},{10,8},{12,14},{14,12},{16,18},{18,... | collective-permute-start | bytes 2752520 | tf_op jit(solution)/shard_map/ppermute | solution.py:301
  79.3 13.4 %collective-permute-start.12 = (bf16[2,256,896]{2,1,0:T(8,128)(2,1)}, bf16[2,256,896]{2,1,0:T(8,128)(2,1)}, u32[]{:S(2)}, u32[]{:S(2)}) collective-permute-start(bf16[2,256,896]{2,1,0:T(8,128)(2,1)} %get-tuple-element.104), channel_id=1, source_target_pairs={{0,254},{2,4},{4,2},{6,8},{8,6},{10,12},{12,10},{14,16},{16,14},{1... | collective-permute-start | bytes 2752520 | tf_op jit(solution)/shard_map/ppermute | solution.py:317
  82.8 24.0 %collective-permute-start.15 = (bf16[384,896]{1,0:T(8,128)(2,1)}, bf16[384,896]{1,0:T(8,128)(2,1)}, u32[]{:S(2)}, u32[]{:S(2)}) collective-permute-start(bf16[384,896]{1,0:T(8,128)(2,1)} %get-tuple-element.118), channel_id=1, source_target_pairs={{0,1},{1,0},{2,3},{3,2},{4,5},{5,4},{6,7},{7,6},{8,9},{9,8},{10,11... | collective-permute-start | bytes 2064392 | tf_op jit(solution)/shard_map/ppermute | solution.py:326
  96.0 20.6 %collective-permute-start.14 = (bf16[256,896]{1,0:T(8,128)(2,1)}, bf16[256,896]{1,0:T(8,128)(2,1)}, u32[]{:S(2)}, u32[]{:S(2)}) collective-permute-start(bf16[256,896]{1,0:T(8,128)(2,1)} %get-tuple-element.117), channel_id=1, source_target_pairs={{0,1},{1,0},{2,3},{3,2},{4,5},{5,4},{6,7},{7,6},{8,9},{9,8},{10,11... | collective-permute-start | bytes 1376264 | tf_op jit(solution)/shard_map/ppermute | solution.py:326

commit v5 on v4

--- a/solution.py
+++ b/solution.py
@@ -398,8 +398,6 @@
             out_q, h0, hc,
         )
         arrived = [(from_near, n - 1)] if n >= 1 else []
-        if n >= 2:
-            arrived.append((kv_parts, n - 2))
         if n >= 1 and n + 1 < count:
             arrived.append((fars, n + 1))
         values = (send_q, own, near_part, far_part)
@@ -408,6 +406,8 @@
         else:
             values = after(arrived, *values)
         send_q, own, near_part, far_part = values
+        if n >= 2:
+            (near_part,) = after([(kv_parts, n - 2)], near_part)
         from_far.append(far_swap(far_part, n in RELAYED))
         if n == 0:
             first_q = swap(send_q)

time: 120 us -> 119 us (level)
  transfers between devices with their start and end apart: 16 -> 16, of which waited for: 7 -> 8; matrix products, arithmetic and copies ran while one was open for 1% -> 1% of each run, Pallas kernels for 37% -> 38%
where the time goes in v5:
time: 119 us; the launch traced here: 118 us
  waiting for transfers between devices  55.6 us (47%)
  Pallas kernels  46 us (39%)
  starting transfers between devices  14.3 us (12%)
    ppermute x4, waiting for transfers between devices, swap(): return lax.ppermute(x, 'section', [(0, 1), (1, 0)])  39.7 us
    pallas_call x3, Pallas kernels, attn_chunk(): pl.pallas_call(attn_kernel, grid_spec=pltpu.PrefetchScalarGridSpec(num_sc...  28.4 us
    ppermute x6, waiting for transfers between devices, far_swap(): return lax.ppermute(x, 'ctx', pairs)  15.9 us
    pallas_call x3, Pallas kernels, combine(): pl.pallas_call(functools.partial(combine_kernel, h0, hc, relayed, extra,...  9.58 us
    ppermute x5, starting transfers between devices, near_swap(): lax.ppermute(x, 'ctx', [(i, i ^ 1) for i in range(lax.axis_size('ctx'))])  4.61 us
    ppermute x4, starting transfers between devices, swap(): return lax.ppermute(x, 'section', [(0, 1), (1, 0)])  4.57 us
    pallas_call x2, Pallas kernels, pack(): pl.pallas_call(functools.partial(pack_kernel, spans), grid=(1,), in_specs...  4.22 us
    pallas_call x2, Pallas kernels, place(): pl.pallas_call(functools.partial(place_kernel, moves), grid_spec=pltpu.Pr...  3.76 us
  transfers between devices with their start and end apart: 16, of which 8 were waited for; matrix products, arithmetic and copies ran while one was open for 1% of the time, Pallas kernels for 38%

profile of v5, /device:TPU:225, one launch (start us, length us, event | category | flops | bytes accessed | tf_op | source)
XLA Modules:
  0.0 117.7 jit_solution(18308882805714886930)
XLA Ops:
  0.6 0.8 collective-permute-start
  1.4 0.1 collective-permute-start.1
  1.5 1.9 %pack.2 = bf16[2,256,768]{2,1,0:T(8,128)(2,1)} custom-call(bf16[256,2560]{1,0:T(8,128)(2,1)} %k_ref.8, bf16[256,2560]{1,0:T(8,128)(2,1)} %v_ref.9), custom_call_target="tpu_custom_call" | custom-call | flops 1000 | bytes 1000 | tf_op jit(solution)/shard_map/pack/pallas_call | solution.py:286
  3.4 1.7 %collective-permute-start.2 = (bf16[2,256,768]{2,1,0:T(8,128)(2,1)}, bf16[2,256,768]{2,1,0:T(8,128)(2,1)}, u32[]{:S(2)}, u32[]{:S(2)}) collective-permute-start(bf16[2,256,768]{2,1,0:T(8,128)(2,1)} %pack.2), channel_id=1, source_target_pairs={{0,254},{2,4},{4,2},{6,8},{8,6},{10,12},{12,10},{14,16},{16,14},{1... | collective-permute-start | bytes 2359304 | tf_op jit(solution)/shard_map/ppermute | solution.py:317
  5.1 2.3 %pack.3 = (bf16[2,256,896]{2,1,0:T(8,128)(2,1)}, bf16[2,256,896]{2,1,0:T(8,128)(2,1)}) custom-call(bf16[256,2560]{1,0:T(8,128)(2,1)} %k_ref.8, bf16[256,2560]{1,0:T(8,128)(2,1)} %v_ref.9), custom_call_target="tpu_custom_call" | custom-call | flops 1000 | bytes 1000 | tf_op jit(solution)/shard_map/pack/pallas_call | solution.py:286
  7.4 0.9 collective-permute-start.3
  8.7 0.9 collective-permute-start.6
  9.6 0.7 maximum_maximum_fusion.bias_ref
  10.2 5.3 %collective-permute-done.2.far_ref = bf16[2,256,768]{2,1,0:T(8,128)(2,1)} collective-permute-done((bf16[2,256,768]{2,1,0:T(8,128)(2,1)}, bf16[2,256,768]{2,1,0:T(8,128)(2,1)}, u32[]{:S(2)}, u32[]{:S(2)}) %collective-permute-start.2) | collective-permute-done | bytes 786464 | tf_op jit(solution)/shard_map/ppermute | solution.py:317
  15.5 8.6 %attn.3 = (bf16[128,5120]{1,0:T(8,128)(2,1)}, bf16[128,768]{1,0:T(8,128)(2,1)}, bf16[2,256,768]{2,1,0:T(8,128)(2,1)}, bf16[2,256,768]{2,1,0:T(8,128)(2,1)}, bf16[2,256,768]{2,1,0:T(8,128)(2,1)}) custom-call(s32[1]{0:T(128)} %bitcast.side_ref, bf16[256,2560]{1,0:T(8,128)(2,1)} %q_ref.5, bf16[256,2560]{1,0:T(8,128)(2,1)} %do_ref.5, bf16[256,2560]{1,0:T(8,128)(2,1)} %k_ref.8, ...), custom_call_target="tpu_custom_call" | custom-call | flops 1000 | bytes 1000 | tf_op jit(solution)/shard_map/attn/pallas_call | solution.py:98
  24.1 1.2 %collective-permute-done.3.far_ref = bf16[2,256,896]{2,1,0:T(8,128)(2,1)} collective-permute-done((bf16[2,256,896]{2,1,0:T(8,128)(2,1)}, bf16[2,256,896]{2,1,0:T(8,128)(2,1)}, u32[]{:S(2)}, u32[]{:S(2)}) %collective-permute-start.3) | collective-permute-done | bytes 917536 | tf_op jit(solution)/shard_map/ppermute | solution.py:317
  25.3 2.2 %collective-permute-start.5 = (bf16[2,256,768]{2,1,0:T(8,128)(2,1)}, bf16[2,256,768]{2,1,0:T(8,128)(2,1)}, u32[]{:S(2)}, u32[]{:S(2)}) collective-permute-start(bf16[2,256,768]{2,1,0:T(8,128)(2,1)} %get-tuple-element.82), channel_id=1, source_target_pairs={{0,2},{2,0},{4,6},{6,4},{8,10},{10,8},{12,14},{14,12},{16,18},{18,... | collective-permute-start | bytes 2359304 | tf_op jit(solution)/shard_map/ppermute | solution.py:301
  27.6 2.7 %collective-permute-start.4 = (bf16[128,768]{1,0:T(8,128)(2,1)}, bf16[128,768]{1,0:T(8,128)(2,1)}, u32[]{:S(2)}, u32[]{:S(2)}) collective-permute-start(bf16[128,768]{1,0:T(8,128)(2,1)} %get-tuple-element.81), channel_id=1, source_target_pairs={{0,1},{1,0},{2,3},{3,2},{4,5},{5,4},{6,7},{7,6},{8,9},{9,8},{10,11... | collective-permute-start | bytes 589832 | tf_op jit(solution)/shard_map/ppermute | solution.py:326
  30.3 9.9 %attn.4 = (bf16[128,5120]{1,0:T(8,128)(2,1)}, bf16[128,896]{1,0:T(8,128)(2,1)}, bf16[2,256,896]{2,1,0:T(8,128)(2,1)}, bf16[2,256,896]{2,1,0:T(8,128)(2,1)}, bf16[2,256,896]{2,1,0:T(8,128)(2,1)}) custom-call(s32[1]{0:T(128)} %bitcast.side_ref, bf16[256,2560]{1,0:T(8,128)(2,1)} %q_ref.5, bf16[256,2560]{1,0:T(8,128)(2,1)} %do_ref.5, ...), custom_call_target="tpu_custom_call", output_to_operand_aliasing={{0}: (9, {})} | custom-call | flops 1000 | bytes 1000 | tf_op jit(solution)/shard_map/attn/pallas_call | solution.py:98
  40.2 14.3 %collective-permute-done.4.refs_5_ = bf16[128,768]{1,0:T(8,128)(2,1)} collective-permute-done((bf16[128,768]{1,0:T(8,128)(2,1)}, bf16[128,768]{1,0:T(8,128)(2,1)}, u32[]{:S(2)}, u32[]{:S(2)}) %collective-permute-start.4) | collective-permute-done | bytes 196640 | tf_op jit(solution)/shard_map/ppermute | solution.py:326
  54.5 0.6 collective-permute-start.9
  55.1 2.8 %combine.3 = (bf16[128,5120]{1,0:T(8,128)(2,1)}, bf16[128,5120]{1,0:T(8,128)(2,1)}, bf16[384,896]{1,0:T(8,128)(2,1)}, bf16[128,5120]{1,0:T(8,128)(2,1)}) custom-call(s32[1]{0:T(128)} %bitcast.side_ref, s32[1]{0:T(128)} %bitcast.1.corner_ref, bf16[2,256,768]{2,1,0:T(8,128)(2,1)} %get-tuple-element.88.refs_0_, ...), custom_call_target="tpu_custom_call", output_to_operand_aliasing={{3}: (6, {})} | custom-call | flops 1000 | bytes 1000 | tf_op jit(solution)/shard_map/combine/pallas_call | solution.py:204
  57.9 0.6 collective-permute-start.10
  58.5 9.9 %attn.5 = (bf16[128,5120]{1,0:T(8,128)(2,1)}, bf16[128,896]{1,0:T(8,128)(2,1)}, bf16[2,256,896]{2,1,0:T(8,128)(2,1)}, bf16[2,256,896]{2,1,0:T(8,128)(2,1)}, bf16[2,256,896]{2,1,0:T(8,128)(2,1)}) custom-call(s32[1]{0:T(128)} %bitcast.side_ref, bf16[256,2560]{1,0:T(8,128)(2,1)} %q_ref.5, bf16[256,2560]{1,0:T(8,128)(2,1)} %do_ref.5, ...), custom_call_target="tpu_custom_call", output_to_operand_aliasing={{0}: (9, {})} | custom-call | flops 1000 | bytes 1000 | tf_op jit(solution)/shard_map/attn/pallas_call | solution.py:98
  68.4 0.1 collective-permute-done.7.refs_2_
  68.5 1.6 %collective-permute-start.13 = (bf16[2,256,896]{2,1,0:T(8,128)(2,1)}, bf16[2,256,896]{2,1,0:T(8,128)(2,1)}, u32[]{:S(2)}, u32[]{:S(2)}) collective-permute-start(bf16[2,256,896]{2,1,0:T(8,128)(2,1)} %collective-permute-done.7.refs_2_), channel_id=1, source_target_pairs={{0,128},{126,254},{128,0},{254,126},{1,129},{127,255},{129,1},{255... | collective-permute-start | bytes 2752520 | tf_op jit(solution)/shard_map/ppermute | solution.py:322
  70.1 6.6 %collective-permute-done.10.refs_3_ = bf16[384,896]{1,0:T(8,128)(2,1)} collective-permute-done((bf16[384,896]{1,0:T(8,128)(2,1)}, bf16[384,896]{1,0:T(8,128)(2,1)}, u32[]{:S(2)}, u32[]{:S(2)}) %collective-permute-start.10) | collective-permute-done | bytes 688160 | tf_op jit(solution)/shard_map/ppermute | solution.py:326
  76.7 0.9 collective-permute-start.11
  77.7 3.5 %combine.4 = (bf16[128,5120]{1,0:T(8,128)(2,1)}, bf16[128,5120]{1,0:T(8,128)(2,1)}, bf16[384,896]{1,0:T(8,128)(2,1)}, bf16[128,5120]{1,0:T(8,128)(2,1)}) custom-call(s32[1]{0:T(128)} %bitcast.side_ref, s32[1]{0:T(128)} %bitcast.1.corner_ref, ...), custom_call_target="tpu_custom_call", output_to_operand_aliasing={{3}: (8, {}), {0}: (9, {}), {1}: (10, {})} | custom-call | flops 1000 | bytes 1000 | tf_op jit(solution)/shard_map/combine/pallas_call | solution.py:204
  81.1 0.6 collective-permute-start.15
  81.8 9.3 %collective-permute-done.12.refs_2_ = bf16[2,256,896]{2,1,0:T(8,128)(2,1)} collective-permute-done((bf16[2,256,896]{2,1,0:T(8,128)(2,1)}, bf16[2,256,896]{2,1,0:T(8,128)(2,1)}, u32[]{:S(2)}, u32[]{:S(2)}) %collective-permute-start.12) | collective-permute-done | bytes 917536 | tf_op jit(solution)/shard_map/ppermute | solution.py:317
  91.1 3.3 %combine.5 = (bf16[128,5120]{1,0:T(8,128)(2,1)}, bf16[128,5120]{1,0:T(8,128)(2,1)}, bf16[256,896]{1,0:T(8,128)(2,1)}, bf16[128,5120]{1,0:T(8,128)(2,1)}) custom-call(s32[1]{0:T(128)} %bitcast.side_ref, s32[1]{0:T(128)} %bitcast.1.corner_ref, ...), custom_call_target="tpu_custom_call", output_to_operand_aliasing={{3}: (6, {}), {0}: (7, {}), {1}: (8, {})} | custom-call | flops 1000 | bytes 1000 | tf_op jit(solution)/shard_map/combine/pallas_call | solution.py:204
  94.4 0.6 collective-permute-start.14
  95.0 11.0 %collective-permute-done.15.refs_0_ = bf16[384,896]{1,0:T(8,128)(2,1)} collective-permute-done((bf16[384,896]{1,0:T(8,128)(2,1)}, bf16[384,896]{1,0:T(8,128)(2,1)}, u32[]{:S(2)}, u32[]{:S(2)}) %collective-permute-start.15) | collective-permute-done | bytes 688160 | tf_op jit(solution)/shard_map/ppermute | solution.py:326
  105.9 2.0 %place.2 = (bf16[128,5120]{1,0:T(8,128)(2,1)}, bf16[128,5120]{1,0:T(8,128)(2,1)}, bf16[128,5120]{1,0:T(8,128)(2,1)}) custom-call(s32[1]{0:T(128)} %bitcast.side_ref, bf16[384,896]{1,0:T(8,128)(2,1)} %collective-permute-done.15.refs_0_, bf16[128,5120]{1,0:T(8,128)(2,1)} %get-tuple-element.121.refs_1_, ...), custom_call_target="tpu_custom_call", output_to_operand_aliasing={{0}: (2, {}), {1}: (3, {}), {2}: (4, {})} | custom-call | flops 1000 | bytes 1000 | tf_op jit(solution)/shard_map/place/pallas_call | solution.py:246
  107.9 7.9 %collective-permute-done.14.refs_0_ = bf16[256,896]{1,0:T(8,128)(2,1)} collective-permute-done((bf16[256,896]{1,0:T(8,128)(2,1)}, bf16[256,896]{1,0:T(8,128)(2,1)}, u32[]{:S(2)}, u32[]{:S(2)}) %collective-permute-start.14) | collective-permute-done | bytes 458784 | tf_op jit(solution)/shard_map/ppermute | solution.py:326
  115.8 1.8 %place.3 = (bf16[128,5120]{1,0:T(8,128)(2,1)}, bf16[128,5120]{1,0:T(8,128)(2,1)}, bf16[128,5120]{1,0:T(8,128)(2,1)}) custom-call(s32[1]{0:T(128)} %bitcast.side_ref, bf16[256,896]{1,0:T(8,128)(2,1)} %collective-permute-done.14.refs_0_, bf16[128,5120]{1,0:T(8,128)(2,1)} %get-tuple-element.124.refs_1_, ...), custom_call_target="tpu_custom_call", output_to_operand_aliasing={{0}: (2, {}), {1}: (3, {}), {2}: (4, {})} | custom-call | flops 1000 | bytes 1000 | tf_op jit(solution)/shard_map/place/pallas_call | solution.py:246
  (22 shorter events, 0.3 us)
Async XLA Ops:
  0.6 4.5 %collective-permute-start = (bf16[256,2560]{1,0:T(8,128)(2,1)}, bf16[256,2560]{1,0:T(8,128)(2,1)}, u32[]{:S(2)}, u32[]{:S(2)}) collective-permute-start(bf16[256,2560]{1,0:T(8,128)(2,1)} %k_ref.8), channel_id=1, source_target_pairs={{0,2},{2,0},{4,6},{6,4},{8,10},{10,8},{12,14},{14,12},{16,18},{18,... | collective-permute-start | bytes 3932168 | tf_op jit(solution)/shard_map/ppermute | solution.py:301
  1.4 14.1 %collective-permute-start.1 = (bf16[256,2560]{1,0:T(8,128)(2,1)}, bf16[256,2560]{1,0:T(8,128)(2,1)}, u32[]{:S(2)}, u32[]{:S(2)}) collective-permute-start(bf16[256,2560]{1,0:T(8,128)(2,1)} %v_ref.9), channel_id=1, source_target_pairs={{0,2},{2,0},{4,6},{6,4},{8,10},{10,8},{12,14},{14,12},{16,18},{18,... | collective-permute-start | bytes 3932168 | tf_op jit(solution)/shard_map/ppermute | solution.py:301
  3.4 12.1 %collective-permute-start.2 = (bf16[2,256,768]{2,1,0:T(8,128)(2,1)}, bf16[2,256,768]{2,1,0:T(8,128)(2,1)}, u32[]{:S(2)}, u32[]{:S(2)}) collective-permute-start(bf16[2,256,768]{2,1,0:T(8,128)(2,1)} %pack.2), channel_id=1, source_target_pairs={{0,254},{2,4},{4,2},{6,8},{8,6},{10,12},{12,10},{14,16},{16,14},{1... | collective-permute-start | bytes 2359304 | tf_op jit(solution)/shard_map/ppermute | solution.py:317
  5.1 3.3 %copy-start = (s32[256,6]{0,1:T(8,128)S(1)}, s32[256,6]{0,1:T(8,128)}, u32[]{:S(2)}) copy-start(s32[256,6]{0,1:T(8,128)} %param.9) | copy-start | bytes 18436
  7.4 17.9 %collective-permute-start.3 = (bf16[2,256,896]{2,1,0:T(8,128)(2,1)}, bf16[2,256,896]{2,1,0:T(8,128)(2,1)}, u32[]{:S(2)}, u32[]{:S(2)}) collective-permute-start(bf16[2,256,896]{2,1,0:T(8,128)(2,1)} %get-tuple-element.67), channel_id=1, source_target_pairs={{0,254},{2,4},{4,2},{6,8},{8,6},{10,12},{12,10},{14,16},{16,14},{1... | collective-permute-start | bytes 2752520 | tf_op jit(solution)/shard_map/ppermute | solution.py:317
  8.7 45.8 %collective-permute-start.6 = (bf16[2,256,896]{2,1,0:T(8,128)(2,1)}, bf16[2,256,896]{2,1,0:T(8,128)(2,1)}, u32[]{:S(2)}, u32[]{:S(2)}) collective-permute-start(bf16[2,256,896]{2,1,0:T(8,128)(2,1)} %get-tuple-element.68), channel_id=1, source_target_pairs={{0,254},{2,4},{4,2},{6,8},{8,6},{10,12},{12,10},{14,16},{16,14},{1... | collective-permute-start | bytes 2752520 | tf_op jit(solution)/shard_map/ppermute | solution.py:317
  25.3 29.1 %collective-permute-start.5 = (bf16[2,256,768]{2,1,0:T(8,128)(2,1)}, bf16[2,256,768]{2,1,0:T(8,128)(2,1)}, u32[]{:S(2)}, u32[]{:S(2)}) collective-permute-start(bf16[2,256,768]{2,1,0:T(8,128)(2,1)} %get-tuple-element.82), channel_id=1, source_target_pairs={{0,2},{2,0},{4,6},{6,4},{8,10},{10,8},{12,14},{14,12},{16,18},{18,... | collective-permute-start | bytes 2359304 | tf_op jit(solution)/shard_map/ppermute | solution.py:301
  27.6 26.9 %collective-permute-start.8 = (bf16[2,256,768]{2,1,0:T(8,128)(2,1)}, bf16[2,256,768]{2,1,0:T(8,128)(2,1)}, u32[]{:S(2)}, u32[]{:S(2)}) collective-permute-start(bf16[2,256,768]{2,1,0:T(8,128)(2,1)} %get-tuple-element.86), channel_id=1, source_target_pairs={{0,254},{2,4},{4,2},{6,8},{8,6},{10,12},{12,10},{14,16},{16,14},{1... | collective-permute-start | bytes 2359304 | tf_op jit(solution)/shard_map/ppermute | solution.py:317
  27.6 26.9 %collective-permute-start.4 = (bf16[128,768]{1,0:T(8,128)(2,1)}, bf16[128,768]{1,0:T(8,128)(2,1)}, u32[]{:S(2)}, u32[]{:S(2)}) collective-permute-start(bf16[128,768]{1,0:T(8,128)(2,1)} %get-tuple-element.81), channel_id=1, source_target_pairs={{0,1},{1,0},{2,3},{3,2},{4,5},{5,4},{6,7},{7,6},{8,9},{9,8},{10,11... | collective-permute-start | bytes 589832 | tf_op jit(solution)/shard_map/ppermute | solution.py:326
  54.5 13.9 %collective-permute-start.9 = (bf16[2,256,896]{2,1,0:T(8,128)(2,1)}, bf16[2,256,896]{2,1,0:T(8,128)(2,1)}, u32[]{:S(2)}, u32[]{:S(2)}) collective-permute-start(bf16[2,256,896]{2,1,0:T(8,128)(2,1)} %get-tuple-element.100), channel_id=1, source_target_pairs={{0,2},{2,0},{4,6},{6,4},{8,10},{10,8},{12,14},{14,12},{16,18},{18,... | collective-permute-start | bytes 2752520 | tf_op jit(solution)/shard_map/ppermute | solution.py:301
  55.1 13.4 %collective-permute-start.7 = (bf16[2,256,896]{2,1,0:T(8,128)(2,1)}, bf16[2,256,896]{2,1,0:T(8,128)(2,1)}, u32[]{:S(2)}, u32[]{:S(2)}) collective-permute-start(bf16[2,256,896]{2,1,0:T(8,128)(2,1)} %get-tuple-element.83), channel_id=1, source_target_pairs={{0,126},{2,4},{4,2},{6,8},{8,6},{10,12},{12,10},{14,16},{16,14},{1... | collective-permute-start | bytes 2752520 | tf_op jit(solution)/shard_map/ppermute | solution.py:317
  57.9 18.8 %collective-permute-start.10 = (bf16[384,896]{1,0:T(8,128)(2,1)}, bf16[384,896]{1,0:T(8,128)(2,1)}, u32[]{:S(2)}, u32[]{:S(2)}) collective-permute-start(bf16[384,896]{1,0:T(8,128)(2,1)} %get-tuple-element.104), channel_id=1, source_target_pairs={{0,1},{1,0},{2,3},{3,2},{4,5},{5,4},{6,7},{7,6},{8,9},{9,8},{10,11... | collective-permute-start | bytes 2064392 | tf_op jit(solution)/shard_map/ppermute | solution.py:326
  68.5 9.2 %collective-permute-start.13 = (bf16[2,256,896]{2,1,0:T(8,128)(2,1)}, bf16[2,256,896]{2,1,0:T(8,128)(2,1)}, u32[]{:S(2)}, u32[]{:S(2)}) collective-permute-start(bf16[2,256,896]{2,1,0:T(8,128)(2,1)} %collective-permute-done.7.refs_2_), channel_id=1, source_target_pairs={{0,128},{126,254},{128,0},{254,126},{1,129},{127,255},{129,1},{255... | collective-permute-start | bytes 2752520 | tf_op jit(solution)/shard_map/ppermute | solution.py:322
  76.7 5.1 %collective-permute-start.11 = (bf16[2,256,896]{2,1,0:T(8,128)(2,1)}, bf16[2,256,896]{2,1,0:T(8,128)(2,1)}, u32[]{:S(2)}, u32[]{:S(2)}) collective-permute-start(bf16[2,256,896]{2,1,0:T(8,128)(2,1)} %get-tuple-element.105), channel_id=1, source_target_pairs={{0,2},{2,0},{4,6},{6,4},{8,10},{10,8},{12,14},{14,12},{16,18},{18,... | collective-permute-start | bytes 2752520 | tf_op jit(solution)/shard_map/ppermute | solution.py:301
  77.6 13.4 %collective-permute-start.12 = (bf16[2,256,896]{2,1,0:T(8,128)(2,1)}, bf16[2,256,896]{2,1,0:T(8,128)(2,1)}, u32[]{:S(2)}, u32[]{:S(2)}) collective-permute-start(bf16[2,256,896]{2,1,0:T(8,128)(2,1)} %get-tuple-element.106), channel_id=1, source_target_pairs={{0,254},{2,4},{4,2},{6,8},{8,6},{10,12},{12,10},{14,16},{16,14},{1... | collective-permute-start | bytes 2752520 | tf_op jit(solution)/shard_map/ppermute | solution.py:317
  81.1 24.8 %collective-permute-start.15 = (bf16[384,896]{1,0:T(8,128)(2,1)}, bf16[384,896]{1,0:T(8,128)(2,1)}, u32[]{:S(2)}, u32[]{:S(2)}) collective-permute-start(bf16[384,896]{1,0:T(8,128)(2,1)} %get-tuple-element.120), channel_id=1, source_target_pairs={{0,1},{1,0},{2,3},{3,2},{4,5},{5,4},{6,7},{7,6},{8,9},{9,8},{10,11... | collective-permute-start | bytes 2064392 | tf_op jit(solution)/shard_map/ppermute | solution.py:326
  94.4 21.4 %collective-permute-start.14 = (bf16[256,896]{1,0:T(8,128)(2,1)}, bf16[256,896]{1,0:T(8,128)(2,1)}, u32[]{:S(2)}, u32[]{:S(2)}) collective-permute-start(bf16[256,896]{1,0:T(8,128)(2,1)} %get-tuple-element.119), channel_id=1, source_target_pairs={{0,1},{1,0},{2,3},{3,2},{4,5},{5,4},{6,7},{7,6},{8,9},{9,8},{10,11... | collective-permute-start | bytes 1376264 | tf_op jit(solution)/shard_map/ppermute | solution.py:326

commit v6 on v5

--- a/solution.py
+++ b/solution.py
@@ -358,7 +358,7 @@
 
     def arrivals(n):
         moves = [(0, 1, *spans[n]), (TILE, 2, *spans[n])]
-        return moves + ([(2 * TILE, 0, *spans[n + 1])] if n + 1 < count else [])
+        return moves + ([(2 * TILE, 0, *spans[n + 1])] if n + 2 < count else [])
 
     def finish(n):
         nonlocal out_q, out_kv
@@ -366,15 +366,18 @@
         if n in RELAYED:
             (first_leg,) = after([(owns, n + 1)], from_far[n])
             legs.append(across_x(first_leg))
-        last = n + 1 == count
+        rides = n + 2 < count
         arrived, moves = [], []
         if n == 1:
             arrived, moves = [first_q], [(0, 0, 0, *spans[0])]
         if n >= 2:
             arrived, moves = [kv_parts[n - 2]], [(0, *move) for move in arrivals(n - 2)]
+        if n + 1 == count:
+            arrived.append(last_q)
+            moves.append((len(arrived) - 1, 0, 0, *spans[n]))
         *out_kv, send, out_q = combine(
             side, at_corner, owns[n], from_near[n], legs, out_q, out_kv,
-            None if last else sends[n + 1], 0 if last else spans[n + 1][1], arrived, moves, *spans[n],
+            sends[n + 1] if rides else None, spans[n + 1][1] if rides else 0, arrived, moves, *spans[n],
         )
         kv_parts.append(swap(send))
 
@@ -411,6 +414,8 @@
         from_far.append(far_swap(far_part, n in RELAYED))
         if n == 0:
             first_q = swap(send_q)
+        if n + 1 == count:
+            last_q = swap(send_q)
         sends.append(send_q)
         nears.append(near_part)
         owns.append(own)

time: 119 us -> 119 us (level)
  starting transfers between devices: 14.3 us -> 16.3 us
  waiting for transfers between devices: 55.6 us -> 53.9 us
    ppermute x6, waiting for transfers between devices: 15.9 us -> 6.62 us  [far_swap(): return lax.ppermute(x, 'ctx', pairs)]
    ppermute x4 -> x5, waiting for transfers between devices: 39.7 us -> 47.2 us  [swap(): return lax.ppermute(x, 'section', [(0, 1), (1, 0)])]
    ppermute x4 -> x5, starting transfers between devices: 4.57 us -> 6.5 us  [swap(): return lax.ppermute(x, 'section', [(0, 1), (1, 0)])]
  transfers between devices with their start and end apart: 16 -> 17, of which waited for: 8 -> 8; matrix products, arithmetic and copies ran while one was open for 1% -> 1% of each run, Pallas kernels for 38% -> 37%
where the time goes in v6:
time: 119 us; the launch traced here: 118 us
  waiting for transfers between devices  53.9 us (45%)
  Pallas kernels  45.8 us (38%)
  starting transfers between devices  16.3 us (14%)
    ppermute x5, waiting for transfers between devices, swap(): return lax.ppermute(x, 'section', [(0, 1), (1, 0)])  47.2 us
    pallas_call x3, Pallas kernels, attn_chunk(): pl.pallas_call(attn_kernel, grid_spec=pltpu.PrefetchScalarGridSpec(num_sc...  28.4 us
    pallas_call x3, Pallas kernels, combine(): pl.pallas_call(functools.partial(combine_kernel, h0, hc, relayed, extra,...  9.58 us
    ppermute x6, waiting for transfers between devices, far_swap(): return lax.ppermute(x, 'ctx', pairs)  6.62 us
    ppermute x5, starting transfers between devices, swap(): return lax.ppermute(x, 'section', [(0, 1), (1, 0)])  6.5 us
    ppermute x5, starting transfers between devices, near_swap(): lax.ppermute(x, 'ctx', [(i, i ^ 1) for i in range(lax.axis_size('ctx'))])  4.61 us
    pallas_call x2, Pallas kernels, pack(): pl.pallas_call(functools.partial(pack_kernel, spans), grid=(1,), in_specs...  4.22 us
    pallas_call x2, Pallas kernels, place(): pl.pallas_call(functools.partial(place_kernel, moves), grid_spec=pltpu.Pr...  3.59 us
  transfers between devices with their start and end apart: 17, of which 8 were waited for; matrix products, arithmetic and copies ran while one was open for 1% of the time, Pallas kernels for 37%

profile of v6, /device:TPU:225, one launch (start us, length us, event | category | flops | bytes accessed | tf_op | source)
XLA Modules:
  0.0 117.7 jit_solution(1960778417782716219)
XLA Ops:
  0.6 0.8 collective-permute-start
  1.4 0.1 collective-permute-start.1
  1.5 1.9 %pack.2 = bf16[2,256,768]{2,1,0:T(8,128)(2,1)} custom-call(bf16[256,2560]{1,0:T(8,128)(2,1)} %k_ref.8, bf16[256,2560]{1,0:T(8,128)(2,1)} %v_ref.9), custom_call_target="tpu_custom_call" | custom-call | flops 1000 | bytes 1000 | tf_op jit(solution)/shard_map/pack/pallas_call | solution.py:286
  3.4 1.7 %collective-permute-start.2 = (bf16[2,256,768]{2,1,0:T(8,128)(2,1)}, bf16[2,256,768]{2,1,0:T(8,128)(2,1)}, u32[]{:S(2)}, u32[]{:S(2)}) collective-permute-start(bf16[2,256,768]{2,1,0:T(8,128)(2,1)} %pack.2), channel_id=1, source_target_pairs={{0,254},{2,4},{4,2},{6,8},{8,6},{10,12},{12,10},{14,16},{16,14},{1... | collective-permute-start | bytes 2359304 | tf_op jit(solution)/shard_map/ppermute | solution.py:317
  5.1 2.3 %pack.3 = (bf16[2,256,896]{2,1,0:T(8,128)(2,1)}, bf16[2,256,896]{2,1,0:T(8,128)(2,1)}) custom-call(bf16[256,2560]{1,0:T(8,128)(2,1)} %k_ref.8, bf16[256,2560]{1,0:T(8,128)(2,1)} %v_ref.9), custom_call_target="tpu_custom_call" | custom-call | flops 1000 | bytes 1000 | tf_op jit(solution)/shard_map/pack/pallas_call | solution.py:286
  7.4 0.9 collective-permute-start.3
  8.7 0.9 collective-permute-start.6
  9.6 0.7 maximum_maximum_fusion.bias_ref
  10.2 5.3 %collective-permute-done.2.far_ref = bf16[2,256,768]{2,1,0:T(8,128)(2,1)} collective-permute-done((bf16[2,256,768]{2,1,0:T(8,128)(2,1)}, bf16[2,256,768]{2,1,0:T(8,128)(2,1)}, u32[]{:S(2)}, u32[]{:S(2)}) %collective-permute-start.2) | collective-permute-done | bytes 786464 | tf_op jit(solution)/shard_map/ppermute | solution.py:317
  15.5 8.6 %attn.3 = (bf16[128,5120]{1,0:T(8,128)(2,1)}, bf16[128,768]{1,0:T(8,128)(2,1)}, bf16[2,256,768]{2,1,0:T(8,128)(2,1)}, bf16[2,256,768]{2,1,0:T(8,128)(2,1)}, bf16[2,256,768]{2,1,0:T(8,128)(2,1)}) custom-call(s32[1]{0:T(128)} %bitcast.side_ref, bf16[256,2560]{1,0:T(8,128)(2,1)} %q_ref.5, bf16[256,2560]{1,0:T(8,128)(2,1)} %do_ref.5, bf16[256,2560]{1,0:T(8,128)(2,1)} %k_ref.8, ...), custom_call_target="tpu_custom_call" | custom-call | flops 1000 | bytes 1000 | tf_op jit(solution)/shard_map/attn/pallas_call | solution.py:98
  24.1 1.2 %collective-permute-done.3.far_ref = bf16[2,256,896]{2,1,0:T(8,128)(2,1)} collective-permute-done((bf16[2,256,896]{2,1,0:T(8,128)(2,1)}, bf16[2,256,896]{2,1,0:T(8,128)(2,1)}, u32[]{:S(2)}, u32[]{:S(2)}) %collective-permute-start.3) | collective-permute-done | bytes 917536 | tf_op jit(solution)/shard_map/ppermute | solution.py:317
  25.3 2.2 %collective-permute-start.5 = (bf16[2,256,768]{2,1,0:T(8,128)(2,1)}, bf16[2,256,768]{2,1,0:T(8,128)(2,1)}, u32[]{:S(2)}, u32[]{:S(2)}) collective-permute-start(bf16[2,256,768]{2,1,0:T(8,128)(2,1)} %get-tuple-element.82), channel_id=1, source_target_pairs={{0,2},{2,0},{4,6},{6,4},{8,10},{10,8},{12,14},{14,12},{16,18},{18,... | collective-permute-start | bytes 2359304 | tf_op jit(solution)/shard_map/ppermute | solution.py:301
  27.6 2.7 %collective-permute-start.4 = (bf16[128,768]{1,0:T(8,128)(2,1)}, bf16[128,768]{1,0:T(8,128)(2,1)}, u32[]{:S(2)}, u32[]{:S(2)}) collective-permute-start(bf16[128,768]{1,0:T(8,128)(2,1)} %get-tuple-element.81), channel_id=1, source_target_pairs={{0,1},{1,0},{2,3},{3,2},{4,5},{5,4},{6,7},{7,6},{8,9},{9,8},{10,11... | collective-permute-start | bytes 589832 | tf_op jit(solution)/shard_map/ppermute | solution.py:326
  30.3 9.9 %attn.4 = (bf16[128,5120]{1,0:T(8,128)(2,1)}, bf16[128,896]{1,0:T(8,128)(2,1)}, bf16[2,256,896]{2,1,0:T(8,128)(2,1)}, bf16[2,256,896]{2,1,0:T(8,128)(2,1)}, bf16[2,256,896]{2,1,0:T(8,128)(2,1)}) custom-call(s32[1]{0:T(128)} %bitcast.side_ref, bf16[256,2560]{1,0:T(8,128)(2,1)} %q_ref.5, bf16[256,2560]{1,0:T(8,128)(2,1)} %do_ref.5, ...), custom_call_target="tpu_custom_call", output_to_operand_aliasing={{0}: (9, {})} | custom-call | flops 1000 | bytes 1000 | tf_op jit(solution)/shard_map/attn/pallas_call | solution.py:98
  40.2 14.3 %collective-permute-done.4.refs_4_ = bf16[128,768]{1,0:T(8,128)(2,1)} collective-permute-done((bf16[128,768]{1,0:T(8,128)(2,1)}, bf16[128,768]{1,0:T(8,128)(2,1)}, u32[]{:S(2)}, u32[]{:S(2)}) %collective-permute-start.4) | collective-permute-done | bytes 196640 | tf_op jit(solution)/shard_map/ppermute | solution.py:326
  54.5 0.6 collective-permute-start.9
  55.1 2.8 %combine.3 = (bf16[128,5120]{1,0:T(8,128)(2,1)}, bf16[128,5120]{1,0:T(8,128)(2,1)}, bf16[384,896]{1,0:T(8,128)(2,1)}, bf16[128,5120]{1,0:T(8,128)(2,1)}) custom-call(s32[1]{0:T(128)} %bitcast.side_ref, s32[1]{0:T(128)} %bitcast.1.corner_ref, bf16[2,256,768]{2,1,0:T(8,128)(2,1)} %get-tuple-element.88.refs_0_, ...), custom_call_target="tpu_custom_call", output_to_operand_aliasing={{3}: (6, {})} | custom-call | flops 1000 | bytes 1000 | tf_op jit(solution)/shard_map/combine/pallas_call | solution.py:204
  57.9 0.6 collective-permute-start.10
  58.5 9.9 %attn.5 = (bf16[128,5120]{1,0:T(8,128)(2,1)}, bf16[128,896]{1,0:T(8,128)(2,1)}, bf16[2,256,896]{2,1,0:T(8,128)(2,1)}, bf16[2,256,896]{2,1,0:T(8,128)(2,1)}, bf16[2,256,896]{2,1,0:T(8,128)(2,1)}) custom-call(s32[1]{0:T(128)} %bitcast.side_ref, bf16[256,2560]{1,0:T(8,128)(2,1)} %q_ref.5, bf16[256,2560]{1,0:T(8,128)(2,1)} %do_ref.5, ...), custom_call_target="tpu_custom_call", output_to_operand_aliasing={{0}: (9, {})} | custom-call | flops 1000 | bytes 1000 | tf_op jit(solution)/shard_map/attn/pallas_call | solution.py:98
  68.4 0.1 collective-permute-done.7.refs_2_
  68.5 1.6 %collective-permute-start.14 = (bf16[2,256,896]{2,1,0:T(8,128)(2,1)}, bf16[2,256,896]{2,1,0:T(8,128)(2,1)}, u32[]{:S(2)}, u32[]{:S(2)}) collective-permute-start(bf16[2,256,896]{2,1,0:T(8,128)(2,1)} %collective-permute-done.7.refs_2_), channel_id=1, source_target_pairs={{0,128},{126,254},{128,0},{254,126},{1,129},{127,255},{129,1},{255... | collective-permute-start | bytes 2752520 | tf_op jit(solution)/shard_map/ppermute | solution.py:322
  70.1 6.6 %collective-permute-done.10.refs_3_ = bf16[384,896]{1,0:T(8,128)(2,1)} collective-permute-done((bf16[384,896]{1,0:T(8,128)(2,1)}, bf16[384,896]{1,0:T(8,128)(2,1)}, u32[]{:S(2)}, u32[]{:S(2)}) %collective-permute-start.10) | collective-permute-done | bytes 688160 | tf_op jit(solution)/shard_map/ppermute | solution.py:326
  76.7 0.9 collective-permute-start.11
  77.6 0.5 collective-permute-start.13
  78.2 3.3 %combine.4 = (bf16[128,5120]{1,0:T(8,128)(2,1)}, bf16[128,5120]{1,0:T(8,128)(2,1)}, bf16[256,896]{1,0:T(8,128)(2,1)}, bf16[128,5120]{1,0:T(8,128)(2,1)}) custom-call(s32[1]{0:T(128)} %bitcast.side_ref, s32[1]{0:T(128)} %bitcast.1.corner_ref, ...), custom_call_target="tpu_custom_call", output_to_operand_aliasing={{3}: (7, {}), {0}: (8, {}), {1}: (9, {})} | custom-call | flops 1000 | bytes 1000 | tf_op jit(solution)/shard_map/combine/pallas_call | solution.py:204
  81.5 2.5 %collective-permute-start.16 = (bf16[256,896]{1,0:T(8,128)(2,1)}, bf16[256,896]{1,0:T(8,128)(2,1)}, u32[]{:S(2)}, u32[]{:S(2)}) collective-permute-start(bf16[256,896]{1,0:T(8,128)(2,1)} %get-tuple-element.120), channel_id=1, source_target_pairs={{0,1},{1,0},{2,3},{3,2},{4,5},{5,4},{6,7},{7,6},{8,9},{9,8},{10,11... | collective-permute-start | bytes 1376264 | tf_op jit(solution)/shard_map/ppermute | solution.py:326
  84.0 12.1 %collective-permute-done.13.refs_4_ = bf16[128,896]{1,0:T(8,128)(2,1)} collective-permute-done((bf16[128,896]{1,0:T(8,128)(2,1)}, bf16[128,896]{1,0:T(8,128)(2,1)}, u32[]{:S(2)}, u32[]{:S(2)}) %collective-permute-start.13) | collective-permute-done | bytes 229408 | tf_op jit(solution)/shard_map/ppermute | solution.py:326
  96.1 3.5 %combine.5 = (bf16[128,5120]{1,0:T(8,128)(2,1)}, bf16[128,5120]{1,0:T(8,128)(2,1)}, bf16[256,896]{1,0:T(8,128)(2,1)}, bf16[128,5120]{1,0:T(8,128)(2,1)}) custom-call(s32[1]{0:T(128)} %bitcast.side_ref, s32[1]{0:T(128)} %bitcast.1.corner_ref, ...), custom_call_target="tpu_custom_call", output_to_operand_aliasing={{3}: (7, {}), {0}: (8, {}), {1}: (9, {})} | custom-call | flops 1000 | bytes 1000 | tf_op jit(solution)/shard_map/combine/pallas_call | solution.py:204
  99.7 6.3 %collective-permute-done.16.refs_0_ = bf16[256,896]{1,0:T(8,128)(2,1)} collective-permute-done((bf16[256,896]{1,0:T(8,128)(2,1)}, bf16[256,896]{1,0:T(8,128)(2,1)}, u32[]{:S(2)}, u32[]{:S(2)}) %collective-permute-start.16) | collective-permute-done | bytes 458784 | tf_op jit(solution)/shard_map/ppermute | solution.py:326
  105.9 1.8 %place.2 = (bf16[128,5120]{1,0:T(8,128)(2,1)}, bf16[128,5120]{1,0:T(8,128)(2,1)}, bf16[128,5120]{1,0:T(8,128)(2,1)}) custom-call(s32[1]{0:T(128)} %bitcast.side_ref, bf16[256,896]{1,0:T(8,128)(2,1)} %collective-permute-done.16.refs_0_, bf16[128,5120]{1,0:T(8,128)(2,1)} %get-tuple-element.121.refs_1_, ...), custom_call_target="tpu_custom_call", output_to_operand_aliasing={{0}: (2, {}), {1}: (3, {}), {2}: (4, {})} | custom-call | flops 1000 | bytes 1000 | tf_op jit(solution)/shard_map/place/pallas_call | solution.py:246
  107.7 8.0 %collective-permute-done.15.refs_0_ = bf16[256,896]{1,0:T(8,128)(2,1)} collective-permute-done((bf16[256,896]{1,0:T(8,128)(2,1)}, bf16[256,896]{1,0:T(8,128)(2,1)}, u32[]{:S(2)}, u32[]{:S(2)}) %collective-permute-start.15) | collective-permute-done | bytes 458784 | tf_op jit(solution)/shard_map/ppermute | solution.py:326
  115.8 1.8 %place.3 = (bf16[128,5120]{1,0:T(8,128)(2,1)}, bf16[128,5120]{1,0:T(8,128)(2,1)}, bf16[128,5120]{1,0:T(8,128)(2,1)}) custom-call(s32[1]{0:T(128)} %bitcast.side_ref, bf16[256,896]{1,0:T(8,128)(2,1)} %collective-permute-done.15.refs_0_, bf16[128,5120]{1,0:T(8,128)(2,1)} %get-tuple-element.124.refs_1_, ...), custom_call_target="tpu_custom_call", output_to_operand_aliasing={{0}: (2, {}), {1}: (3, {}), {2}: (4, {})} | custom-call | flops 1000 | bytes 1000 | tf_op jit(solution)/shard_map/place/pallas_call | solution.py:246
  (24 shorter events, 0.4 us)
Async XLA Ops:
  0.6 4.5 %collective-permute-start = (bf16[256,2560]{1,0:T(8,128)(2,1)}, bf16[256,2560]{1,0:T(8,128)(2,1)}, u32[]{:S(2)}, u32[]{:S(2)}) collective-permute-start(bf16[256,2560]{1,0:T(8,128)(2,1)} %k_ref.8), channel_id=1, source_target_pairs={{0,2},{2,0},{4,6},{6,4},{8,10},{10,8},{12,14},{14,12},{16,18},{18,... | collective-permute-start | bytes 3932168 | tf_op jit(solution)/shard_map/ppermute | solution.py:301
  1.4 14.1 %collective-permute-start.1 = (bf16[256,2560]{1,0:T(8,128)(2,1)}, bf16[256,2560]{1,0:T(8,128)(2,1)}, u32[]{:S(2)}, u32[]{:S(2)}) collective-permute-start(bf16[256,2560]{1,0:T(8,128)(2,1)} %v_ref.9), channel_id=1, source_target_pairs={{0,2},{2,0},{4,6},{6,4},{8,10},{10,8},{12,14},{14,12},{16,18},{18,... | collective-permute-start | bytes 3932168 | tf_op jit(solution)/shard_map/ppermute | solution.py:301
  3.4 12.1 %collective-permute-start.2 = (bf16[2,256,768]{2,1,0:T(8,128)(2,1)}, bf16[2,256,768]{2,1,0:T(8,128)(2,1)}, u32[]{:S(2)}, u32[]{:S(2)}) collective-permute-start(bf16[2,256,768]{2,1,0:T(8,128)(2,1)} %pack.2), channel_id=1, source_target_pairs={{0,254},{2,4},{4,2},{6,8},{8,6},{10,12},{12,10},{14,16},{16,14},{1... | collective-permute-start | bytes 2359304 | tf_op jit(solution)/shard_map/ppermute | solution.py:317
  5.1 3.3 %copy-start = (s32[256,6]{0,1:T(8,128)S(1)}, s32[256,6]{0,1:T(8,128)}, u32[]{:S(2)}) copy-start(s32[256,6]{0,1:T(8,128)} %param.9) | copy-start | bytes 18436
  7.4 17.9 %collective-permute-start.3 = (bf16[2,256,896]{2,1,0:T(8,128)(2,1)}, bf16[2,256,896]{2,1,0:T(8,128)(2,1)}, u32[]{:S(2)}, u32[]{:S(2)}) collective-permute-start(bf16[2,256,896]{2,1,0:T(8,128)(2,1)} %get-tuple-element.67), channel_id=1, source_target_pairs={{0,254},{2,4},{4,2},{6,8},{8,6},{10,12},{12,10},{14,16},{16,14},{1... | collective-permute-start | bytes 2752520 | tf_op jit(solution)/shard_map/ppermute | solution.py:317
  8.7 45.8 %collective-permute-start.6 = (bf16[2,256,896]{2,1,0:T(8,128)(2,1)}, bf16[2,256,896]{2,1,0:T(8,128)(2,1)}, u32[]{:S(2)}, u32[]{:S(2)}) collective-permute-start(bf16[2,256,896]{2,1,0:T(8,128)(2,1)} %get-tuple-element.68), channel_id=1, source_target_pairs={{0,254},{2,4},{4,2},{6,8},{8,6},{10,12},{12,10},{14,16},{16,14},{1... | collective-permute-start | bytes 2752520 | tf_op jit(solution)/shard_map/ppermute | solution.py:317
  25.3 29.1 %collective-permute-start.5 = (bf16[2,256,768]{2,1,0:T(8,128)(2,1)}, bf16[2,256,768]{2,1,0:T(8,128)(2,1)}, u32[]{:S(2)}, u32[]{:S(2)}) collective-permute-start(bf16[2,256,768]{2,1,0:T(8,128)(2,1)} %get-tuple-element.82), channel_id=1, source_target_pairs={{0,2},{2,0},{4,6},{6,4},{8,10},{10,8},{12,14},{14,12},{16,18},{18,... | collective-permute-start | bytes 2359304 | tf_op jit(solution)/shard_map/ppermute | solution.py:301
  27.6 26.9 %collective-permute-start.8 = (bf16[2,256,768]{2,1,0:T(8,128)(2,1)}, bf16[2,256,768]{2,1,0:T(8,128)(2,1)}, u32[]{:S(2)}, u32[]{:S(2)}) collective-permute-start(bf16[2,256,768]{2,1,0:T(8,128)(2,1)} %get-tuple-element.86), channel_id=1, source_target_pairs={{0,254},{2,4},{4,2},{6,8},{8,6},{10,12},{12,10},{14,16},{16,14},{1... | collective-permute-start | bytes 2359304 | tf_op jit(solution)/shard_map/ppermute | solution.py:317
  27.6 26.9 %collective-permute-start.4 = (bf16[128,768]{1,0:T(8,128)(2,1)}, bf16[128,768]{1,0:T(8,128)(2,1)}, u32[]{:S(2)}, u32[]{:S(2)}) collective-permute-start(bf16[128,768]{1,0:T(8,128)(2,1)} %get-tuple-element.81), channel_id=1, source_target_pairs={{0,1},{1,0},{2,3},{3,2},{4,5},{5,4},{6,7},{7,6},{8,9},{9,8},{10,11... | collective-permute-start | bytes 589832 | tf_op jit(solution)/shard_map/ppermute | solution.py:326
  54.5 13.9 %collective-permute-start.9 = (bf16[2,256,896]{2,1,0:T(8,128)(2,1)}, bf16[2,256,896]{2,1,0:T(8,128)(2,1)}, u32[]{:S(2)}, u32[]{:S(2)}) collective-permute-start(bf16[2,256,896]{2,1,0:T(8,128)(2,1)} %get-tuple-element.100), channel_id=1, source_target_pairs={{0,2},{2,0},{4,6},{6,4},{8,10},{10,8},{12,14},{14,12},{16,18},{18,... | collective-permute-start | bytes 2752520 | tf_op jit(solution)/shard_map/ppermute | solution.py:301
  55.1 13.4 %collective-permute-start.7 = (bf16[2,256,896]{2,1,0:T(8,128)(2,1)}, bf16[2,256,896]{2,1,0:T(8,128)(2,1)}, u32[]{:S(2)}, u32[]{:S(2)}) collective-permute-start(bf16[2,256,896]{2,1,0:T(8,128)(2,1)} %get-tuple-element.83), channel_id=1, source_target_pairs={{0,126},{2,4},{4,2},{6,8},{8,6},{10,12},{12,10},{14,16},{16,14},{1... | collective-permute-start | bytes 2752520 | tf_op jit(solution)/shard_map/ppermute | solution.py:317
  57.9 18.8 %collective-permute-start.10 = (bf16[384,896]{1,0:T(8,128)(2,1)}, bf16[384,896]{1,0:T(8,128)(2,1)}, u32[]{:S(2)}, u32[]{:S(2)}) collective-permute-start(bf16[384,896]{1,0:T(8,128)(2,1)} %get-tuple-element.104), channel_id=1, source_target_pairs={{0,1},{1,0},{2,3},{3,2},{4,5},{5,4},{6,7},{7,6},{8,9},{9,8},{10,11... | collective-permute-start | bytes 2064392 | tf_op jit(solution)/shard_map/ppermute | solution.py:326
  68.5 9.7 %collective-permute-start.14 = (bf16[2,256,896]{2,1,0:T(8,128)(2,1)}, bf16[2,256,896]{2,1,0:T(8,128)(2,1)}, u32[]{:S(2)}, u32[]{:S(2)}) collective-permute-start(bf16[2,256,896]{2,1,0:T(8,128)(2,1)} %collective-permute-done.7.refs_2_), channel_id=1, source_target_pairs={{0,128},{126,254},{128,0},{254,126},{1,129},{127,255},{129,1},{255... | collective-permute-start | bytes 2752520 | tf_op jit(solution)/shard_map/ppermute | solution.py:322
  76.7 19.4 %collective-permute-start.11 = (bf16[2,256,896]{2,1,0:T(8,128)(2,1)}, bf16[2,256,896]{2,1,0:T(8,128)(2,1)}, u32[]{:S(2)}, u32[]{:S(2)}) collective-permute-start(bf16[2,256,896]{2,1,0:T(8,128)(2,1)} %get-tuple-element.105), channel_id=1, source_target_pairs={{0,2},{2,0},{4,6},{6,4},{8,10},{10,8},{12,14},{14,12},{16,18},{18,... | collective-permute-start | bytes 2752520 | tf_op jit(solution)/shard_map/ppermute | solution.py:301
  77.6 18.5 %collective-permute-start.12 = (bf16[2,256,896]{2,1,0:T(8,128)(2,1)}, bf16[2,256,896]{2,1,0:T(8,128)(2,1)}, u32[]{:S(2)}, u32[]{:S(2)}) collective-permute-start(bf16[2,256,896]{2,1,0:T(8,128)(2,1)} %get-tuple-element.106), channel_id=1, source_target_pairs={{0,254},{2,4},{4,2},{6,8},{8,6},{10,12},{12,10},{14,16},{16,14},{1... | collective-permute-start | bytes 2752520 | tf_op jit(solution)/shard_map/ppermute | solution.py:317
  77.6 18.5 %collective-permute-start.13 = (bf16[128,896]{1,0:T(8,128)(2,1)}, bf16[128,896]{1,0:T(8,128)(2,1)}, u32[]{:S(2)}, u32[]{:S(2)}) collective-permute-start(bf16[128,896]{1,0:T(8,128)(2,1)} %get-tuple-element.108), channel_id=1, source_target_pairs={{0,1},{1,0},{2,3},{3,2},{4,5},{5,4},{6,7},{7,6},{8,9},{9,8},{10,11... | collective-permute-start | bytes 688136 | tf_op jit(solution)/shard_map/ppermute | solution.py:326
  81.5 24.4 %collective-permute-start.16 = (bf16[256,896]{1,0:T(8,128)(2,1)}, bf16[256,896]{1,0:T(8,128)(2,1)}, u32[]{:S(2)}, u32[]{:S(2)}) collective-permute-start(bf16[256,896]{1,0:T(8,128)(2,1)} %get-tuple-element.120), channel_id=1, source_target_pairs={{0,1},{1,0},{2,3},{3,2},{4,5},{5,4},{6,7},{7,6},{8,9},{9,8},{10,11... | collective-permute-start | bytes 1376264 | tf_op jit(solution)/shard_map/ppermute | solution.py:326
  99.6 16.2 %collective-permute-start.15 = (bf16[256,896]{1,0:T(8,128)(2,1)}, bf16[256,896]{1,0:T(8,128)(2,1)}, u32[]{:S(2)}, u32[]{:S(2)}) collective-permute-start(bf16[256,896]{1,0:T(8,128)(2,1)} %get-tuple-element.119), channel_id=1, source_target_pairs={{0,1},{1,0},{2,3},{3,2},{4,5},{5,4},{6,7},{7,6},{8,9},{9,8},{10,11... | collective-permute-start | bytes 1376264 | tf_op jit(solution)/shard_map/ppermute | solution.py:326

commit v7 on v6

--- a/solution.py
+++ b/solution.py
@@ -140,7 +140,7 @@
     fetches = [
         [
             pltpu.make_async_copy(ins[n].at[j], parts.at[j, n], in_sems.at[j, n])
-            for n in range(3 + relayed)
+            for n in range(3)
         ]
         for j in range(2)
     ]
@@ -158,16 +158,23 @@
         )
         for n, (source, target) in enumerate(carries)
     ]
-    for copy in fetches[0] + fetches[1] + [fetch for fetch, _ in carries]:
-        copy.start()
+    if relayed:
+        at_corner = corner_ref[0] == 1
+        for j in range(2):
+            straight = fetches[j][2]
+            across = pltpu.make_async_copy(ins[3].at[j], parts.at[j, 2], in_sems.at[j, 2])
+            pl.when(at_corner)(across.start)
+            pl.when(jnp.logical_not(at_corner))(straight.start)
+    for j in range(2):
+        for copy in fetches[j][: 2 if relayed else 3]:
+            copy.start()
+    for fetch, _ in carries:
+        fetch.start()
     leaving = []
     for j, keep in enumerate((keep_k, keep_v)):
         for copy in fetches[j]:
             copy.wait()
-        far = parts[j, 2]
-        if relayed:
-            far = jnp.where(corner_ref[0] == 1, parts[j, 3], far)
-        total = parts[j, 0].astype(f32) + parts[j, 1].astype(f32) + far.astype(f32)
+        total = parts[j, 0].astype(f32) + parts[j, 1].astype(f32) + parts[j, 2].astype(f32)
         split_rows(side, total.astype(BF16), kept.at[j], sent.at[j])
         leaving += [
             pltpu.make_async_copy(
@@ -209,10 +216,10 @@
             in_specs=[anywhere] * len(args),
             out_specs=[anywhere] * 4,
             scratch_shapes=[
-                pltpu.VMEM((2, 3 + relayed, ROWS, width), BF16),
+                pltpu.VMEM((2, 3, ROWS, width), BF16),
                 pltpu.VMEM((2, TILE, width), BF16),
                 pltpu.VMEM((2, TILE, width), BF16),
-                pltpu.SemaphoreType.DMA((2, 3 + relayed)),
+                pltpu.SemaphoreType.DMA((2, 3)),
                 pltpu.SemaphoreType.DMA((2, 2)),
                 pltpu.SemaphoreType.DMA((max(len(stages), 1), 2)),
             ]

time: 119 us -> 119 us (level)
  no operation moved by 1% of the time
where the time goes in v7:
time: 119 us; the launch traced here: 118 us
  waiting for transfers between devices  54.1 us (45%)
  Pallas kernels  45.5 us (38%)
  starting transfers between devices  16.2 us (14%)
    ppermute x5, waiting for transfers between devices, swap(): return lax.ppermute(x, 'section', [(0, 1), (1, 0)])  47.4 us
    pallas_call x3, Pallas kernels, attn_chunk(): pl.pallas_call(attn_kernel, grid_spec=pltpu.PrefetchScalarGridSpec(num_sc...  28.4 us
    pallas_call x3, Pallas kernels, combine(): pl.pallas_call(functools.partial(combine_kernel, h0, hc, relayed, extra,...  9.36 us
    ppermute x6, waiting for transfers between devices, far_swap(): return lax.ppermute(x, 'ctx', pairs)  6.62 us
    ppermute x5, starting transfers between devices, swap(): return lax.ppermute(x, 'section', [(0, 1), (1, 0)])  6.49 us
    ppermute x5, starting transfers between devices, near_swap(): lax.ppermute(x, 'ctx', [(i, i ^ 1) for i in range(lax.axis_size('ctx'))])  4.61 us
    pallas_call x2, Pallas kernels, pack(): pl.pallas_call(functools.partial(pack_kernel, spans), grid=(1,), in_specs...  4.22 us
    pallas_call x2, Pallas kernels, place(): pl.pallas_call(functools.partial(place_kernel, moves), grid_spec=pltpu.Pr...  3.59 us
  transfers between devices with their start and end apart: 17, of which 8 were waited for; matrix products, arithmetic and copies ran while one was open for 1% of the time, Pallas kernels for 37%

profile of v7, /device:TPU:225, one launch (start us, length us, event | category | flops | bytes accessed | tf_op | source)
XLA Modules:
  0.0 117.7 jit_solution(17733563577803258231)
XLA Ops:
  0.6 0.8 collective-permute-start
  1.4 0.1 collective-permute-start.1
  1.5 1.9 %pack.2 = bf16[2,256,768]{2,1,0:T(8,128)(2,1)} custom-call(bf16[256,2560]{1,0:T(8,128)(2,1)} %k_ref.8, bf16[256,2560]{1,0:T(8,128)(2,1)} %v_ref.9), custom_call_target="tpu_custom_call" | custom-call | flops 1000 | bytes 1000 | tf_op jit(solution)/shard_map/pack/pallas_call | solution.py:293
  3.4 1.7 %collective-permute-start.2 = (bf16[2,256,768]{2,1,0:T(8,128)(2,1)}, bf16[2,256,768]{2,1,0:T(8,128)(2,1)}, u32[]{:S(2)}, u32[]{:S(2)}) collective-permute-start(bf16[2,256,768]{2,1,0:T(8,128)(2,1)} %pack.2), channel_id=1, source_target_pairs={{0,254},{2,4},{4,2},{6,8},{8,6},{10,12},{12,10},{14,16},{16,14},{1... | collective-permute-start | bytes 2359304 | tf_op jit(solution)/shard_map/ppermute | solution.py:324
  5.1 2.3 %pack.3 = (bf16[2,256,896]{2,1,0:T(8,128)(2,1)}, bf16[2,256,896]{2,1,0:T(8,128)(2,1)}) custom-call(bf16[256,2560]{1,0:T(8,128)(2,1)} %k_ref.8, bf16[256,2560]{1,0:T(8,128)(2,1)} %v_ref.9), custom_call_target="tpu_custom_call" | custom-call | flops 1000 | bytes 1000 | tf_op jit(solution)/shard_map/pack/pallas_call | solution.py:293
  7.4 0.9 collective-permute-start.3
  8.7 0.9 collective-permute-start.6
  9.6 0.7 maximum_maximum_fusion.bias_ref
  10.2 5.3 %collective-permute-done.2.far_ref = bf16[2,256,768]{2,1,0:T(8,128)(2,1)} collective-permute-done((bf16[2,256,768]{2,1,0:T(8,128)(2,1)}, bf16[2,256,768]{2,1,0:T(8,128)(2,1)}, u32[]{:S(2)}, u32[]{:S(2)}) %collective-permute-start.2) | collective-permute-done | bytes 786464 | tf_op jit(solution)/shard_map/ppermute | solution.py:324
  15.5 8.6 %attn.3 = (bf16[128,5120]{1,0:T(8,128)(2,1)}, bf16[128,768]{1,0:T(8,128)(2,1)}, bf16[2,256,768]{2,1,0:T(8,128)(2,1)}, bf16[2,256,768]{2,1,0:T(8,128)(2,1)}, bf16[2,256,768]{2,1,0:T(8,128)(2,1)}) custom-call(s32[1]{0:T(128)} %bitcast.side_ref, bf16[256,2560]{1,0:T(8,128)(2,1)} %q_ref.5, bf16[256,2560]{1,0:T(8,128)(2,1)} %do_ref.5, bf16[256,2560]{1,0:T(8,128)(2,1)} %k_ref.8, ...), custom_call_target="tpu_custom_call" | custom-call | flops 1000 | bytes 1000 | tf_op jit(solution)/shard_map/attn/pallas_call | solution.py:98
  24.1 1.2 %collective-permute-done.3.far_ref = bf16[2,256,896]{2,1,0:T(8,128)(2,1)} collective-permute-done((bf16[2,256,896]{2,1,0:T(8,128)(2,1)}, bf16[2,256,896]{2,1,0:T(8,128)(2,1)}, u32[]{:S(2)}, u32[]{:S(2)}) %collective-permute-start.3) | collective-permute-done | bytes 917536 | tf_op jit(solution)/shard_map/ppermute | solution.py:324
  25.3 2.2 %collective-permute-start.5 = (bf16[2,256,768]{2,1,0:T(8,128)(2,1)}, bf16[2,256,768]{2,1,0:T(8,128)(2,1)}, u32[]{:S(2)}, u32[]{:S(2)}) collective-permute-start(bf16[2,256,768]{2,1,0:T(8,128)(2,1)} %get-tuple-element.82), channel_id=1, source_target_pairs={{0,2},{2,0},{4,6},{6,4},{8,10},{10,8},{12,14},{14,12},{16,18},{18,... | collective-permute-start | bytes 2359304 | tf_op jit(solution)/shard_map/ppermute | solution.py:308
  27.6 2.7 %collective-permute-start.4 = (bf16[128,768]{1,0:T(8,128)(2,1)}, bf16[128,768]{1,0:T(8,128)(2,1)}, u32[]{:S(2)}, u32[]{:S(2)}) collective-permute-start(bf16[128,768]{1,0:T(8,128)(2,1)} %get-tuple-element.81), channel_id=1, source_target_pairs={{0,1},{1,0},{2,3},{3,2},{4,5},{5,4},{6,7},{7,6},{8,9},{9,8},{10,11... | collective-permute-start | bytes 589832 | tf_op jit(solution)/shard_map/ppermute | solution.py:333
  30.3 9.9 %attn.4 = (bf16[128,5120]{1,0:T(8,128)(2,1)}, bf16[128,896]{1,0:T(8,128)(2,1)}, bf16[2,256,896]{2,1,0:T(8,128)(2,1)}, bf16[2,256,896]{2,1,0:T(8,128)(2,1)}, bf16[2,256,896]{2,1,0:T(8,128)(2,1)}) custom-call(s32[1]{0:T(128)} %bitcast.side_ref, bf16[256,2560]{1,0:T(8,128)(2,1)} %q_ref.5, bf16[256,2560]{1,0:T(8,128)(2,1)} %do_ref.5, ...), custom_call_target="tpu_custom_call", output_to_operand_aliasing={{0}: (9, {})} | custom-call | flops 1000 | bytes 1000 | tf_op jit(solution)/shard_map/attn/pallas_call | solution.py:98
  40.2 14.3 %collective-permute-done.4.refs_4_ = bf16[128,768]{1,0:T(8,128)(2,1)} collective-permute-done((bf16[128,768]{1,0:T(8,128)(2,1)}, bf16[128,768]{1,0:T(8,128)(2,1)}, u32[]{:S(2)}, u32[]{:S(2)}) %collective-permute-start.4) | collective-permute-done | bytes 196640 | tf_op jit(solution)/shard_map/ppermute | solution.py:333
  54.5 0.6 collective-permute-start.9
  55.1 2.8 %combine.3 = (bf16[128,5120]{1,0:T(8,128)(2,1)}, bf16[128,5120]{1,0:T(8,128)(2,1)}, bf16[384,896]{1,0:T(8,128)(2,1)}, bf16[128,5120]{1,0:T(8,128)(2,1)}) custom-call(s32[1]{0:T(128)} %bitcast.side_ref, s32[1]{0:T(128)} %bitcast.1.corner_ref, bf16[2,256,768]{2,1,0:T(8,128)(2,1)} %get-tuple-element.88.refs_0_, ...), custom_call_target="tpu_custom_call", output_to_operand_aliasing={{3}: (6, {})} | custom-call | flops 1000 | bytes 1000 | tf_op jit(solution)/shard_map/combine/pallas_call | solution.py:211
  57.9 0.6 collective-permute-start.10
  58.5 9.9 %attn.5 = (bf16[128,5120]{1,0:T(8,128)(2,1)}, bf16[128,896]{1,0:T(8,128)(2,1)}, bf16[2,256,896]{2,1,0:T(8,128)(2,1)}, bf16[2,256,896]{2,1,0:T(8,128)(2,1)}, bf16[2,256,896]{2,1,0:T(8,128)(2,1)}) custom-call(s32[1]{0:T(128)} %bitcast.side_ref, bf16[256,2560]{1,0:T(8,128)(2,1)} %q_ref.5, bf16[256,2560]{1,0:T(8,128)(2,1)} %do_ref.5, ...), custom_call_target="tpu_custom_call", output_to_operand_aliasing={{0}: (9, {})} | custom-call | flops 1000 | bytes 1000 | tf_op jit(solution)/shard_map/attn/pallas_call | solution.py:98
  68.4 0.1 collective-permute-done.7.refs_2_
  68.5 1.6 %collective-permute-start.14 = (bf16[2,256,896]{2,1,0:T(8,128)(2,1)}, bf16[2,256,896]{2,1,0:T(8,128)(2,1)}, u32[]{:S(2)}, u32[]{:S(2)}) collective-permute-start(bf16[2,256,896]{2,1,0:T(8,128)(2,1)} %collective-permute-done.7.refs_2_), channel_id=1, source_target_pairs={{0,128},{126,254},{128,0},{254,126},{1,129},{127,255},{129,1},{255... | collective-permute-start | bytes 2752520 | tf_op jit(solution)/shard_map/ppermute | solution.py:329
  70.1 6.6 %collective-permute-done.10.refs_3_ = bf16[384,896]{1,0:T(8,128)(2,1)} collective-permute-done((bf16[384,896]{1,0:T(8,128)(2,1)}, bf16[384,896]{1,0:T(8,128)(2,1)}, u32[]{:S(2)}, u32[]{:S(2)}) %collective-permute-start.10) | collective-permute-done | bytes 688160 | tf_op jit(solution)/shard_map/ppermute | solution.py:333
  76.7 0.9 collective-permute-start.11
  77.6 0.5 collective-permute-start.13
  78.2 3.1 %combine.4 = (bf16[128,5120]{1,0:T(8,128)(2,1)}, bf16[128,5120]{1,0:T(8,128)(2,1)}, bf16[256,896]{1,0:T(8,128)(2,1)}, bf16[128,5120]{1,0:T(8,128)(2,1)}) custom-call(s32[1]{0:T(128)} %bitcast.side_ref, s32[1]{0:T(128)} %bitcast.1.corner_ref, ...), custom_call_target="tpu_custom_call", output_to_operand_aliasing={{3}: (7, {}), {0}: (8, {}), {1}: (9, {})} | custom-call | flops 1000 | bytes 1000 | tf_op jit(solution)/shard_map/combine/pallas_call | solution.py:211
  81.3 2.5 %collective-permute-start.16 = (bf16[256,896]{1,0:T(8,128)(2,1)}, bf16[256,896]{1,0:T(8,128)(2,1)}, u32[]{:S(2)}, u32[]{:S(2)}) collective-permute-start(bf16[256,896]{1,0:T(8,128)(2,1)} %get-tuple-element.120), channel_id=1, source_target_pairs={{0,1},{1,0},{2,3},{3,2},{4,5},{5,4},{6,7},{7,6},{8,9},{9,8},{10,11... | collective-permute-start | bytes 1376264 | tf_op jit(solution)/shard_map/ppermute | solution.py:333
  83.8 12.3 %collective-permute-done.13.refs_4_ = bf16[128,896]{1,0:T(8,128)(2,1)} collective-permute-done((bf16[128,896]{1,0:T(8,128)(2,1)}, bf16[128,896]{1,0:T(8,128)(2,1)}, u32[]{:S(2)}, u32[]{:S(2)}) %collective-permute-start.13) | collective-permute-done | bytes 229408 | tf_op jit(solution)/shard_map/ppermute | solution.py:333
  96.1 3.5 %combine.5 = (bf16[128,5120]{1,0:T(8,128)(2,1)}, bf16[128,5120]{1,0:T(8,128)(2,1)}, bf16[256,896]{1,0:T(8,128)(2,1)}, bf16[128,5120]{1,0:T(8,128)(2,1)}) custom-call(s32[1]{0:T(128)} %bitcast.side_ref, s32[1]{0:T(128)} %bitcast.1.corner_ref, ...), custom_call_target="tpu_custom_call", output_to_operand_aliasing={{3}: (7, {}), {0}: (8, {}), {1}: (9, {})} | custom-call | flops 1000 | bytes 1000 | tf_op jit(solution)/shard_map/combine/pallas_call | solution.py:211
  99.7 6.3 %collective-permute-done.16.refs_0_ = bf16[256,896]{1,0:T(8,128)(2,1)} collective-permute-done((bf16[256,896]{1,0:T(8,128)(2,1)}, bf16[256,896]{1,0:T(8,128)(2,1)}, u32[]{:S(2)}, u32[]{:S(2)}) %collective-permute-start.16) | collective-permute-done | bytes 458784 | tf_op jit(solution)/shard_map/ppermute | solution.py:333
  105.9 1.8 %place.2 = (bf16[128,5120]{1,0:T(8,128)(2,1)}, bf16[128,5120]{1,0:T(8,128)(2,1)}, bf16[128,5120]{1,0:T(8,128)(2,1)}) custom-call(s32[1]{0:T(128)} %bitcast.side_ref, bf16[256,896]{1,0:T(8,128)(2,1)} %collective-permute-done.16.refs_0_, bf16[128,5120]{1,0:T(8,128)(2,1)} %get-tuple-element.121.refs_1_, ...), custom_call_target="tpu_custom_call", output_to_operand_aliasing={{0}: (2, {}), {1}: (3, {}), {2}: (4, {})} | custom-call | flops 1000 | bytes 1000 | tf_op jit(solution)/shard_map/place/pallas_call | solution.py:253
  107.7 8.0 %collective-permute-done.15.refs_0_ = bf16[256,896]{1,0:T(8,128)(2,1)} collective-permute-done((bf16[256,896]{1,0:T(8,128)(2,1)}, bf16[256,896]{1,0:T(8,128)(2,1)}, u32[]{:S(2)}, u32[]{:S(2)}) %collective-permute-start.15) | collective-permute-done | bytes 458784 | tf_op jit(solution)/shard_map/ppermute | solution.py:333
  115.8 1.8 %place.3 = (bf16[128,5120]{1,0:T(8,128)(2,1)}, bf16[128,5120]{1,0:T(8,128)(2,1)}, bf16[128,5120]{1,0:T(8,128)(2,1)}) custom-call(s32[1]{0:T(128)} %bitcast.side_ref, bf16[256,896]{1,0:T(8,128)(2,1)} %collective-permute-done.15.refs_0_, bf16[128,5120]{1,0:T(8,128)(2,1)} %get-tuple-element.124.refs_1_, ...), custom_call_target="tpu_custom_call", output_to_operand_aliasing={{0}: (2, {}), {1}: (3, {}), {2}: (4, {})} | custom-call | flops 1000 | bytes 1000 | tf_op jit(solution)/shard_map/place/pallas_call | solution.py:253
  (24 shorter events, 0.4 us)
Async XLA Ops:
  0.6 4.5 %collective-permute-start = (bf16[256,2560]{1,0:T(8,128)(2,1)}, bf16[256,2560]{1,0:T(8,128)(2,1)}, u32[]{:S(2)}, u32[]{:S(2)}) collective-permute-start(bf16[256,2560]{1,0:T(8,128)(2,1)} %k_ref.8), channel_id=1, source_target_pairs={{0,2},{2,0},{4,6},{6,4},{8,10},{10,8},{12,14},{14,12},{16,18},{18,... | collective-permute-start | bytes 3932168 | tf_op jit(solution)/shard_map/ppermute | solution.py:308
  1.4 14.1 %collective-permute-start.1 = (bf16[256,2560]{1,0:T(8,128)(2,1)}, bf16[256,2560]{1,0:T(8,128)(2,1)}, u32[]{:S(2)}, u32[]{:S(2)}) collective-permute-start(bf16[256,2560]{1,0:T(8,128)(2,1)} %v_ref.9), channel_id=1, source_target_pairs={{0,2},{2,0},{4,6},{6,4},{8,10},{10,8},{12,14},{14,12},{16,18},{18,... | collective-permute-start | bytes 3932168 | tf_op jit(solution)/shard_map/ppermute | solution.py:308
  3.4 12.1 %collective-permute-start.2 = (bf16[2,256,768]{2,1,0:T(8,128)(2,1)}, bf16[2,256,768]{2,1,0:T(8,128)(2,1)}, u32[]{:S(2)}, u32[]{:S(2)}) collective-permute-start(bf16[2,256,768]{2,1,0:T(8,128)(2,1)} %pack.2), channel_id=1, source_target_pairs={{0,254},{2,4},{4,2},{6,8},{8,6},{10,12},{12,10},{14,16},{16,14},{1... | collective-permute-start | bytes 2359304 | tf_op jit(solution)/shard_map/ppermute | solution.py:324
  5.1 3.3 %copy-start = (s32[256,6]{0,1:T(8,128)S(1)}, s32[256,6]{0,1:T(8,128)}, u32[]{:S(2)}) copy-start(s32[256,6]{0,1:T(8,128)} %param.9) | copy-start | bytes 18436
  7.4 17.9 %collective-permute-start.3 = (bf16[2,256,896]{2,1,0:T(8,128)(2,1)}, bf16[2,256,896]{2,1,0:T(8,128)(2,1)}, u32[]{:S(2)}, u32[]{:S(2)}) collective-permute-start(bf16[2,256,896]{2,1,0:T(8,128)(2,1)} %get-tuple-element.67), channel_id=1, source_target_pairs={{0,254},{2,4},{4,2},{6,8},{8,6},{10,12},{12,10},{14,16},{16,14},{1... | collective-permute-start | bytes 2752520 | tf_op jit(solution)/shard_map/ppermute | solution.py:324
  8.7 45.8 %collective-permute-start.6 = (bf16[2,256,896]{2,1,0:T(8,128)(2,1)}, bf16[2,256,896]{2,1,0:T(8,128)(2,1)}, u32[]{:S(2)}, u32[]{:S(2)}) collective-permute-start(bf16[2,256,896]{2,1,0:T(8,128)(2,1)} %get-tuple-element.68), channel_id=1, source_target_pairs={{0,254},{2,4},{4,2},{6,8},{8,6},{10,12},{12,10},{14,16},{16,14},{1... | collective-permute-start | bytes 2752520 | tf_op jit(solution)/shard_map/ppermute | solution.py:324
  25.3 29.1 %collective-permute-start.5 = (bf16[2,256,768]{2,1,0:T(8,128)(2,1)}, bf16[2,256,768]{2,1,0:T(8,128)(2,1)}, u32[]{:S(2)}, u32[]{:S(2)}) collective-permute-start(bf16[2,256,768]{2,1,0:T(8,128)(2,1)} %get-tuple-element.82), channel_id=1, source_target_pairs={{0,2},{2,0},{4,6},{6,4},{8,10},{10,8},{12,14},{14,12},{16,18},{18,... | collective-permute-start | bytes 2359304 | tf_op jit(solution)/shard_map/ppermute | solution.py:308
  27.6 26.9 %collective-permute-start.8 = (bf16[2,256,768]{2,1,0:T(8,128)(2,1)}, bf16[2,256,768]{2,1,0:T(8,128)(2,1)}, u32[]{:S(2)}, u32[]{:S(2)}) collective-permute-start(bf16[2,256,768]{2,1,0:T(8,128)(2,1)} %get-tuple-element.86), channel_id=1, source_target_pairs={{0,254},{2,4},{4,2},{6,8},{8,6},{10,12},{12,10},{14,16},{16,14},{1... | collective-permute-start | bytes 2359304 | tf_op jit(solution)/shard_map/ppermute | solution.py:324
  27.6 26.9 %collective-permute-start.4 = (bf16[128,768]{1,0:T(8,128)(2,1)}, bf16[128,768]{1,0:T(8,128)(2,1)}, u32[]{:S(2)}, u32[]{:S(2)}) collective-permute-start(bf16[128,768]{1,0:T(8,128)(2,1)} %get-tuple-element.81), channel_id=1, source_target_pairs={{0,1},{1,0},{2,3},{3,2},{4,5},{5,4},{6,7},{7,6},{8,9},{9,8},{10,11... | collective-permute-start | bytes 589832 | tf_op jit(solution)/shard_map/ppermute | solution.py:333
  54.5 13.9 %collective-permute-start.9 = (bf16[2,256,896]{2,1,0:T(8,128)(2,1)}, bf16[2,256,896]{2,1,0:T(8,128)(2,1)}, u32[]{:S(2)}, u32[]{:S(2)}) collective-permute-start(bf16[2,256,896]{2,1,0:T(8,128)(2,1)} %get-tuple-element.100), channel_id=1, source_target_pairs={{0,2},{2,0},{4,6},{6,4},{8,10},{10,8},{12,14},{14,12},{16,18},{18,... | collective-permute-start | bytes 2752520 | tf_op jit(solution)/shard_map/ppermute | solution.py:308
  55.1 13.4 %collective-permute-start.7 = (bf16[2,256,896]{2,1,0:T(8,128)(2,1)}, bf16[2,256,896]{2,1,0:T(8,128)(2,1)}, u32[]{:S(2)}, u32[]{:S(2)}) collective-permute-start(bf16[2,256,896]{2,1,0:T(8,128)(2,1)} %get-tuple-element.83), channel_id=1, source_target_pairs={{0,126},{2,4},{4,2},{6,8},{8,6},{10,12},{12,10},{14,16},{16,14},{1... | collective-permute-start | bytes 2752520 | tf_op jit(solution)/shard_map/ppermute | solution.py:324
  57.9 18.8 %collective-permute-start.10 = (bf16[384,896]{1,0:T(8,128)(2,1)}, bf16[384,896]{1,0:T(8,128)(2,1)}, u32[]{:S(2)}, u32[]{:S(2)}) collective-permute-start(bf16[384,896]{1,0:T(8,128)(2,1)} %get-tuple-element.104), channel_id=1, source_target_pairs={{0,1},{1,0},{2,3},{3,2},{4,5},{5,4},{6,7},{7,6},{8,9},{9,8},{10,11... | collective-permute-start | bytes 2064392 | tf_op jit(solution)/shard_map/ppermute | solution.py:333
  68.5 9.7 %collective-permute-start.14 = (bf16[2,256,896]{2,1,0:T(8,128)(2,1)}, bf16[2,256,896]{2,1,0:T(8,128)(2,1)}, u32[]{:S(2)}, u32[]{:S(2)}) collective-permute-start(bf16[2,256,896]{2,1,0:T(8,128)(2,1)} %collective-permute-done.7.refs_2_), channel_id=1, source_target_pairs={{0,128},{126,254},{128,0},{254,126},{1,129},{127,255},{129,1},{255... | collective-permute-start | bytes 2752520 | tf_op jit(solution)/shard_map/ppermute | solution.py:329
  76.7 19.4 %collective-permute-start.11 = (bf16[2,256,896]{2,1,0:T(8,128)(2,1)}, bf16[2,256,896]{2,1,0:T(8,128)(2,1)}, u32[]{:S(2)}, u32[]{:S(2)}) collective-permute-start(bf16[2,256,896]{2,1,0:T(8,128)(2,1)} %get-tuple-element.105), channel_id=1, source_target_pairs={{0,2},{2,0},{4,6},{6,4},{8,10},{10,8},{12,14},{14,12},{16,18},{18,... | collective-permute-start | bytes 2752520 | tf_op jit(solution)/shard_map/ppermute | solution.py:308
  77.6 18.5 %collective-permute-start.12 = (bf16[2,256,896]{2,1,0:T(8,128)(2,1)}, bf16[2,256,896]{2,1,0:T(8,128)(2,1)}, u32[]{:S(2)}, u32[]{:S(2)}) collective-permute-start(bf16[2,256,896]{2,1,0:T(8,128)(2,1)} %get-tuple-element.106), channel_id=1, source_target_pairs={{0,254},{2,4},{4,2},{6,8},{8,6},{10,12},{12,10},{14,16},{16,14},{1... | collective-permute-start | bytes 2752520 | tf_op jit(solution)/shard_map/ppermute | solution.py:324
  77.6 18.5 %collective-permute-start.13 = (bf16[128,896]{1,0:T(8,128)(2,1)}, bf16[128,896]{1,0:T(8,128)(2,1)}, u32[]{:S(2)}, u32[]{:S(2)}) collective-permute-start(bf16[128,896]{1,0:T(8,128)(2,1)} %get-tuple-element.108), channel_id=1, source_target_pairs={{0,1},{1,0},{2,3},{3,2},{4,5},{5,4},{6,7},{7,6},{8,9},{9,8},{10,11... | collective-permute-start | bytes 688136 | tf_op jit(solution)/shard_map/ppermute | solution.py:333
  81.3 24.7 %collective-permute-start.16 = (bf16[256,896]{1,0:T(8,128)(2,1)}, bf16[256,896]{1,0:T(8,128)(2,1)}, u32[]{:S(2)}, u32[]{:S(2)}) collective-permute-start(bf16[256,896]{1,0:T(8,128)(2,1)} %get-tuple-element.120), channel_id=1, source_target_pairs={{0,1},{1,0},{2,3},{3,2},{4,5},{5,4},{6,7},{7,6},{8,9},{9,8},{10,11... | collective-permute-start | bytes 1376264 | tf_op jit(solution)/shard_map/ppermute | solution.py:333
  99.6 16.2 %collective-permute-start.15 = (bf16[256,896]{1,0:T(8,128)(2,1)}, bf16[256,896]{1,0:T(8,128)(2,1)}, u32[]{:S(2)}, u32[]{:S(2)}) collective-permute-start(bf16[256,896]{1,0:T(8,128)(2,1)} %get-tuple-element.119), channel_id=1, source_target_pairs={{0,1},{1,0},{2,3},{3,2},{4,5},{5,4},{6,7},{7,6},{8,9},{9,8},{10,11... | collective-permute-start | bytes 1376264 | tf_op jit(solution)/shard_map/ppermute | solution.py:333
